TPU v7x, 512 devices: a whole 4x4x16 slice. The times are simulated.
512 devices in a mesh: tgt: 128 (over x, z, core), band: 4 (over y).
Axes of the slice: x: 4, y: 4, z: 16, core: 2. Of those that a mesh axis runs over, the one named last changes fastest.
Arguments:
- exposure_flux: bfloat16 [16384, 4096], P('tgt', 'band'), may hold values from -6 to 6
- exposure_ivar: bfloat16 [16384, 4096], P('tgt', 'band'), may hold values from 0.19921875 to 5
- exposure_res: bfloat16 [16384, 11, 4096], P('tgt', None, 'band'), may hold values from 0 to 1
- target_of_row: int32 [16384], replicated, may hold values from 0 to 2047, as said below
- valid_of_row: int32 [16384], replicated, may hold values from 0 to 1, as said below
- rest_basis: float32 [10, 4608], replicated, may hold values from -6 to 6
- redshift_shift: int32 [32], replicated, may hold values from 0 to 511
Outputs:
- coadd_flux: float32 [2048, 4096], P('tgt', 'band')
- coadd_res: bfloat16 [2048, 11, 4096], P('tgt', None, 'band')
- fit_gain: float32 [2048, 32], P('tgt', 'band')
Inputs may be any that keep to these rules, and one draw needn't show every extreme that they name: `target_of_row`: every target has exactly 8 rows. The rows held by one index of tgt (rows j * 128 to (j + 1) * 128 - 1) include at most 2 rows of the targets of any one owner, where the owner of target t is t // 16; some pairs reach 2. `valid_of_row`: every target has at least one row with flag 1.
All inputs are finite; a program needn't handle non-finite values.
Results may differ from a plain program's by a relative error of at most 0.004.
Values may be sent and summed in bfloat16 or wider, within the bound.
No kernel may reach another device: no remote copies, remote signals or barrier semaphores. Data moves between devices by JAX's collectives and lax.ppermute only.
A program may use at most 128 MiB of HBM per device.

v0:
```python
import jax
import jax.numpy as jnp
import numpy as np
from jax import lax
from jax.sharding import PartitionSpec as P

TGT_DEV = 16
NDIAG = 11
Z_DEV = 8


pair_first, pair_second = np.triu_indices(10)


def solve_normal(matrix, right_side):
    basis_count = right_side.shape[0]
    rows_of = [[None] * basis_count for column in range(basis_count)]
    for p in range(len(pair_first)):
        b = int(pair_first[p])
        c = int(pair_second[p])
        rows_of[b][c] = matrix[p]
        rows_of[c][b] = matrix[p]
    vector = [right_side[b] for b in range(basis_count)]
    for k in range(basis_count):
        inverse = 1.0 / rows_of[k][k]
        for r in range(k + 1, basis_count):
            factor = rows_of[r][k] * inverse
            for c in range(k + 1, basis_count):
                rows_of[r][c] = rows_of[r][c] - factor * rows_of[k][c]
            vector[r] = vector[r] - factor * vector[k]
    answer = [None] * basis_count
    for k in reversed(range(basis_count)):
        running = vector[k]
        for c in range(k + 1, basis_count):
            running = running - rows_of[k][c] * answer[c]
        answer[k] = running / rows_of[k][k]
    gain_total = right_side[0] * answer[0]
    for b in range(1, basis_count):
        gain_total = gain_total + right_side[b] * answer[b]
    return gain_total


def basis_windows(rest_basis, shifts, first_wave, length):

    def one_shift(shift_value):
        return lax.dynamic_slice_in_dim(rest_basis, first_wave + shift_value, length, axis=1)

    return jax.vmap(one_shift)(shifts)


def normal_terms(weight_sum, flux_sum, windows):
    products = windows[:, pair_first, :] * windows[:, pair_second, :]
    matrix = jnp.einsum("ti,zpi->ztp", weight_sum, products, precision=lax.Precision.HIGHEST)
    right_side = jnp.einsum("ti,zbi->ztb", flux_sum, windows, precision=lax.Precision.HIGHEST)
    return (matrix, right_side)


def blocked_normals(weight_sum, flux_sum, rest_basis, shifts, first_wave, length):
    total_shifts = shifts.shape[0]
    block_size = 8
    grouped = shifts.reshape(total_shifts // block_size, block_size)

    def one_block(shift_block):
        return normal_terms(
            weight_sum, flux_sum, basis_windows(rest_basis, shift_block, first_wave, length)
        )

    matrix, right_side = lax.map(one_block, grouped)
    return (
        matrix.reshape((total_shifts,) + matrix.shape[2:]),
        right_side.reshape((total_shifts,) + right_side.shape[2:]),
    )


def fit_from(matrix, right_side):
    pairs = jnp.transpose(matrix, (2, 0, 1)).reshape(matrix.shape[2], -1)
    sides = jnp.transpose(right_side, (2, 0, 1)).reshape(right_side.shape[2], -1)
    gain = solve_normal(pairs, sides).reshape(matrix.shape[0], matrix.shape[1])
    return gain.T


def shards(
    exposure_flux,
    exposure_ivar,
    exposure_res,
    target_of_row,
    valid_of_row,
    rest_basis,
    redshift_shift,
):
    owners = lax.axis_size("tgt")
    device = lax.axis_index("tgt")
    row_count = exposure_flux.shape[0]
    wave_dev = exposure_flux.shape[1]
    capacity = 2 * row_count // owners
    own_target = lax.dynamic_slice_in_dim(target_of_row, device * row_count, row_count)
    owner_of = own_target // TGT_DEV
    row_ids = jnp.arange(row_count, dtype=jnp.int32)
    earlier = row_ids[None, :] < row_ids[:, None]
    position = jnp.sum(jnp.logical_and(owner_of[:, None] == owner_of[None, :], earlier), axis=1)
    slot_index = owner_of * capacity + position
    source_row = jnp.full((owners * capacity,), row_count, jnp.int32).at[slot_index].set(row_ids)

    def packed(values):
        gathered = jnp.take(values, source_row, axis=0, mode="fill", fill_value=0)
        return gathered.reshape((owners, capacity) + values.shape[1:])

    target_table = target_of_row.reshape(owners, row_count)
    is_mine = (target_table // TGT_DEV == device).astype(jnp.int32)
    before = jnp.cumsum(is_mine, axis=1) - is_mine
    matches = jnp.logical_and(
        is_mine[:, :, None] == 1,
        before[:, :, None] == jnp.arange(capacity, dtype=jnp.int32)[None, None, :],
    ).astype(jnp.int32)
    present = jnp.sum(matches, axis=1)
    local_target = jnp.sum(matches * (target_table % TGT_DEV)[:, :, None], axis=1)
    member = (
        jnp.logical_and(
            local_target[None] == jnp.arange(TGT_DEV, dtype=jnp.int32)[:, None, None],
            present[None] == 1,
        )
        .astype(jnp.float32)
        .reshape(TGT_DEV, owners * capacity)
    )
    outgoing = (packed(exposure_flux), packed(exposure_ivar), packed(exposure_res))
    got_flux, got_ivar, got_res = (
        lax.all_to_all(outgoing[0], "tgt", split_axis=0, concat_axis=0, tiled=True),
        lax.all_to_all(outgoing[1], "tgt", split_axis=0, concat_axis=0, tiled=True),
        lax.all_to_all(outgoing[2], "tgt", split_axis=0, concat_axis=0, tiled=True),
    )
    flag_table = valid_of_row.reshape(owners, row_count)
    usable = jnp.sum(matches * flag_table[:, :, None], axis=1)
    weight = got_ivar.astype(jnp.float32) * usable[:, :, None].astype(jnp.float32)
    flux_terms = weight * got_flux.astype(jnp.float32)
    res_terms = (weight[:, :, None, :] * got_res.astype(jnp.float32)).reshape(owners * capacity, -1)
    weight_sum = jnp.dot(
        member, weight.reshape(owners * capacity, wave_dev), precision=lax.Precision.HIGHEST
    )
    flux_sum = jnp.dot(
        member, flux_terms.reshape(owners * capacity, wave_dev), precision=lax.Precision.HIGHEST
    )
    res_sum = jnp.dot(member, res_terms, precision=lax.Precision.HIGHEST).reshape(
        TGT_DEV, NDIAG, wave_dev
    )
    coadd_flux = flux_sum / weight_sum
    coadd_res = (res_sum / weight_sum[:, None, :]).astype(jnp.bfloat16)
    band_index = lax.axis_index("band")
    weight_all, flux_all = (
        lax.all_gather(weight_sum.astype(jnp.bfloat16), "band", axis=1, tiled=True).astype(
            weight_sum.dtype
        ),
        lax.all_gather(flux_sum.astype(jnp.bfloat16), "band", axis=1, tiled=True).astype(
            flux_sum.dtype
        ),
    )
    shifts = lax.dynamic_slice_in_dim(redshift_shift, band_index * Z_DEV, Z_DEV)
    matrix, right_side = blocked_normals(
        weight_all, flux_all, rest_basis, shifts, 0, weight_all.shape[1]
    )
    fit_gain = fit_from(matrix, right_side)
    return (coadd_flux, coadd_res, fit_gain)


def solution(mesh):
    in_specs = (P("tgt", "band"), P("tgt", "band"), P("tgt", None, "band"), P(), P(), P(), P())
    out_specs = (P("tgt", "band"), P("tgt", None, "band"), P("tgt", "band"))
    return jax.shard_map(shards, mesh=mesh, in_specs=in_specs, out_specs=out_specs, check_vma=False)
```

profile of v0, /device:TPU:60, one launch (start us, length us, event | category | flops | bytes accessed | tf_op | source)
XLA Modules:
  0.0 455.0 jit_solution(5095595172221407455)
XLA Ops:
  0.7 0.9 and_select_fusion
  1.6 0.2 convert_reduce_fusion.1
  1.8 0.8 compare_select_fusion.2
  2.6 1.0 scatter_custom_fusion
  3.6 3.3 gather_fusion.3
  6.9 2.0 gather_fusion.4
  8.9 2.1 broadcast_select_fusion.2
  11.0 2.0 reshape.361
  13.1 19.7 %all-to-all-start = ((bf16[128,2,1024]{2,1,0:T(2,128)(2,1)}), bf16[128,2,1024]{2,1,0:T(2,128)(2,1)}, u32[]{:S(2)}, u32[]{:S(2)}) async-start(bf16[128,2,1024]{2,1,0:T(2,128)(2,1)} %reshape.361), calls=%async_computation | async-start | bytes 1048576 | tf_op jit(solution)/shard_map/all_to_all | solution.py:128
  32.8 1.0 reshape.362
  33.8 31.5 %all-to-all-done = bf16[128,2,1024]{2,1,0:T(2,128)(2,1)} async-done(((bf16[128,2,1024]{2,1,0:T(2,128)(2,1)}), bf16[128,2,1024]{2,1,0:T(2,128)(2,1)}, u32[]{:S(2)}, u32[]{:S(2)}) %all-to-all-start) | async-done | bytes 524320 | tf_op jit(solution)/shard_map/all_to_all | solution.py:128
  65.4 7.6 %all-to-all-start.1 = ((bf16[128,2,1024]{2,1,0:T(2,128)(2,1)}), bf16[128,2,1024]{2,1,0:T(2,128)(2,1)S(1)}, u32[]{:S(2)}, u32[]{:S(2)}) async-start(bf16[128,2,1024]{2,1,0:T(2,128)(2,1)} %reshape.362), calls=%async_computation.1 | async-start | bytes 1048576 | tf_op jit(solution)/shard_map/all_to_all | solution.py:127
  73.0 0.2 broadcast_in_dim.65
  73.2 20.2 %gather_fusion = bf16[256,11,1024]{2,0,1:T(8,128)(2,1)} fusion(bf16[128,11,1024]{2,0,1:T(8,128)(2,1)S(1)} %copy-done, s32[1024]{0:T(1024)S(1)} %pad_clamp_fusion.2), kind=kCustom, calls=%fused_computation.2 | custom fusion | bytes 11535360 | tf_op jit(solution)/shard_map/jit(_take)/gather | solution.py:105
  93.4 9.5 %gather.22 = bf16[128,2,11,1024]{3,1,0,2:T(2,128)(2,1)} reshape(bf16[256,11,1024]{2,0,1:T(8,128)(2,1)} %gather_fusion) | data formatting | bytes 11534336 | tf_op jit(solution)/shard_map/jit(_take)/gather | solution.py:105
  102.9 8.1 %broadcast_select_fusion = bf16[128,2,11,1024]{3,1,2,0:T(2,128)(2,1)} fusion(pred[128,2]{1,0:T(8,128)(4,1)S(1)} %broadcast_in_dim.65, bf16[128,2,11,1024]{3,1,0,2:T(2,128)(2,1)} %gather.22), kind=kLoop, calls=%fused_computation.9 | loop fusion | flops 2883584 | bytes 11534592 | tf_op jit(solution)/shard_map/jit(_take)/select_n | solution.py:105
  111.1 16.7 %all-to-all-start.2 = ((bf16[128,2,11,1024]{3,1,2,0:T(2,128)(2,1)}), bf16[128,2,11,1024]{3,1,2,0:T(2,128)(2,1)}, u32[]{:S(2)}, u32[]{:S(2)}) async-start(bf16[128,2,11,1024]{3,1,2,0:T(2,128)(2,1)} %broadcast_select_fusion), calls=%async_computation.2 | async-start | bytes 11534336 | tf_op jit(solution)/shard_map/all_to_all | solution.py:129
  127.9 0.1 copy.86
  128.0 0.2 reduce_window_sum.11
  128.2 0.1 copy.91
  128.3 0.1 copy.90
  128.5 0.1 copy.92
  128.6 0.2 convert_reduce_fusion
  128.8 0.1 fusion.94
  128.9 16.7 %while.1 = (s32[]{:T(128)}, f32[10,4608]{1,0:T(8,128)S(1)}, s32[8,2]{0,1:T(2,128)S(1)}, f32[8,10,4096]{2,1,0:T(8,128)}, s32[]{:T(128)}) while((s32[]{:T(128)}, f32[10,4608]{1,0:T(8,128)S(1)}, s32[8,2]{0,1:T(2,128)S(1)}, f32[8,10,4096]{2,1,0:T(8,128)}, s32[]{:T(128)}) %tuple.42), condition=%wide.while_cond, body=%wide.while_body.sunk | while | flops 2 | bytes 427097 | solution.py:46
  128.9 0.1 constant_dynamic-slice_fusion.2
  129.0 0.5 slice.734
  129.5 1.5 bitcast_dynamic-update-slice_fusion.2
  130.9 0.1 constant_dynamic-slice_fusion.2
  131.0 0.5 slice.734
  131.5 1.5 bitcast_dynamic-update-slice_fusion.2
  133.1 0.5 slice.734
  133.6 1.5 bitcast_dynamic-update-slice_fusion.2
  135.2 0.5 slice.734
  135.7 1.5 bitcast_dynamic-update-slice_fusion.2
  137.3 0.5 slice.734
  137.8 1.5 bitcast_dynamic-update-slice_fusion.2
  139.4 0.5 slice.734
  139.9 1.5 bitcast_dynamic-update-slice_fusion.2
  141.5 0.5 slice.734
  142.0 1.5 bitcast_dynamic-update-slice_fusion.2
  143.5 0.5 slice.734
  144.1 1.5 bitcast_dynamic-update-slice_fusion.2
  145.5 2.4 copy.101
  147.9 3.9 gather_fusion.1
  151.8 4.0 gather_fusion.2
  155.8 0.1 copy.95
  155.9 0.1 eq.105
  156.0 0.1 copy.96
  156.2 0.1 eq.109
  156.3 1.8 convolution_bitcast_fusion.2
  158.1 2.3 fusion.98
  160.4 12.0 %all_gather.7 = bf16[16,4096]{1,0:T(8,128)(2,1)S(1)} all-gather(bf16[16,1024]{1,0:T(8,128)(2,1)S(1)} %get-tuple-element.58), channel_id=1, replica_groups=mesh['tgt'=128,'band'=4] {'band'}, dimensions={1}, use_global_device_ids=true | all-gather | bytes 163840 | tf_op jit(solution)/shard_map/all_gather | solution.py:149
  172.3 12.0 %all_gather.6 = bf16[16,4096]{1,0:T(8,128)(2,1)S(1)} all-gather(bf16[16,1024]{1,0:T(8,128)(2,1)S(1)} %get-tuple-element.60), channel_id=1, replica_groups=mesh['tgt'=128,'band'=4] {'band'}, dimensions={1}, use_global_device_ids=true | all-gather | bytes 163840 | tf_op jit(solution)/shard_map/all_gather | solution.py:152
  184.3 2.6 convolution_bitcast_fusion
  187.0 7.2 %fusion.4 = f32[55,8,16]{2,1,0:T(8,128)S(1)} fusion(f32[55,8,4096]{2,1,0:T(8,128)} %gather_fusion.1, f32[55,8,4096]{2,1,0:T(8,128)} %gather_fusion.2, bf16[16,4096]{1,0:T(8,128)(2,1)S(1)} %all_gather.7), kind=kOutput, calls=%fused_computation.15 | convolution fusion | flops 347832320 | bytes 14577152 | tf_op jit(solution)/shard_map/while/body/eval_jaxpr/ti,zpi->ztp/dot_general | solution.py:53
  194.2 0.8 add_bitcast_fusion
  195.0 1.2 convert_multiply_fusion.1
  196.2 187.7 %all-to-all-done.2 = bf16[128,2,11,1024]{3,1,2,0:T(2,128)(2,1)} async-done(((bf16[128,2,11,1024]{3,1,2,0:T(2,128)(2,1)}), bf16[128,2,11,1024]{3,1,2,0:T(2,128)(2,1)}, u32[]{:S(2)}, u32[]{:S(2)}) %all-to-all-start.2) | async-done | bytes 5767200 | tf_op jit(solution)/shard_map/all_to_all | solution.py:129
  383.9 9.3 %convert_multiply_fusion = f32[128,2,11,1024]{3,0,2,1:T(8,128)} fusion(bf16[128,2,11,1024]{3,1,2,0:T(2,128)(2,1)} %all-to-all-done.2, f32[128,2,1024]{2,0,1:T(8,128)S(1)} %convert_multiply_fusion.1), kind=kLoop, calls=%fused_computation.8 | loop fusion | flops 5767168 | bytes 18350080 | tf_op jit(solution)/shard_map/mul | solution.py:135
  393.2 17.0 %copy.99 = f32[128,2,11,1024]{3,2,1,0:T(8,128)} copy(f32[128,2,11,1024]{3,0,2,1:T(8,128)} %convert_multiply_fusion) | data formatting | bytes 23068672 | tf_op jit(solution)/shard_map/mul | solution.py:135
  410.2 21.9 %copy.103 = f32[32,8,11,1024]{3,1,2,0:T(8,128)} copy(f32[32,8,11,1024]{3,2,1,0:T(8,128)} %bitcast.367) | data formatting | bytes 23068672
  432.1 12.2 %copy.100 = f32[11264,256]{1,0:T(8,128)} copy(f32[11264,256]{0,1:T(8,128)} %bitcast.368) | data formatting | bytes 23068672 | tf_op jit(solution)/shard_map/dot_general | solution.py:142
  444.3 10.5 %fusion.3 = bf16[16,11,1024]{2,0,1:T(8,128)(2,1)} fusion(f32[11,1024,256]{2,1,0:T(8,128)} %bitcast.369, f32[16,1024]{1,0:T(8,128)S(1)} %get-tuple-element.73, s32[256]{0:T(256)S(1)} %eq.105, pred[256]{0:T(512)(128)(4,1)S(1)} %eq.109), kind=kOutput, calls=%fused_computation.14 | convolution fusion | flops 554016768 | bytes 11961600 | tf_op jit(solution)/shard_map/dot_general | solution.py:142
  (39 shorter events, 0.7 us)
Async XLA Ops:
  0.6 72.5 %copy-start = (bf16[128,11,1024]{2,0,1:T(8,128)(2,1)S(1)}, bf16[128,11,1024]{2,0,1:T(8,128)(2,1)}, u32[]{:S(2)}) copy-start(bf16[128,11,1024]{2,0,1:T(8,128)(2,1)} %param.15) | copy-start | bytes 8650756
  0.6 6.3 %copy-start.2 = (bf16[128,1024]{1,0:T(8,128)(2,1)S(1)}, bf16[128,1024]{1,0:T(8,128)(2,1)}, u32[]{:S(2)}) copy-start(bf16[128,1024]{1,0:T(8,128)(2,1)} %param.13) | copy-start | bytes 786436
  13.1 52.3 %all-to-all-start = ((bf16[128,2,1024]{2,1,0:T(2,128)(2,1)}), bf16[128,2,1024]{2,1,0:T(2,128)(2,1)}, u32[]{:S(2)}, u32[]{:S(2)}) async-start(bf16[128,2,1024]{2,1,0:T(2,128)(2,1)} %reshape.361), calls=%async_computation | async-start | bytes 1048576 | tf_op jit(solution)/shard_map/all_to_all | solution.py:128
  65.4 45.7 %all-to-all-start.1 = ((bf16[128,2,1024]{2,1,0:T(2,128)(2,1)}), bf16[128,2,1024]{2,1,0:T(2,128)(2,1)S(1)}, u32[]{:S(2)}, u32[]{:S(2)}) async-start(bf16[128,2,1024]{2,1,0:T(2,128)(2,1)} %reshape.362), calls=%async_computation.1 | async-start | bytes 1048576 | tf_op jit(solution)/shard_map/all_to_all | solution.py:127
  111.1 16.8 %copy-start.4 = (s32[16384]{0:T(1024)S(1)}, s32[16384]{0:T(1024)}, u32[]{:S(2)}) copy-start(s32[16384]{0:T(1024)} %param.16) | copy-start | bytes 196612
  111.1 17.5 %copy-start.5 = (s32[16384]{0:T(1024)S(1)}, s32[16384]{0:T(1024)}, u32[]{:S(2)}) copy-start(s32[16384]{0:T(1024)} %param.17) | copy-start | bytes 196612
  111.1 17.7 %copy-start.8 = (s32[32]{0:T(128)S(1)}, s32[32]{0:T(128)}, u32[]{:S(2)}) copy-start(s32[32]{0:T(128)} %param.19) | copy-start | bytes 388
  111.1 17.8 %copy-start.3 = (f32[10,4608]{1,0:T(8,128)S(1)}, f32[10,4608]{1,0:T(8,128)}, u32[]{:S(2)}) copy-start(f32[10,4608]{1,0:T(8,128)} %param.18) | copy-start | bytes 552964
  111.1 272.8 %all-to-all-start.2 = ((bf16[128,2,11,1024]{3,1,2,0:T(2,128)(2,1)}), bf16[128,2,11,1024]{3,1,2,0:T(2,128)(2,1)}, u32[]{:S(2)}, u32[]{:S(2)}) async-start(bf16[128,2,11,1024]{3,1,2,0:T(2,128)(2,1)} %broadcast_select_fusion), calls=%async_computation.2 | async-start | bytes 11534336 | tf_op jit(solution)/shard_map/all_to_all | solution.py:129
  127.8 20.1 %copy-start.7 = (s32[55]{0:T(128)S(1)}, s32[55]{0:T(128)}, u32[]{:S(2)}) copy-start(s32[55]{0:T(128)} %constant.142) | copy-start | bytes 664
  147.9 3.9 copy-start.6
  444.3 10.5 %copy-start.1 = (bf16[128,11,1024]{2,0,1:T(8,128)(2,1)S(1)}, bf16[128,11,1024]{2,0,1:T(8,128)(2,1)}, u32[]{:S(2)}) copy-start(bf16[128,11,1024]{2,0,1:T(8,128)(2,1)} %param.15) | copy-start | bytes 8650756
where the time goes:
time: 462 us; the launch traced here: 455 us
  waiting for transfers between devices  219 us (47%)
  local copies, waits for them, and re-layouts  118 us (26%)
  starting transfers between devices  44.1 us (10%)
  matrix products  24.3 us (5%)
  other arithmetic  24 us (5%)
  blocking collectives  24 us (5%)
    all_to_all x1, waiting for transfers between devices, shards(): lax.all_to_all(outgoing[2], 'tgt', split_axis=0, concat_axis=0, tiled=True)  188 us
    gather x4, local copies, waits for them, and re-layouts, packed(): gathered = jnp.take(values, source_row, axis=0, mode='fill', fill_value=0)  35.1 us
    all_to_all x1, waiting for transfers between devices, shards(): lax.all_to_all(outgoing[1], 'tgt', split_axis=0, concat_axis=0, tiled=True)  31.5 us
    unnamed x19, local copies, waits for them, and re-layouts  22 us
    all_to_all x1, starting transfers between devices, shards(): lax.all_to_all(outgoing[1], 'tgt', split_axis=0, concat_axis=0, tiled=True)  19.7 us
    mul x1, local copies, waits for them, and re-layouts, shards(): weight[:, :, None, :] * got_res.astype(jnp.float32)  17 us
    all_to_all x1, starting transfers between devices, shards(): lax.all_to_all(outgoing[2], 'tgt', split_axis=0, concat_axis=0, tiled=True)  16.7 us
    gather x24, local copies, waits for them, and re-layouts  16.7 us
  transfers between devices with their start and end apart: 3, of which 2 were waited for; matrix products, arithmetic and copies ran while one was open for 18% of the time, Pallas kernels for 0%

commit v1 on v0

v1 whole, which is shorter than its diff:
```python
import jax
import jax.numpy as jnp
import numpy as np
from jax import lax
from jax.experimental import pallas as pl
from jax.experimental.pallas import tpu as pltpu
from jax.sharding import PartitionSpec as P

TGT_DEV = 16
NDIAG = 11
Z_DEV = 8

XS, ZS, CS = 4, 16, 2
PLANE = XS * CS
QROWS = PLANE * TGT_DEV


def place(x, z, c):
    return ((x % XS) * ZS + z % ZS) * CS + c % CS


plane_groups = [[place(x, z, c) for x in range(XS) for c in range(CS)] for z in range(ZS)]
ring_groups = [[place(x, z, c) for z in range(ZS)] for x in range(XS) for c in range(CS)]


def ring_step(values, step):
    pairs = [
        (place(x, z, c), place(x, z + step, c))
        for x in range(XS)
        for z in range(ZS)
        for c in range(CS)
    ]
    return lax.ppermute(values, "tgt", pairs)


pair_first, pair_second = np.triu_indices(10)


def solve_normal(matrix, right_side):
    basis_count = right_side.shape[0]
    rows_of = [[None] * basis_count for column in range(basis_count)]
    for p in range(len(pair_first)):
        b = int(pair_first[p])
        c = int(pair_second[p])
        rows_of[b][c] = matrix[p]
        rows_of[c][b] = matrix[p]
    vector = [right_side[b] for b in range(basis_count)]
    for k in range(basis_count):
        inverse = 1.0 / rows_of[k][k]
        for r in range(k + 1, basis_count):
            factor = rows_of[r][k] * inverse
            for c in range(k + 1, basis_count):
                rows_of[r][c] = rows_of[r][c] - factor * rows_of[k][c]
            vector[r] = vector[r] - factor * vector[k]
    answer = [None] * basis_count
    for k in reversed(range(basis_count)):
        running = vector[k]
        for c in range(k + 1, basis_count):
            running = running - rows_of[k][c] * answer[c]
        answer[k] = running / rows_of[k][k]
    gain_total = right_side[0] * answer[0]
    for b in range(1, basis_count):
        gain_total = gain_total + right_side[b] * answer[b]
    return gain_total


def basis_windows(rest_basis, shifts, first_wave, length):

    def one_shift(shift_value):
        return lax.dynamic_slice_in_dim(rest_basis, first_wave + shift_value, length, axis=1)

    return jax.vmap(one_shift)(shifts)


def normal_terms(weight_sum, flux_sum, windows):
    products = windows[:, pair_first, :] * windows[:, pair_second, :]
    matrix = jnp.einsum("ti,zpi->ztp", weight_sum, products, precision=lax.Precision.HIGHEST)
    right_side = jnp.einsum("ti,zbi->ztb", flux_sum, windows, precision=lax.Precision.HIGHEST)
    return (matrix, right_side)


def fit_from(matrix, right_side):
    pairs = jnp.transpose(matrix, (2, 0, 1)).reshape(matrix.shape[2], -1)
    sides = jnp.transpose(right_side, (2, 0, 1)).reshape(right_side.shape[2], -1)
    gain = solve_normal(pairs, sides).reshape(matrix.shape[0], matrix.shape[1])
    return gain.T


GROUP = 4


def pack_kernel(ivar_ref, flux_ref, res_ref, out_ref):
    out_ref[0, 0] = ivar_ref[...]
    out_ref[0, 1] = flux_ref[...]
    for diagonal in range(NDIAG):
        out_ref[0, 2 + diagonal] = res_ref[diagonal]


def pack(ivar, flux, res):
    row_count, wave_dev = ivar.shape
    lanes = wave_dev // PLANE
    planes = NDIAG + 2
    return pl.pallas_call(
        pack_kernel,
        out_shape=jax.ShapeDtypeStruct((PLANE, planes, row_count, lanes), ivar.dtype),
        grid=(PLANE,),
        in_specs=[
            pl.BlockSpec((row_count, lanes), lambda i: (0, i)),
            pl.BlockSpec((row_count, lanes), lambda i: (0, i)),
            pl.BlockSpec((NDIAG, row_count, lanes), lambda i: (0, 0, i)),
        ],
        out_specs=pl.BlockSpec((1, planes, row_count, lanes), lambda i: (i, 0, 0, 0)),
        cost_estimate=pl.CostEstimate(
            flops=0, bytes_accessed=4 * planes * row_count * wave_dev, transcendentals=0
        ),
    )(ivar, flux, res)


def coadd_kernel(target_ref, rows_ref, sums_ref, res_ref, terms):
    sources, planes, row_count, lanes = rows_ref.shape
    step = pl.program_id(0)

    @pl.when(step == 0)
    def fill_terms():
        def one_source(source, carry):
            rows = pl.ds(pl.multiple_of(source * row_count, row_count), row_count)
            weight = rows_ref[source, 0].astype(jnp.float32)
            terms[rows, 0:lanes] = rows_ref[source, 0]
            product = weight * rows_ref[source, 1].astype(jnp.float32)
            rounded = product.astype(jnp.bfloat16)
            terms[rows, lanes : 2 * lanes] = rounded
            rest = product - rounded.astype(jnp.float32)
            terms[rows, 2 * lanes : 3 * lanes] = rest.astype(jnp.bfloat16)
            for plane in range(2, planes):
                product = weight * rows_ref[source, plane].astype(jnp.float32)
                terms[rows, (plane + 1) * lanes : (plane + 2) * lanes] = product.astype(
                    jnp.bfloat16
                )
            return carry

        lax.fori_loop(0, sources, one_source, 0)

    per_x = CS * TGT_DEV
    local = lax.broadcasted_iota(jnp.int32, (GROUP * QROWS, 1), 0)
    q = local % QROWS
    plane_z = step * GROUP + local // QROWS
    wanted = (q // per_x) * (ZS * per_x) + plane_z * per_x + q % per_x
    member = jnp.where(target_ref[...] == wanted, 1.0, 0.0).astype(jnp.bfloat16)
    sums = jnp.dot(member, terms[...], preferred_element_type=jnp.float32)
    for g in range(GROUP):
        block = sums[g * QROWS : (g + 1) * QROWS]
        sums_ref[g, 0] = block[:, 0:lanes]
        sums_ref[g, 1] = block[:, lanes : 2 * lanes] + block[:, 2 * lanes : 3 * lanes]
        for diagonal in range(planes - 2):
            piece = block[:, (diagonal + 3) * lanes : (diagonal + 4) * lanes]
            res_ref[g, diagonal] = piece.astype(jnp.bfloat16)


def coadd(targets, rows):
    sources, planes, row_count, lanes = rows.shape
    return pl.pallas_call(
        coadd_kernel,
        out_shape=(
            jax.ShapeDtypeStruct((ZS, 2, QROWS, lanes), jnp.float32),
            jax.ShapeDtypeStruct((ZS, planes - 2, QROWS, lanes), jnp.bfloat16),
        ),
        grid=(ZS // GROUP,),
        in_specs=[
            pl.BlockSpec((1, sources * row_count), lambda i: (0, 0)),
            pl.BlockSpec(rows.shape, lambda i: (0, 0, 0, 0)),
        ],
        out_specs=(
            pl.BlockSpec((GROUP, 2, QROWS, lanes), lambda i: (i, 0, 0, 0)),
            pl.BlockSpec((GROUP, planes - 2, QROWS, lanes), lambda i: (i, 0, 0, 0)),
        ),
        scratch_shapes=[pltpu.VMEM((sources * row_count, (planes + 1) * lanes), jnp.bfloat16)],
        compiler_params=pltpu.CompilerParams(vmem_limit_bytes=56 << 20),
        cost_estimate=pl.CostEstimate(
            flops=2 * ZS * QROWS * sources * row_count * (planes + 1) * lanes,
            bytes_accessed=2 * (rows.size + ZS * QROWS * planes * lanes),
            transcendentals=0,
        ),
    )(targets, rows)


def shards(
    exposure_flux,
    exposure_ivar,
    exposure_res,
    target_of_row,
    valid_of_row,
    rest_basis,
    redshift_shift,
):
    device = lax.axis_index("tgt")
    my_z = (device // CS) % ZS
    row_count, wave_dev = exposure_flux.shape
    lanes = wave_dev // PLANE
    outgoing = pack(exposure_ivar, exposure_flux, jnp.transpose(exposure_res, (1, 0, 2)))
    rows = lax.all_to_all(
        outgoing, "tgt", split_axis=0, concat_axis=0, axis_index_groups=plane_groups, tiled=True
    )
    masked = jnp.where(valid_of_row == 1, target_of_row, -1).reshape(XS, ZS, CS * row_count)
    targets = lax.dynamic_index_in_dim(masked, my_z, 1, keepdims=False).reshape(1, -1)
    part_sums, part_res = coadd(targets, rows)

    res_sum = lax.psum_scatter(
        part_res, "tgt", scatter_dimension=0, axis_index_groups=ring_groups, tiled=False
    )

    def part(offset):
        return lax.dynamic_index_in_dim(part_sums, (my_z + offset) % ZS, 0, keepdims=False)

    half = ZS // 2
    up, down = part(half), part(half + 1)
    for s in range(half):
        up = ring_step(up, 1)
        if s < half - 1:
            up = up + part(half - 1 - s)
            down = ring_step(down, -1)
            if s < half - 2:
                down = down + part(half + 2 + s)
    sums = part(0) + up + down

    def to_owner(values):
        kinds = values.shape[0]
        split = jnp.transpose(values.reshape(kinds, PLANE, TGT_DEV, lanes), (1, 0, 2, 3))
        back = lax.all_to_all(
            split, "tgt", split_axis=0, concat_axis=0, axis_index_groups=plane_groups, tiled=True
        )
        return jnp.transpose(back, (1, 2, 0, 3)).reshape(kinds, TGT_DEV, wave_dev)

    own = to_owner(sums)
    everything = lax.all_gather(own.astype(jnp.bfloat16), "band", axis=2, tiled=True)
    everything = everything.astype(jnp.float32)
    own_weight = own[0]
    coadd_flux = own[1] / own_weight
    band_index = lax.axis_index("band")
    shifts = lax.dynamic_slice_in_dim(redshift_shift, band_index * Z_DEV, Z_DEV)
    windows = basis_windows(rest_basis, shifts, 0, everything.shape[2])
    fit_gain = fit_from(*normal_terms(everything[0], everything[1], windows))

    own_res = to_owner(res_sum).astype(jnp.float32)
    coadd_res = jnp.transpose((own_res / own_weight[None]).astype(jnp.bfloat16), (1, 0, 2))
    return (coadd_flux, coadd_res, fit_gain)


def solution(mesh):
    in_specs = (P("tgt", "band"), P("tgt", "band"), P("tgt", None, "band"), P(), P(), P(), P())
    out_specs = (P("tgt", "band"), P("tgt", None, "band"), P("tgt", "band"))
    return jax.shard_map(shards, mesh=mesh, in_specs=in_specs, out_specs=out_specs, check_vma=False)
```

time: 462 us -> 242 us (0.52)
  the two profiles are of different devices: /device:TPU:60 before, /device:TPU:1 now
where the time goes in v1:
time: 242 us; the launch traced here: 241 us
  starting transfers between devices  83.8 us (35%)
  waiting for transfers between devices  73.2 us (30%)
  local copies, waits for them, and re-layouts  26 us (11%)
  Pallas kernels  18.5 us (8%)
  between operations  14.7 us (6%)
  blocking collectives  10.1 us (4%)
  matrix products  8.07 us (3%)
  other arithmetic  5.95 us (2%)
    ppermute x15, starting transfers between devices, ring_step(): return lax.ppermute(values, 'tgt', pairs)  53.5 us
    all_to_all x1, waiting for transfers between devices, shards(): lax.all_to_all(outgoing, 'tgt', split_axis=0, concat_axis=0, axis_index_g...  38.9 us
    ppermute x15, waiting for transfers between devices, ring_step(): return lax.ppermute(values, 'tgt', pairs)  28 us
    all_to_all x2, starting transfers between devices, to_owner(): lax.all_to_all(split, 'tgt', split_axis=0, concat_axis=0, axis_index_grou...  19.8 us
    pallas_call x1, Pallas kernels, coadd(): pl.pallas_call(coadd_kernel, out_shape=(jax.ShapeDtypeStruct((ZS, 2, QROW...  12.2 us
    gather x24, local copies, waits for them, and re-layouts  10.9 us
    all_to_all x1, starting transfers between devices, shards(): lax.all_to_all(outgoing, 'tgt', split_axis=0, concat_axis=0, axis_index_g...  10.6 us
    all_gather x1, blocking collectives, shards(): lax.all_gather(own.astype(jnp.bfloat16), 'band', axis=2, tiled=True)  10.1 us
  transfers between devices with their start and end apart: 19, of which 14 were waited for; matrix products, arithmetic and copies ran while one was open for 14% of the time, Pallas kernels for 0%

profile of v1, /device:TPU:1, one launch (start us, length us, event | category | flops | bytes accessed | tf_op | source)
XLA Modules:
  0.0 240.5 jit_solution(3582095878799384056)
XLA Ops:
  7.2 6.3 %shard_map.130 = bf16[8,13,128,128]{3,2,1,0:T(8,128)(2,1)} custom-call(bf16[128,1024]{1,0:T(8,128)(2,1)} %ivar_ref.1, bf16[128,1024]{1,0:T(8,128)(2,1)} %flux_ref.1, bf16[11,128,1024]{2,1,0:T(8,128)(2,1)} %bitcast.425), custom_call_target="tpu_custom_call" | custom-call | bytes 6815744 | tf_op jit(solution)/shard_map/pallas_call | solution.py:103
  13.5 10.6 %all-to-all-start = ((bf16[8,13,128,128]{3,2,1,0:T(8,128)(2,1)}), bf16[8,13,128,128]{3,2,1,0:T(8,128)(2,1)S(1)}, u32[]{:S(2)}, u32[]{:S(2)}) async-start(bf16[8,13,128,128]{3,2,1,0:T(8,128)(2,1)} %shard_map.130), calls=%async_computation | async-start | bytes 6815744 | tf_op jit(solution)/shard_map/all_to_all | solution.py:200
  24.1 0.9 compare_select_fusion
  24.9 0.6 constant_dynamic-slice_fusion.1
  25.5 38.9 %all-to-all-done.rows_ref = bf16[8,13,128,128]{3,2,1,0:T(8,128)(2,1)S(1)} async-done(((bf16[8,13,128,128]{3,2,1,0:T(8,128)(2,1)}), bf16[8,13,128,128]{3,2,1,0:T(8,128)(2,1)S(1)}, u32[]{:S(2)}, u32[]{:S(2)}) %all-to-all-start) | async-done | bytes 3407904 | tf_op jit(solution)/shard_map/all_to_all | solution.py:200
  64.5 1.7 copy-done.1
  66.2 12.2 %shard_map.131 = (f32[16,2,128,128]{3,2,1,0:T(8,128)}, bf16[16,11,128,128]{3,2,1,0:T(8,128)(2,1)}) custom-call(s32[1,1024]{1,0:T(1,128)} %bitcast.443, bf16[8,13,128,128]{3,2,1,0:T(8,128)(2,1)} %copy-done.1), custom_call_target="tpu_custom_call" | custom-call | flops 7516192768 | bytes 10223616 | tf_op jit(solution)/shard_map/pallas_call | solution.py:161
  78.5 1.5 copy-done.2
  80.0 1.9 collective-permute-start
  81.9 6.5 %collective-permute-start.8 = (f32[2,128,128]{2,1,0:T(8,128)S(1)}, f32[2,128,128]{2,1,0:T(8,128)S(1)}, u32[]{:S(2)}, u32[]{:S(2)}) collective-permute-start(f32[2,128,128]{2,1,0:T(8,128)S(1)} %get-tuple-element.36), channel_id=1, source_target_pairs={{0,120},{4,124},{8,0},{12,4},{16,8},{20,12},{24,16},{28,20},{32,24... | collective-permute-start | bytes 393224 | tf_op jit(solution)/shard_map/ppermute | solution.py:33
  88.4 1.0 collective-permute-done
  89.5 1.9 collective-permute-start.1
  91.4 4.9 %collective-permute-done.1 = f32[2,128,128]{2,1,0:T(8,128)S(1)} collective-permute-done((f32[2,128,128]{2,1,0:T(8,128)S(1)}, f32[2,128,128]{2,1,0:T(8,128)S(1)}, u32[]{:S(2)}, u32[]{:S(2)}) %collective-permute-start.1) | collective-permute-done | bytes 131104 | tf_op jit(solution)/shard_map/ppermute | solution.py:33
  96.4 1.9 collective-permute-start.2
  98.3 4.6 %collective-permute-start.9 = (f32[2,128,128]{2,1,0:T(8,128)S(1)}, f32[2,128,128]{2,1,0:T(8,128)S(1)}, u32[]{:S(2)}, u32[]{:S(2)}) collective-permute-start(f32[2,128,128]{2,1,0:T(8,128)S(1)} %get-tuple-element.34), channel_id=1, source_target_pairs={{0,120},{4,124},{8,0},{12,4},{16,8},{20,12},{24,16},{28,20},{32,24... | collective-permute-start | bytes 393224 | tf_op jit(solution)/shard_map/ppermute | solution.py:33
  103.0 3.5 %collective-permute-done.2 = f32[2,128,128]{2,1,0:T(8,128)S(1)} collective-permute-done((f32[2,128,128]{2,1,0:T(8,128)S(1)}, f32[2,128,128]{2,1,0:T(8,128)S(1)}, u32[]{:S(2)}, u32[]{:S(2)}) %collective-permute-start.2) | collective-permute-done | bytes 131104 | tf_op jit(solution)/shard_map/ppermute | solution.py:33
  106.5 0.9 collective-permute-done.9
  107.5 1.9 collective-permute-start.3
  109.4 5.4 %collective-permute-start.10 = (f32[2,128,128]{2,1,0:T(8,128)S(1)}, f32[2,128,128]{2,1,0:T(8,128)S(1)}, u32[]{:S(2)}, u32[]{:S(2)}) collective-permute-start(f32[2,128,128]{2,1,0:T(8,128)S(1)} %get-tuple-element.32), channel_id=1, source_target_pairs={{0,120},{4,124},{8,0},{12,4},{16,8},{20,12},{24,16},{28,20},{32,24... | collective-permute-start | bytes 393224 | tf_op jit(solution)/shard_map/ppermute | solution.py:33
  114.9 3.7 %collective-permute-done.3 = f32[2,128,128]{2,1,0:T(8,128)S(1)} collective-permute-done((f32[2,128,128]{2,1,0:T(8,128)S(1)}, f32[2,128,128]{2,1,0:T(8,128)S(1)}, u32[]{:S(2)}, u32[]{:S(2)}) %collective-permute-start.3) | collective-permute-done | bytes 131104 | tf_op jit(solution)/shard_map/ppermute | solution.py:33
  118.6 0.7 collective-permute-done.10
  119.4 1.9 collective-permute-start.4
  121.3 5.4 %collective-permute-start.11 = (f32[2,128,128]{2,1,0:T(8,128)S(1)}, f32[2,128,128]{2,1,0:T(8,128)S(1)}, u32[]{:S(2)}, u32[]{:S(2)}) collective-permute-start(f32[2,128,128]{2,1,0:T(8,128)S(1)} %get-tuple-element.30), channel_id=1, source_target_pairs={{0,120},{4,124},{8,0},{12,4},{16,8},{20,12},{24,16},{28,20},{32,24... | collective-permute-start | bytes 393224 | tf_op jit(solution)/shard_map/ppermute | solution.py:33
  126.8 3.7 %collective-permute-done.4 = f32[2,128,128]{2,1,0:T(8,128)S(1)} collective-permute-done((f32[2,128,128]{2,1,0:T(8,128)S(1)}, f32[2,128,128]{2,1,0:T(8,128)S(1)}, u32[]{:S(2)}, u32[]{:S(2)}) %collective-permute-start.4) | collective-permute-done | bytes 131104 | tf_op jit(solution)/shard_map/ppermute | solution.py:33
  130.5 0.6 collective-permute-done.11
  131.2 1.9 collective-permute-start.5
  133.1 5.4 %collective-permute-start.12 = (f32[2,128,128]{2,1,0:T(8,128)S(1)}, f32[2,128,128]{2,1,0:T(8,128)S(1)}, u32[]{:S(2)}, u32[]{:S(2)}) collective-permute-start(f32[2,128,128]{2,1,0:T(8,128)S(1)} %get-tuple-element.28), channel_id=1, source_target_pairs={{0,120},{4,124},{8,0},{12,4},{16,8},{20,12},{24,16},{28,20},{32,24... | collective-permute-start | bytes 393224 | tf_op jit(solution)/shard_map/ppermute | solution.py:33
  138.6 3.7 %collective-permute-done.5 = f32[2,128,128]{2,1,0:T(8,128)S(1)} collective-permute-done((f32[2,128,128]{2,1,0:T(8,128)S(1)}, f32[2,128,128]{2,1,0:T(8,128)S(1)}, u32[]{:S(2)}, u32[]{:S(2)}) %collective-permute-start.5) | collective-permute-done | bytes 131104 | tf_op jit(solution)/shard_map/ppermute | solution.py:33
  142.3 0.6 collective-permute-done.12
  142.9 0.7 bitcast_add_fusion.7
  143.6 3.3 %collective-permute-start.6 = (f32[2,128,128]{2,1,0:T(8,128)}, f32[2,128,128]{2,1,0:T(8,128)S(1)}, u32[]{:S(2)}, u32[]{:S(2)}) collective-permute-start(f32[2,128,128]{2,1,0:T(8,128)} %get-tuple-element.25), channel_id=1, source_target_pairs={{0,8},{4,12},{8,16},{12,20},{16,24},{20,28},{24,32},{28,36},{32,40... | collective-permute-start | bytes 393224 | tf_op jit(solution)/shard_map/ppermute | solution.py:33
  146.9 4.0 %collective-permute-start.13 = (f32[2,128,128]{2,1,0:T(8,128)S(1)}, f32[2,128,128]{2,1,0:T(8,128)S(1)}, u32[]{:S(2)}, u32[]{:S(2)}) collective-permute-start(f32[2,128,128]{2,1,0:T(8,128)S(1)} %get-tuple-element.26), channel_id=1, source_target_pairs={{0,120},{4,124},{8,0},{12,4},{16,8},{20,12},{24,16},{28,20},{32,24... | collective-permute-start | bytes 393224 | tf_op jit(solution)/shard_map/ppermute | solution.py:33
  151.1 3.8 %collective-permute-done.6 = f32[2,128,128]{2,1,0:T(8,128)S(1)} collective-permute-done((f32[2,128,128]{2,1,0:T(8,128)}, f32[2,128,128]{2,1,0:T(8,128)S(1)}, u32[]{:S(2)}, u32[]{:S(2)}) %collective-permute-start.6) | collective-permute-done | bytes 131104 | tf_op jit(solution)/shard_map/ppermute | solution.py:33
  155.0 0.5 collective-permute-done.13
  155.5 1.0 bitcast_add_fusion.6
  156.5 4.7 %collective-permute-start.7 = (f32[2,128,128]{2,1,0:T(8,128)S(1)}, f32[2,128,128]{2,1,0:T(8,128)S(1)}, u32[]{:S(2)}, u32[]{:S(2)}) collective-permute-start(f32[2,128,128]{2,1,0:T(8,128)S(1)} %get-tuple-element.23), channel_id=1, source_target_pairs={{0,8},{4,12},{8,16},{12,20},{16,24},{20,28},{24,32},{28,36},{32,40... | collective-permute-start | bytes 393224 | tf_op jit(solution)/shard_map/ppermute | solution.py:33
  161.2 2.6 %collective-permute-start.14 = (f32[2,128,128]{2,1,0:T(8,128)S(1)}, f32[2,128,128]{2,1,0:T(8,128)S(1)}, u32[]{:S(2)}, u32[]{:S(2)}) collective-permute-start(f32[2,128,128]{2,1,0:T(8,128)S(1)} %get-tuple-element.24), channel_id=1, source_target_pairs={{0,120},{4,124},{8,0},{12,4},{16,8},{20,12},{24,16},{28,20},{32,24... | collective-permute-start | bytes 393224 | tf_op jit(solution)/shard_map/ppermute | solution.py:33
  163.9 11.1 %while.1 = (s32[]{:T(128)}, f32[10,4608]{1,0:T(8,128)S(1)}, s32[8,2]{0,1:T(2,128)S(1)}, f32[8,10,4096]{2,1,0:T(8,128)S(1)}, s32[]{:T(128)}) while((s32[]{:T(128)}, f32[10,4608]{1,0:T(8,128)S(1)}, s32[8,2]{0,1:T(2,128)S(1)}, f32[8,10,4096]{2,1,0:T(8,128)S(1)}, s32[]{:T(128)}) %tuple.42), condition=%wide.while_cond, body=%wide.while_body.sunk | while | flops 2 | bytes 524393 | solution.py:70
  164.0 0.5 slice.756
  164.5 0.8 bitcast_dynamic-update-slice_fusion.2
  165.4 0.5 slice.756
  165.9 0.8 bitcast_dynamic-update-slice_fusion.2
  166.8 0.5 slice.756
  167.3 0.8 bitcast_dynamic-update-slice_fusion.2
  168.7 0.8 bitcast_dynamic-update-slice_fusion.2
  170.0 0.8 bitcast_dynamic-update-slice_fusion.2
  171.4 0.8 bitcast_dynamic-update-slice_fusion.2
  172.8 0.8 bitcast_dynamic-update-slice_fusion.2
  174.2 0.8 bitcast_dynamic-update-slice_fusion.2
  175.0 0.9 fusion.8
  176.0 0.7 copy.33
  176.6 12.6 %all-to-all-start.1 = ((f32[8,2,16,128]{3,2,1,0:T(8,128)}), f32[8,2,16,128]{3,2,1,0:T(8,128)S(1)}, u32[]{:S(2)}, u32[]{:S(2)}) async-start(f32[8,2,16,128]{3,2,1,0:T(8,128)} %copy.33), calls=%async_computation.1 | async-start | bytes 262144 | tf_op jit(solution)/shard_map/all_to_all | solution.py:228
  189.2 0.8 copy.39
  190.0 4.0 %gather_fusion.1 = f32[55,8,4096]{2,1,0:T(8,128)} fusion(f32[8,10,4096]{2,0,1:T(8,128)S(1)} %copy.39, s32[1024]{0:T(1024)S(1)} %pad_clamp_fusion), kind=kCustom, calls=%fused_computation.1 | custom fusion | bytes 14418140 | tf_op jit(solution)/shard_map/gather | solution.py:76
  194.0 3.9 %gather_fusion = f32[55,8,4096]{2,1,0:T(8,128)} fusion(f32[8,10,4096]{2,0,1:T(8,128)S(1)} %copy.39, s32[1024]{0:T(1024)S(1)} %pad_clamp_fusion.1), kind=kCustom, calls=%fused_computation | custom fusion | bytes 14418140 | tf_op jit(solution)/shard_map/gather | solution.py:76
  197.9 10.1 %all_gather.3 = bf16[2,16,4096]{2,1,0:T(8,128)(2,1)S(1)} all-gather(bf16[2,16,1024]{2,1,0:T(8,128)(2,1)S(1)} %copy_bitcast_fusion.2), channel_id=1, replica_groups=mesh['tgt'=128,'band'=4] {'band'}, dimensions={2}, use_global_device_ids=true | all-gather | bytes 327680 | tf_op jit(solution)/shard_map/all_gather | solution.py:234
  208.0 1.1 convolution_bitcast_fusion
  209.2 7.0 %fusion.3 = f32[55,8,16]{2,1,0:T(8,128)S(1)} fusion(f32[55,8,4096]{2,1,0:T(8,128)} %gather_fusion, f32[55,8,4096]{2,1,0:T(8,128)} %gather_fusion.1, bf16[2,16,4096]{2,1,0:T(8,128)(2,1)S(1)} %all_gather.3), kind=kOutput, calls=%fused_computation.7 | convolution fusion | flops 347832320 | bytes 14577152 | tf_op jit(solution)/shard_map/ti,zpi->ztp/dot_general | solution.py:77
  216.2 1.7 copy.54
  217.9 7.2 %all-to-all-start.2 = ((bf16[8,11,16,128]{3,2,1,0:T(8,128)(2,1)}), bf16[8,11,16,128]{3,2,1,0:T(8,128)(2,1)S(1)}, u32[]{:S(2)}, u32[]{:S(2)}) async-start(bf16[8,11,16,128]{3,2,1,0:T(8,128)(2,1)} %bitcast.419), calls=%async_computation.3 | async-start | bytes 720896 | tf_op jit(solution)/shard_map/all_to_all | solution.py:228
  225.1 0.8 add_bitcast_fusion
  226.0 0.7 bitcast_divide_fusion.1
  226.7 6.2 %all-to-all-done.2 = bf16[8,11,16,128]{3,2,1,0:T(8,128)(2,1)S(1)} async-done(((bf16[8,11,16,128]{3,2,1,0:T(8,128)(2,1)}), bf16[8,11,16,128]{3,2,1,0:T(8,128)(2,1)S(1)}, u32[]{:S(2)}, u32[]{:S(2)}) %all-to-all-start.2) | async-done | bytes 360480 | tf_op jit(solution)/shard_map/all_to_all | solution.py:228
  232.9 0.8 fusion.7
  (50 shorter events, 3.6 us)
Async XLA Ops:
  13.5 10.6 %copy-start.3 = (s32[16384]{0:T(1024)S(1)}, s32[16384]{0:T(1024)}, u32[]{:S(2)}) copy-start(s32[16384]{0:T(1024)} %param.14) | copy-start | bytes 196612
  13.5 51.0 %all-to-all-start = ((bf16[8,13,128,128]{3,2,1,0:T(8,128)(2,1)}), bf16[8,13,128,128]{3,2,1,0:T(8,128)(2,1)S(1)}, u32[]{:S(2)}, u32[]{:S(2)}) async-start(bf16[8,13,128,128]{3,2,1,0:T(8,128)(2,1)} %shard_map.130), calls=%async_computation | async-start | bytes 6815744 | tf_op jit(solution)/shard_map/all_to_all | solution.py:200
  24.1 192.1 %reduce-scatter.2.cloned.1.call-start = ((), (), s32[]{:S(2)}) async-start(), calls=%async_computation.4 | async-start | bytes 6127616 | tf_op jit(solution)/shard_map/reduce_scatter | solution.py:207
  64.4 1.7 copy-start.1
  78.4 1.6 copy-start.2
  80.0 9.4 %collective-permute-start = (f32[2,128,128]{2,1,0:T(8,128)S(1)}, f32[2,128,128]{2,1,0:T(8,128)S(1)}, u32[]{:S(2)}, u32[]{:S(2)}) collective-permute-start(f32[2,128,128]{2,1,0:T(8,128)S(1)} %get-tuple-element.35), channel_id=1, source_target_pairs={{0,8},{4,12},{8,16},{12,20},{16,24},{20,28},{24,32},{28,36},{32,40... | collective-permute-start | bytes 393224 | tf_op jit(solution)/shard_map/ppermute | solution.py:33
  81.9 9.5 %collective-permute-start.8 = (f32[2,128,128]{2,1,0:T(8,128)S(1)}, f32[2,128,128]{2,1,0:T(8,128)S(1)}, u32[]{:S(2)}, u32[]{:S(2)}) collective-permute-start(f32[2,128,128]{2,1,0:T(8,128)S(1)} %get-tuple-element.36), channel_id=1, source_target_pairs={{0,120},{4,124},{8,0},{12,4},{16,8},{20,12},{24,16},{28,20},{32,24... | collective-permute-start | bytes 393224 | tf_op jit(solution)/shard_map/ppermute | solution.py:33
  89.5 6.9 %collective-permute-start.1 = (f32[2,128,128]{2,1,0:T(8,128)S(1)}, f32[2,128,128]{2,1,0:T(8,128)S(1)}, u32[]{:S(2)}, u32[]{:S(2)}) collective-permute-start(f32[2,128,128]{2,1,0:T(8,128)S(1)} %bitcast_add_fusion.12), channel_id=1, source_target_pairs={{0,8},{4,12},{8,16},{12,20},{16,24},{20,28},{24,32},{28,36},{32,40... | collective-permute-start | bytes 393224 | tf_op jit(solution)/shard_map/ppermute | solution.py:33
  91.4 59.6 %copy-start.6 = (s32[32]{0:T(128)S(1)}, s32[32]{0:T(128)}, u32[]{:S(2)}) copy-start(s32[32]{0:T(128)} %param.17) | copy-start | bytes 388
  96.4 10.1 %collective-permute-start.2 = (f32[2,128,128]{2,1,0:T(8,128)S(1)}, f32[2,128,128]{2,1,0:T(8,128)S(1)}, u32[]{:S(2)}, u32[]{:S(2)}) collective-permute-start(f32[2,128,128]{2,1,0:T(8,128)S(1)} %get-tuple-element.33), channel_id=1, source_target_pairs={{0,8},{4,12},{8,16},{12,20},{16,24},{20,28},{24,32},{28,36},{32,40... | collective-permute-start | bytes 393224 | tf_op jit(solution)/shard_map/ppermute | solution.py:33
  98.3 9.1 %collective-permute-start.9 = (f32[2,128,128]{2,1,0:T(8,128)S(1)}, f32[2,128,128]{2,1,0:T(8,128)S(1)}, u32[]{:S(2)}, u32[]{:S(2)}) collective-permute-start(f32[2,128,128]{2,1,0:T(8,128)S(1)} %get-tuple-element.34), channel_id=1, source_target_pairs={{0,120},{4,124},{8,0},{12,4},{16,8},{20,12},{24,16},{28,20},{32,24... | collective-permute-start | bytes 393224 | tf_op jit(solution)/shard_map/ppermute | solution.py:33
  103.0 60.9 %copy-start = (f32[10,4608]{1,0:T(8,128)S(1)}, f32[10,4608]{1,0:T(8,128)}, u32[]{:S(2)}) copy-start(f32[10,4608]{1,0:T(8,128)} %param.16) | copy-start | bytes 552964
  107.5 11.1 %collective-permute-start.3 = (f32[2,128,128]{2,1,0:T(8,128)S(1)}, f32[2,128,128]{2,1,0:T(8,128)S(1)}, u32[]{:S(2)}, u32[]{:S(2)}) collective-permute-start(f32[2,128,128]{2,1,0:T(8,128)S(1)} %get-tuple-element.31), channel_id=1, source_target_pairs={{0,8},{4,12},{8,16},{12,20},{16,24},{20,28},{24,32},{28,36},{32,40... | collective-permute-start | bytes 393224 | tf_op jit(solution)/shard_map/ppermute | solution.py:33
  109.4 10.0 %collective-permute-start.10 = (f32[2,128,128]{2,1,0:T(8,128)S(1)}, f32[2,128,128]{2,1,0:T(8,128)S(1)}, u32[]{:S(2)}, u32[]{:S(2)}) collective-permute-start(f32[2,128,128]{2,1,0:T(8,128)S(1)} %get-tuple-element.32), channel_id=1, source_target_pairs={{0,120},{4,124},{8,0},{12,4},{16,8},{20,12},{24,16},{28,20},{32,24... | collective-permute-start | bytes 393224 | tf_op jit(solution)/shard_map/ppermute | solution.py:33
  119.4 11.2 %collective-permute-start.4 = (f32[2,128,128]{2,1,0:T(8,128)S(1)}, f32[2,128,128]{2,1,0:T(8,128)S(1)}, u32[]{:S(2)}, u32[]{:S(2)}) collective-permute-start(f32[2,128,128]{2,1,0:T(8,128)S(1)} %get-tuple-element.29), channel_id=1, source_target_pairs={{0,8},{4,12},{8,16},{12,20},{16,24},{20,28},{24,32},{28,36},{32,40... | collective-permute-start | bytes 393224 | tf_op jit(solution)/shard_map/ppermute | solution.py:33
  121.3 9.9 %collective-permute-start.11 = (f32[2,128,128]{2,1,0:T(8,128)S(1)}, f32[2,128,128]{2,1,0:T(8,128)S(1)}, u32[]{:S(2)}, u32[]{:S(2)}) collective-permute-start(f32[2,128,128]{2,1,0:T(8,128)S(1)} %get-tuple-element.30), channel_id=1, source_target_pairs={{0,120},{4,124},{8,0},{12,4},{16,8},{20,12},{24,16},{28,20},{32,24... | collective-permute-start | bytes 393224 | tf_op jit(solution)/shard_map/ppermute | solution.py:33
  131.2 11.1 %collective-permute-start.5 = (f32[2,128,128]{2,1,0:T(8,128)S(1)}, f32[2,128,128]{2,1,0:T(8,128)S(1)}, u32[]{:S(2)}, u32[]{:S(2)}) collective-permute-start(f32[2,128,128]{2,1,0:T(8,128)S(1)} %get-tuple-element.27), channel_id=1, source_target_pairs={{0,8},{4,12},{8,16},{12,20},{16,24},{20,28},{24,32},{28,36},{32,40... | collective-permute-start | bytes 393224 | tf_op jit(solution)/shard_map/ppermute | solution.py:33
  133.1 9.8 %collective-permute-start.12 = (f32[2,128,128]{2,1,0:T(8,128)S(1)}, f32[2,128,128]{2,1,0:T(8,128)S(1)}, u32[]{:S(2)}, u32[]{:S(2)}) collective-permute-start(f32[2,128,128]{2,1,0:T(8,128)S(1)} %get-tuple-element.28), channel_id=1, source_target_pairs={{0,120},{4,124},{8,0},{12,4},{16,8},{20,12},{24,16},{28,20},{32,24... | collective-permute-start | bytes 393224 | tf_op jit(solution)/shard_map/ppermute | solution.py:33
  143.6 11.3 %collective-permute-start.6 = (f32[2,128,128]{2,1,0:T(8,128)}, f32[2,128,128]{2,1,0:T(8,128)S(1)}, u32[]{:S(2)}, u32[]{:S(2)}) collective-permute-start(f32[2,128,128]{2,1,0:T(8,128)} %get-tuple-element.25), channel_id=1, source_target_pairs={{0,8},{4,12},{8,16},{12,20},{16,24},{20,28},{24,32},{28,36},{32,40... | collective-permute-start | bytes 393224 | tf_op jit(solution)/shard_map/ppermute | solution.py:33
  146.9 8.6 %collective-permute-start.13 = (f32[2,128,128]{2,1,0:T(8,128)S(1)}, f32[2,128,128]{2,1,0:T(8,128)S(1)}, u32[]{:S(2)}, u32[]{:S(2)}) collective-permute-start(f32[2,128,128]{2,1,0:T(8,128)S(1)} %get-tuple-element.26), channel_id=1, source_target_pairs={{0,120},{4,124},{8,0},{12,4},{16,8},{20,12},{24,16},{28,20},{32,24... | collective-permute-start | bytes 393224 | tf_op jit(solution)/shard_map/ppermute | solution.py:33
  156.5 32.7 %copy-start.5 = (s32[55]{0:T(128)S(1)}, s32[55]{0:T(128)}, u32[]{:S(2)}) copy-start(s32[55]{0:T(128)} %constant.205) | copy-start | bytes 664
  156.5 18.5 %collective-permute-start.7 = (f32[2,128,128]{2,1,0:T(8,128)S(1)}, f32[2,128,128]{2,1,0:T(8,128)S(1)}, u32[]{:S(2)}, u32[]{:S(2)}) collective-permute-start(f32[2,128,128]{2,1,0:T(8,128)S(1)} %get-tuple-element.23), channel_id=1, source_target_pairs={{0,8},{4,12},{8,16},{12,20},{16,24},{20,28},{24,32},{28,36},{32,40... | collective-permute-start | bytes 393224 | tf_op jit(solution)/shard_map/ppermute | solution.py:33
  161.2 13.8 %collective-permute-start.14 = (f32[2,128,128]{2,1,0:T(8,128)S(1)}, f32[2,128,128]{2,1,0:T(8,128)S(1)}, u32[]{:S(2)}, u32[]{:S(2)}) collective-permute-start(f32[2,128,128]{2,1,0:T(8,128)S(1)} %get-tuple-element.24), channel_id=1, source_target_pairs={{0,120},{4,124},{8,0},{12,4},{16,8},{20,12},{24,16},{28,20},{32,24... | collective-permute-start | bytes 393224 | tf_op jit(solution)/shard_map/ppermute | solution.py:33
  176.6 21.3 %all-to-all-start.1 = ((f32[8,2,16,128]{3,2,1,0:T(8,128)}), f32[8,2,16,128]{3,2,1,0:T(8,128)S(1)}, u32[]{:S(2)}, u32[]{:S(2)}) async-start(f32[8,2,16,128]{3,2,1,0:T(8,128)} %copy.33), calls=%async_computation.1 | async-start | bytes 262144 | tf_op jit(solution)/shard_map/all_to_all | solution.py:228
  190.0 4.0 %copy-start.4 = (s32[55]{0:T(128)S(1)}, s32[55]{0:T(128)}, u32[]{:S(2)}) copy-start(s32[55]{0:T(128)} %constant.204) | copy-start | bytes 664
  217.9 14.9 %all-to-all-start.2 = ((bf16[8,11,16,128]{3,2,1,0:T(8,128)(2,1)}), bf16[8,11,16,128]{3,2,1,0:T(8,128)(2,1)S(1)}, u32[]{:S(2)}, u32[]{:S(2)}) async-start(bf16[8,11,16,128]{3,2,1,0:T(8,128)(2,1)} %bitcast.419), calls=%async_computation.3 | async-start | bytes 720896 | tf_op jit(solution)/shard_map/all_to_all | solution.py:228
Sparse Core Ops, SparseCore 0:
  78.5 93.7 reduce-scatter.1

commit v2 on v1

v2 whole, which is shorter than its diff:
```python
import jax
import jax.numpy as jnp
import numpy as np
from jax import lax
from jax.experimental import pallas as pl
from jax.experimental.pallas import tpu as pltpu
from jax.sharding import PartitionSpec as P

TGT_DEV = 16
NDIAG = 11
Z_DEV = 8

XS, ZS, CS = 4, 16, 2
PLANE = XS * CS
QROWS = PLANE * TGT_DEV


def place(x, z, c):
    return ((x % XS) * ZS + z % ZS) * CS + c % CS


plane_groups = [[place(x, z, c) for x in range(XS) for c in range(CS)] for z in range(ZS)]
ring_groups = [[place(x, z, c) for z in range(ZS)] for x in range(XS) for c in range(CS)]


def ring_step(values, step):
    pairs = [
        (place(x, z, c), place(x, z + step, c))
        for x in range(XS)
        for z in range(ZS)
        for c in range(CS)
    ]
    return lax.ppermute(values, "tgt", pairs)


pair_first, pair_second = np.triu_indices(10)


def solve_normal(matrix, right_side):
    basis_count = right_side.shape[0]
    rows_of = [[None] * basis_count for column in range(basis_count)]
    for p in range(len(pair_first)):
        b = int(pair_first[p])
        c = int(pair_second[p])
        rows_of[b][c] = matrix[p]
        rows_of[c][b] = matrix[p]
    vector = [right_side[b] for b in range(basis_count)]
    for k in range(basis_count):
        inverse = 1.0 / rows_of[k][k]
        for r in range(k + 1, basis_count):
            factor = rows_of[r][k] * inverse
            for c in range(k + 1, basis_count):
                rows_of[r][c] = rows_of[r][c] - factor * rows_of[k][c]
            vector[r] = vector[r] - factor * vector[k]
    answer = [None] * basis_count
    for k in reversed(range(basis_count)):
        running = vector[k]
        for c in range(k + 1, basis_count):
            running = running - rows_of[k][c] * answer[c]
        answer[k] = running / rows_of[k][k]
    gain_total = right_side[0] * answer[0]
    for b in range(1, basis_count):
        gain_total = gain_total + right_side[b] * answer[b]
    return gain_total


def basis_windows(rest_basis, shifts, first_wave, length):

    def one_shift(shift_value):
        return lax.dynamic_slice_in_dim(rest_basis, first_wave + shift_value, length, axis=1)

    return jax.vmap(one_shift)(shifts)


def normal_terms(weight_sum, flux_sum, windows):
    products = windows[:, pair_first, :] * windows[:, pair_second, :]
    matrix = jnp.einsum("ti,zpi->ztp", weight_sum, products, precision=lax.Precision.HIGHEST)
    right_side = jnp.einsum("ti,zbi->ztb", flux_sum, windows, precision=lax.Precision.HIGHEST)
    return (matrix, right_side)


def fit_from(matrix, right_side):
    pairs = jnp.transpose(matrix, (2, 0, 1)).reshape(matrix.shape[2], -1)
    sides = jnp.transpose(right_side, (2, 0, 1)).reshape(right_side.shape[2], -1)
    gain = solve_normal(pairs, sides).reshape(matrix.shape[0], matrix.shape[1])
    return gain.T


GROUP = 4


def split_lanes_kernel(source_ref, out_ref):
    lanes = out_ref.shape[-1]
    for part in range(PLANE):
        out_ref[part] = source_ref[:, :, part * lanes : (part + 1) * lanes]


def split_lanes(values):
    planes, row_count, wave_dev = values.shape
    lanes = wave_dev // PLANE
    return pl.pallas_call(
        split_lanes_kernel,
        out_shape=jax.ShapeDtypeStruct((PLANE, planes, row_count, lanes), values.dtype),
        grid=(planes,),
        in_specs=[pl.BlockSpec((1, row_count, wave_dev), lambda i: (i, 0, 0))],
        out_specs=pl.BlockSpec((PLANE, 1, row_count, lanes), lambda i: (0, i, 0, 0)),
        cost_estimate=pl.CostEstimate(
            flops=0, bytes_accessed=4 * planes * row_count * wave_dev, transcendentals=0
        ),
    )(values)


def split_pair_kernel(ivar_ref, flux_ref, out_ref):
    lanes = out_ref.shape[-1]
    for part in range(PLANE):
        out_ref[part, 0] = ivar_ref[:, part * lanes : (part + 1) * lanes]
        out_ref[part, 1] = flux_ref[:, part * lanes : (part + 1) * lanes]


def split_pair(ivar, flux):
    row_count, wave_dev = ivar.shape
    lanes = wave_dev // PLANE
    return pl.pallas_call(
        split_pair_kernel,
        out_shape=jax.ShapeDtypeStruct((PLANE, 2, row_count, lanes), ivar.dtype),
        cost_estimate=pl.CostEstimate(
            flops=0, bytes_accessed=8 * row_count * wave_dev, transcendentals=0
        ),
    )(ivar, flux)


def members(target_ref, step):
    per_x = CS * TGT_DEV
    local = lax.broadcasted_iota(jnp.int32, (GROUP * QROWS, 1), 0)
    q = local % QROWS
    plane_z = step * GROUP + local // QROWS
    wanted = (q // per_x) * (ZS * per_x) + plane_z * per_x + q % per_x
    return jnp.where(target_ref[...] == wanted, 1.0, 0.0).astype(jnp.bfloat16)


def pair_kernel(target_ref, rows_ref, sums_ref, terms):
    sources, planes, row_count, lanes = rows_ref.shape
    step = pl.program_id(0)

    @pl.when(step == 0)
    def fill_terms():
        for source in range(sources):
            rows = slice(source * row_count, (source + 1) * row_count)
            weight = rows_ref[source, 0].astype(jnp.float32)
            terms[rows, 0:lanes] = rows_ref[source, 0]
            product = weight * rows_ref[source, 1].astype(jnp.float32)
            rounded = product.astype(jnp.bfloat16)
            terms[rows, lanes : 2 * lanes] = rounded
            rest = product - rounded.astype(jnp.float32)
            terms[rows, 2 * lanes : 3 * lanes] = rest.astype(jnp.bfloat16)

    sums = jnp.dot(members(target_ref, step), terms[...], preferred_element_type=jnp.float32)
    for g in range(GROUP):
        block = sums[g * QROWS : (g + 1) * QROWS]
        sums_ref[g, 0] = block[:, 0:lanes]
        sums_ref[g, 1] = block[:, lanes : 2 * lanes] + block[:, 2 * lanes : 3 * lanes]


def coadd_pair(targets, rows):
    sources, planes, row_count, lanes = rows.shape
    return pl.pallas_call(
        pair_kernel,
        out_shape=jax.ShapeDtypeStruct((ZS, 2, QROWS, lanes), jnp.float32),
        grid=(ZS // GROUP,),
        in_specs=[
            pl.BlockSpec((1, sources * row_count), lambda i: (0, 0)),
            pl.BlockSpec(rows.shape, lambda i: (0, 0, 0, 0)),
        ],
        out_specs=pl.BlockSpec((GROUP, 2, QROWS, lanes), lambda i: (i, 0, 0, 0)),
        scratch_shapes=[pltpu.VMEM((sources * row_count, 3 * lanes), jnp.bfloat16)],
        compiler_params=pltpu.CompilerParams(vmem_limit_bytes=40 << 20),
        cost_estimate=pl.CostEstimate(
            flops=2 * ZS * QROWS * sources * row_count * 3 * lanes,
            bytes_accessed=2 * rows.size + 8 * ZS * QROWS * lanes,
            transcendentals=0,
        ),
    )(targets, rows)


def res_kernel(target_ref, pair_ref, rows_ref, res_ref, terms):
    sources, planes, row_count, lanes = rows_ref.shape
    step = pl.program_id(0)

    @pl.when(step == 0)
    def fill_terms():
        def one_source(source, carry):
            rows = pl.ds(pl.multiple_of(source * row_count, row_count), row_count)
            weight = pair_ref[source, 0].astype(jnp.float32)
            for plane in range(planes):
                product = weight * rows_ref[source, plane].astype(jnp.float32)
                terms[rows, plane * lanes : (plane + 1) * lanes] = product.astype(jnp.bfloat16)
            return carry

        lax.fori_loop(0, sources, one_source, 0)

    sums = jnp.dot(members(target_ref, step), terms[...], preferred_element_type=jnp.float32)
    for g in range(GROUP):
        for owner in range(PLANE):
            first = g * QROWS + owner * TGT_DEV
            block = sums[first : first + TGT_DEV].astype(jnp.bfloat16)
            for diagonal in range(planes):
                res_ref[g, owner, diagonal] = block[:, diagonal * lanes : (diagonal + 1) * lanes]


def coadd_res_rows(targets, pair, rows):
    sources, planes, row_count, lanes = rows.shape
    return pl.pallas_call(
        res_kernel,
        out_shape=jax.ShapeDtypeStruct((ZS, PLANE, planes, TGT_DEV, lanes), jnp.bfloat16),
        grid=(ZS // GROUP,),
        in_specs=[
            pl.BlockSpec((1, sources * row_count), lambda i: (0, 0)),
            pl.BlockSpec(pair.shape, lambda i: (0, 0, 0, 0)),
            pl.BlockSpec(rows.shape, lambda i: (0, 0, 0, 0)),
        ],
        out_specs=pl.BlockSpec(
            (GROUP, PLANE, planes, TGT_DEV, lanes), lambda i: (i, 0, 0, 0, 0)
        ),
        scratch_shapes=[pltpu.VMEM((sources * row_count, planes * lanes), jnp.bfloat16)],
        compiler_params=pltpu.CompilerParams(vmem_limit_bytes=56 << 20),
        cost_estimate=pl.CostEstimate(
            flops=2 * ZS * QROWS * sources * row_count * planes * lanes,
            bytes_accessed=2 * (rows.size + ZS * QROWS * planes * lanes),
            transcendentals=0,
        ),
    )(targets, pair, rows)


def exchange(values):
    return lax.all_to_all(
        values, "tgt", split_axis=0, concat_axis=0, axis_index_groups=plane_groups, tiled=True
    )


def scatter_sum(values):
    return lax.psum_scatter(
        values, "tgt", scatter_dimension=0, axis_index_groups=ring_groups, tiled=False
    )


def ring_sum(parts, my_z):
    def part(offset):
        return lax.dynamic_index_in_dim(parts, (my_z + offset) % ZS, 0, keepdims=False)

    half = ZS // 2
    up, down = part(half), part(half + 1)
    for s in range(half):
        up = ring_step(up, 1)
        if s < half - 1:
            up = up + part(half - 1 - s)
            down = ring_step(down, -1)
            if s < half - 2:
                down = down + part(half + 2 + s)
    return part(0) + up + down


def shards(
    exposure_flux,
    exposure_ivar,
    exposure_res,
    target_of_row,
    valid_of_row,
    rest_basis,
    redshift_shift,
):
    device = lax.axis_index("tgt")
    my_z = (device // CS) % ZS
    row_count, wave_dev = exposure_flux.shape
    lanes = wave_dev // PLANE
    masked = jnp.where(valid_of_row == 1, target_of_row, -1).reshape(XS, ZS, CS * row_count)
    targets = lax.dynamic_index_in_dim(masked, my_z, 1, keepdims=False).reshape(1, -1)

    pair = exchange(split_pair(exposure_ivar, exposure_flux))
    packed = split_lanes(jnp.transpose(exposure_res, (1, 0, 2)))
    packed, pair = lax.optimization_barrier((packed, pair))
    rows = exchange(packed)
    sums = ring_sum(coadd_pair(targets, pair), my_z)
    rows, sums = lax.optimization_barrier((rows, sums))
    res_sum = scatter_sum(coadd_res_rows(targets, pair, rows))

    split = jnp.transpose(sums.reshape(2, PLANE, TGT_DEV, lanes), (1, 0, 2, 3))
    own = jnp.transpose(exchange(split), (1, 2, 0, 3)).reshape(2, TGT_DEV, wave_dev)
    everything = lax.all_gather(own.astype(jnp.bfloat16), "band", axis=2, tiled=True)
    everything = everything.astype(jnp.float32)
    coadd_flux = own[1] / own[0]
    band_index = lax.axis_index("band")
    shifts = lax.dynamic_slice_in_dim(redshift_shift, band_index * Z_DEV, Z_DEV)
    windows = basis_windows(rest_basis, shifts, 0, everything.shape[2])
    fit_gain = fit_from(*normal_terms(everything[0], everything[1], windows))

    back = exchange(res_sum)
    own_res = jnp.transpose(back, (1, 2, 0, 3)).reshape(NDIAG, TGT_DEV, wave_dev)
    coadd_res = (own_res.astype(jnp.float32) / own[0][None]).astype(jnp.bfloat16)
    return (coadd_flux, jnp.transpose(coadd_res, (1, 0, 2)), fit_gain)


def solution(mesh):
    in_specs = (P("tgt", "band"), P("tgt", "band"), P("tgt", None, "band"), P(), P(), P(), P())
    out_specs = (P("tgt", "band"), P("tgt", None, "band"), P("tgt", "band"))
    return jax.shard_map(shards, mesh=mesh, in_specs=in_specs, out_specs=out_specs, check_vma=False)
```

time: 242 us -> 226 us (0.934)
  waiting for transfers between devices: 73.2 us -> 42.7 us
  starting transfers between devices: 83.8 us -> 92.5 us
  Pallas kernels: 18.5 us -> 23.6 us
  other arithmetic: 5.95 us -> 2.58 us
  local copies, waits for them, and re-layouts: 26 us -> 28.6 us
    all_to_all x3 -> x4, waiting for transfers between devices: 45.1 us -> 8.14 us  [exchange(): lax.all_to_all(values, 'tgt', split_axis=0, concat_axis=0, axis_index_gro...]
    reduce_scatter x1, waiting for transfers between devices: 0.02 us -> 18.1 us  [scatter_sum(): lax.psum_scatter(values, 'tgt', scatter_dimension=0, axis_index_groups=ri...]
    ppermute x15, waiting for transfers between devices: 28 us -> 16.4 us  [ring_step(): return lax.ppermute(values, 'tgt', pairs)]
    all_to_all x3 -> x4, starting transfers between devices: 30.3 us -> 40.7 us  [exchange(): lax.all_to_all(values, 'tgt', split_axis=0, concat_axis=0, axis_index_gro...]
    gather x24, local copies, waits for them, and re-layouts: 10.9 us -> 16.6 us
    pallas_call x2 -> x4, Pallas kernels: 18.5 us -> 23.6 us  [the longest x1 11 us: coadd_res_rows(): pl.pallas_call(res_kernel, out_shape=jax.ShapeDtypeStruct((ZS, PLANE, pla...]
    add x8, other arithmetic: 2.75 us -> 0.22 us  [the longest x7 0.2 us: ring_sum(): up = up + part(half - 1 - s)]
  transfers between devices with their start and end apart: 19 -> 20, of which waited for: 14 -> 16; matrix products, arithmetic and copies ran while one was open for 14% -> 17% of each run, Pallas kernels for 0% -> 3%
where the time goes in v2:
time: 226 us; the launch traced here: 225 us
  starting transfers between devices  92.5 us (41%)
  waiting for transfers between devices  42.7 us (19%)
  local copies, waits for them, and re-layouts  28.6 us (13%)
  Pallas kernels  23.6 us (10%)
  between operations  14.6 us (6%)
  blocking collectives  10.9 us (5%)
  matrix products  9.86 us (4%)
  other arithmetic  2.58 us (1%)
    ppermute x15, starting transfers between devices, ring_step(): return lax.ppermute(values, 'tgt', pairs)  51.8 us
    all_to_all x4, starting transfers between devices, exchange(): lax.all_to_all(values, 'tgt', split_axis=0, concat_axis=0, axis_index_gro...  40.7 us
    reduce_scatter x1, waiting for transfers between devices, scatter_sum(): lax.psum_scatter(values, 'tgt', scatter_dimension=0, axis_index_groups=ri...  18.1 us
    gather x24, local copies, waits for them, and re-layouts  16.6 us
    ppermute x15, waiting for transfers between devices, ring_step(): return lax.ppermute(values, 'tgt', pairs)  16.4 us
    pallas_call x1, Pallas kernels, coadd_res_rows(): pl.pallas_call(res_kernel, out_shape=jax.ShapeDtypeStruct((ZS, PLANE, pla...  11 us
    all_gather x1, blocking collectives, shards(): lax.all_gather(own.astype(jnp.bfloat16), 'band', axis=2, tiled=True)  10.9 us
    all_to_all x4, waiting for transfers between devices, exchange(): lax.all_to_all(values, 'tgt', split_axis=0, concat_axis=0, axis_index_gro...  8.14 us
  transfers between devices with their start and end apart: 20, of which 16 were waited for; matrix products, arithmetic and copies ran while one was open for 17% of the time, Pallas kernels for 3%

profile of v2, /device:TPU:1, one launch (start us, length us, event | category | flops | bytes accessed | tf_op | source)
XLA Modules:
  0.0 225.2 jit_solution(5329484522088708666)
XLA Ops:
  7.2 1.9 shard_map.131
  9.1 10.3 %all-to-all-start = ((bf16[8,2,128,128]{3,2,1,0:T(8,128)(2,1)}), bf16[8,2,128,128]{3,2,1,0:T(8,128)(2,1)S(1)}, u32[]{:S(2)}, u32[]{:S(2)}) async-start(bf16[8,2,128,128]{3,2,1,0:T(8,128)(2,1)} %shard_map.131), calls=%async_computation | async-start | bytes 1048576 | tf_op jit(solution)/shard_map/all_to_all | solution.py:235
  19.4 7.5 %shard_map.130 = bf16[8,11,128,128]{3,2,1,0:T(8,128)(2,1)} custom-call(bf16[11,128,1024]{2,1,0:T(8,128)(2,1)} %bitcast.424), custom_call_target="tpu_custom_call" | custom-call | bytes 5767168 | tf_op jit(solution)/shard_map/pallas_call | solution.py:101
  27.0 1.9 all-to-all-done.rows_ref.pair_ref
  28.9 3.1 %shard_map.132 = f32[16,2,128,128]{3,2,1,0:T(8,128)S(1)} custom-call(s32[1,1024]{1,0:T(1,128)S(1)} %bitcast.422, bf16[8,2,128,128]{3,2,1,0:T(8,128)(2,1)S(1)} %all-to-all-done.rows_ref.pair_ref), custom_call_target="tpu_custom_call" | custom-call | flops 1610612736 | bytes 2621440 | tf_op jit(solution)/shard_map/pallas_call | solution.py:166
  32.0 1.9 collective-permute-start
  34.0 6.6 %collective-permute-start.8 = (f32[2,128,128]{2,1,0:T(8,128)S(1)}, f32[2,128,128]{2,1,0:T(8,128)S(1)}, u32[]{:S(2)}, u32[]{:S(2)}) collective-permute-start(f32[2,128,128]{2,1,0:T(8,128)S(1)} %get-tuple-element.40), channel_id=1, source_target_pairs={{0,120},{4,124},{8,0},{12,4},{16,8},{20,12},{24,16},{28,20},{32,24... | collective-permute-start | bytes 393224 | tf_op jit(solution)/shard_map/ppermute | solution.py:33
  40.6 1.0 collective-permute-done
  41.7 1.9 collective-permute-start.1
  43.6 5.8 %all-to-all-start.1 = ((bf16[8,11,128,128]{3,2,1,0:T(8,128)(2,1)}), bf16[8,11,128,128]{3,2,1,0:T(8,128)(2,1)}, u32[]{:S(2)}, u32[]{:S(2)}) async-start(bf16[8,11,128,128]{3,2,1,0:T(8,128)(2,1)} %shard_map.130), calls=%async_computation.1 | async-start | bytes 5767168 | tf_op jit(solution)/shard_map/all_to_all | solution.py:235
  49.4 1.9 collective-permute-start.2
  51.4 4.9 %collective-permute-start.9 = (f32[2,128,128]{2,1,0:T(8,128)S(1)}, f32[2,128,128]{2,1,0:T(8,128)S(1)}, u32[]{:S(2)}, u32[]{:S(2)}) collective-permute-start(f32[2,128,128]{2,1,0:T(8,128)S(1)} %get-tuple-element.38), channel_id=1, source_target_pairs={{0,120},{4,124},{8,0},{12,4},{16,8},{20,12},{24,16},{28,20},{32,24... | collective-permute-start | bytes 393224 | tf_op jit(solution)/shard_map/ppermute | solution.py:33
  56.3 0.8 collective-permute-done.2
  57.0 1.1 collective-permute-done.9
  58.2 1.9 collective-permute-start.3
  60.1 5.4 %collective-permute-start.10 = (f32[2,128,128]{2,1,0:T(8,128)S(1)}, f32[2,128,128]{2,1,0:T(8,128)S(1)}, u32[]{:S(2)}, u32[]{:S(2)}) collective-permute-start(f32[2,128,128]{2,1,0:T(8,128)S(1)} %get-tuple-element.36), channel_id=1, source_target_pairs={{0,120},{4,124},{8,0},{12,4},{16,8},{20,12},{24,16},{28,20},{32,24... | collective-permute-start | bytes 393224 | tf_op jit(solution)/shard_map/ppermute | solution.py:33
  65.6 0.8 collective-permute-done.3
  66.3 1.1 collective-permute-done.10
  67.5 1.9 collective-permute-start.4
  69.4 5.4 %collective-permute-start.11 = (f32[2,128,128]{2,1,0:T(8,128)S(1)}, f32[2,128,128]{2,1,0:T(8,128)S(1)}, u32[]{:S(2)}, u32[]{:S(2)}) collective-permute-start(f32[2,128,128]{2,1,0:T(8,128)S(1)} %get-tuple-element.34), channel_id=1, source_target_pairs={{0,120},{4,124},{8,0},{12,4},{16,8},{20,12},{24,16},{28,20},{32,24... | collective-permute-start | bytes 393224 | tf_op jit(solution)/shard_map/ppermute | solution.py:33
  74.8 0.8 collective-permute-done.4
  75.6 1.1 collective-permute-done.11
  76.8 4.4 %collective-permute-start.5 = (f32[2,128,128]{2,1,0:T(8,128)S(1)}, f32[2,128,128]{2,1,0:T(8,128)S(1)}, u32[]{:S(2)}, u32[]{:S(2)}) collective-permute-start(f32[2,128,128]{2,1,0:T(8,128)S(1)} %get-tuple-element.31), channel_id=1, source_target_pairs={{0,8},{4,12},{8,16},{12,20},{16,24},{20,28},{24,32},{28,36},{32,40... | collective-permute-start | bytes 393224 | tf_op jit(solution)/shard_map/ppermute | solution.py:33
  81.2 2.5 %collective-permute-start.12 = (f32[2,128,128]{2,1,0:T(8,128)S(1)}, f32[2,128,128]{2,1,0:T(8,128)S(1)}, u32[]{:S(2)}, u32[]{:S(2)}) collective-permute-start(f32[2,128,128]{2,1,0:T(8,128)S(1)} %get-tuple-element.32), channel_id=1, source_target_pairs={{0,120},{4,124},{8,0},{12,4},{16,8},{20,12},{24,16},{28,20},{32,24... | collective-permute-start | bytes 393224 | tf_op jit(solution)/shard_map/ppermute | solution.py:33
  83.7 0.8 collective-permute-done.5
  84.5 2.4 %collective-permute-done.12 = f32[2,128,128]{2,1,0:T(8,128)S(1)} collective-permute-done((f32[2,128,128]{2,1,0:T(8,128)S(1)}, f32[2,128,128]{2,1,0:T(8,128)S(1)}, u32[]{:S(2)}, u32[]{:S(2)}) %collective-permute-start.12) | collective-permute-done | bytes 131104 | tf_op jit(solution)/shard_map/ppermute | solution.py:33
  86.9 4.6 %collective-permute-start.6 = (f32[2,128,128]{2,1,0:T(8,128)S(1)}, f32[2,128,128]{2,1,0:T(8,128)S(1)}, u32[]{:S(2)}, u32[]{:S(2)}) collective-permute-start(f32[2,128,128]{2,1,0:T(8,128)S(1)} %get-tuple-element.29), channel_id=1, source_target_pairs={{0,8},{4,12},{8,16},{12,20},{16,24},{20,28},{24,32},{28,36},{32,40... | collective-permute-start | bytes 393224 | tf_op jit(solution)/shard_map/ppermute | solution.py:33
  91.5 1.9 collective-permute-start.13
  93.9 3.4 %collective-permute-done.13 = f32[2,128,128]{2,1,0:T(8,128)S(1)} collective-permute-done((f32[2,128,128]{2,1,0:T(8,128)S(1)}, f32[2,128,128]{2,1,0:T(8,128)S(1)}, u32[]{:S(2)}, u32[]{:S(2)}) %collective-permute-start.13) | collective-permute-done | bytes 131104 | tf_op jit(solution)/shard_map/ppermute | solution.py:33
  97.3 3.7 %collective-permute-start.7 = (f32[2,128,128]{2,1,0:T(8,128)S(1)}, f32[2,128,128]{2,1,0:T(8,128)S(1)}, u32[]{:S(2)}, u32[]{:S(2)}) collective-permute-start(f32[2,128,128]{2,1,0:T(8,128)S(1)} %get-tuple-element.27), channel_id=1, source_target_pairs={{0,8},{4,12},{8,16},{12,20},{16,24},{20,28},{24,32},{28,36},{32,40... | collective-permute-start | bytes 393224 | tf_op jit(solution)/shard_map/ppermute | solution.py:33
  100.9 2.8 %collective-permute-start.14 = (f32[2,128,128]{2,1,0:T(8,128)S(1)}, f32[2,128,128]{2,1,0:T(8,128)S(1)}, u32[]{:S(2)}, u32[]{:S(2)}) collective-permute-start(f32[2,128,128]{2,1,0:T(8,128)S(1)} %get-tuple-element.28), channel_id=1, source_target_pairs={{0,120},{4,124},{8,0},{12,4},{16,8},{20,12},{24,16},{28,20},{32,24... | collective-permute-start | bytes 393224 | tf_op jit(solution)/shard_map/ppermute | solution.py:33
  104.2 2.5 %collective-permute-done.14 = f32[2,128,128]{2,1,0:T(8,128)S(1)} collective-permute-done((f32[2,128,128]{2,1,0:T(8,128)S(1)}, f32[2,128,128]{2,1,0:T(8,128)S(1)}, u32[]{:S(2)}, u32[]{:S(2)}) %collective-permute-start.14) | collective-permute-done | bytes 131104 | tf_op jit(solution)/shard_map/ppermute | solution.py:33
  106.7 11.0 %shard_map.133 = bf16[16,8,11,16,128]{4,3,2,1,0:T(8,128)(2,1)} custom-call(s32[1,1024]{1,0:T(1,128)} %bitcast.423, bf16[8,2,128,128]{3,2,1,0:T(8,128)(2,1)} %copy-done, bf16[8,11,128,128]{3,2,1,0:T(8,128)(2,1)} %all-to-all-done.1.rows_ref), custom_call_target="tpu_custom_call" | custom-call | flops 5905580032 | bytes 8650752 | tf_op jit(solution)/shard_map/pallas_call | solution.py:212
  117.8 0.6 copy-done.7
  118.7 16.6 %while.1 = (s32[]{:T(128)}, f32[10,4608]{1,0:T(8,128)S(1)}, s32[8,2]{0,1:T(2,128)S(1)}, f32[8,10,4096]{2,1,0:T(8,128)}, s32[]{:T(128)}) while((s32[]{:T(128)}, f32[10,4608]{1,0:T(8,128)S(1)}, s32[8,2]{0,1:T(2,128)S(1)}, f32[8,10,4096]{2,1,0:T(8,128)}, s32[]{:T(128)}) %tuple.46), condition=%wide.while_cond, body=%wide.while_body.sunk | while | flops 2 | bytes 426597 | solution.py:70
  118.8 0.5 slice.757
  119.3 1.5 bitcast_dynamic-update-slice_fusion.2
  120.8 0.5 slice.757
  121.4 1.5 bitcast_dynamic-update-slice_fusion.2
  122.9 0.5 slice.757
  123.4 1.5 bitcast_dynamic-update-slice_fusion.2
  125.0 0.5 slice.757
  125.5 1.5 bitcast_dynamic-update-slice_fusion.2
  127.1 0.5 slice.757
  127.6 1.5 bitcast_dynamic-update-slice_fusion.2
  129.1 0.5 slice.757
  129.7 1.5 bitcast_dynamic-update-slice_fusion.2
  131.8 1.5 bitcast_dynamic-update-slice_fusion.2
  133.3 0.5 slice.757
  133.8 1.5 bitcast_dynamic-update-slice_fusion.2
  135.3 0.7 copy.25
  136.0 11.5 %all-to-all-start.2 = ((f32[8,2,16,128]{3,2,1,0:T(8,128)}), f32[8,2,16,128]{3,2,1,0:T(8,128)S(1)}, u32[]{:S(2)}, u32[]{:S(2)}) async-start(f32[8,2,16,128]{3,2,1,0:T(8,128)} %copy.25), calls=%async_computation.2 | async-start | bytes 262144 | tf_op jit(solution)/shard_map/all_to_all | solution.py:235
  147.4 2.4 %copy.30 = f32[8,10,4096]{2,0,1:T(8,128)S(1)} copy(f32[8,10,4096]{2,1,0:T(8,128)} %get-tuple-element.18) | data formatting | bytes 2621440 | tf_op jit(solution)/shard_map/vmap()/gather | solution.py:70
  149.8 4.0 %gather_fusion.1 = f32[55,8,4096]{2,1,0:T(8,128)} fusion(f32[8,10,4096]{2,0,1:T(8,128)S(1)} %copy.30, s32[1024]{0:T(1024)S(1)} %pad_clamp_fusion), kind=kCustom, calls=%fused_computation.1 | custom fusion | bytes 14418140 | tf_op jit(solution)/shard_map/gather | solution.py:76
  153.8 3.9 %gather_fusion = f32[55,8,4096]{2,1,0:T(8,128)} fusion(f32[8,10,4096]{2,0,1:T(8,128)S(1)} %copy.30, s32[1024]{0:T(1024)S(1)} %pad_clamp_fusion.1), kind=kCustom, calls=%fused_computation | custom fusion | bytes 14418140 | tf_op jit(solution)/shard_map/gather | solution.py:76
  157.8 10.9 %all_gather.3 = bf16[2,16,4096]{2,1,0:T(8,128)(2,1)S(1)} all-gather(bf16[2,16,1024]{2,1,0:T(8,128)(2,1)S(1)} %copy_bitcast_fusion.1), channel_id=1, replica_groups=mesh['tgt'=128,'band'=4] {'band'}, dimensions={2}, use_global_device_ids=true | all-gather | bytes 327680 | tf_op jit(solution)/shard_map/all_gather | solution.py:288
  168.6 2.7 %convolution_bitcast_fusion = f32[10,8,16]{2,0,1:T(8,128)S(1)} fusion(f32[8,10,4096]{2,1,0:T(8,128)} %get-tuple-element.18, bf16[2,16,4096]{2,1,0:T(8,128)(2,1)S(1)} %all_gather.3), kind=kOutput, calls=%fused_computation.8 | convolution fusion | flops 62914560 | bytes 1446912 | tf_op jit(solution)/shard_map/ti,zbi->ztb/dot_general | solution.py:78
  171.3 7.2 %fusion.3 = f32[55,8,16]{2,1,0:T(8,128)S(1)} fusion(f32[55,8,4096]{2,1,0:T(8,128)} %gather_fusion, f32[55,8,4096]{2,1,0:T(8,128)} %gather_fusion.1, bf16[2,16,4096]{2,1,0:T(8,128)(2,1)S(1)} %all_gather.3), kind=kOutput, calls=%fused_computation.7 | convolution fusion | flops 347832320 | bytes 14577152 | tf_op jit(solution)/shard_map/ti,zpi->ztp/dot_general | solution.py:77
  178.5 18.1 %reduce-scatter.2.cloned.1.call-done = bf16[1,8,11,16,128]{4,3,2,1,0:T(8,128)(2,1)} async-done(((bf16[16,8,11,16,128]{4,3,2,1,0:T(8,128)(2,1)}), bf16[1,8,11,16,128]{4,3,2,1,0:T(8,128)(2,1)}) %reduce-scatter.2.cloned.1.call-update) | async-done | bytes 360464 | tf_op jit(solution)/shard_map/reduce_scatter | solution.py:241
  196.6 13.2 %all-to-all-start.3 = ((bf16[8,11,16,128]{3,2,1,0:T(8,128)(2,1)}), bf16[8,11,16,128]{3,2,1,0:T(8,128)(2,1)S(1)}, u32[]{:S(2)}, u32[]{:S(2)}) async-start(bf16[8,11,16,128]{3,2,1,0:T(8,128)(2,1)} %bitcast.429), calls=%async_computation.4 | async-start | bytes 720896 | tf_op jit(solution)/shard_map/all_to_all | solution.py:235
  209.8 0.8 add_bitcast_fusion
  210.7 0.7 bitcast_divide_fusion.1
  211.3 6.2 %all-to-all-done.3 = bf16[8,11,16,128]{3,2,1,0:T(8,128)(2,1)S(1)} async-done(((bf16[8,11,16,128]{3,2,1,0:T(8,128)(2,1)}), bf16[8,11,16,128]{3,2,1,0:T(8,128)(2,1)S(1)}, u32[]{:S(2)}, u32[]{:S(2)}) %all-to-all-start.3) | async-done | bytes 360480 | tf_op jit(solution)/shard_map/all_to_all | solution.py:235
  217.6 0.8 fusion.7
  (55 shorter events, 2.7 us)
Async XLA Ops:
  7.2 12.2 %copy-start.4 = (s32[16384]{0:T(1024)S(1)}, s32[16384]{0:T(1024)}, u32[]{:S(2)}) copy-start(s32[16384]{0:T(1024)} %param.15) | copy-start | bytes 196612
  7.2 12.2 %copy-start.3 = (s32[16384]{0:T(1024)S(1)}, s32[16384]{0:T(1024)}, u32[]{:S(2)}) copy-start(s32[16384]{0:T(1024)} %param.14) | copy-start | bytes 196612
  9.1 19.8 %all-to-all-start = ((bf16[8,2,128,128]{3,2,1,0:T(8,128)(2,1)}), bf16[8,2,128,128]{3,2,1,0:T(8,128)(2,1)S(1)}, u32[]{:S(2)}, u32[]{:S(2)}) async-start(bf16[8,2,128,128]{3,2,1,0:T(8,128)(2,1)} %shard_map.131), calls=%async_computation | async-start | bytes 1048576 | tf_op jit(solution)/shard_map/all_to_all | solution.py:235
  27.0 5.0 %copy-start.1 = (s32[4,1,256]{2,1,0:T(1,128)}, s32[4,1,256]{2,1,0:T(1,128)S(1)}, u32[]{:S(2)}) copy-start(s32[4,1,256]{2,1,0:T(1,128)S(1)} %constant_dynamic-slice_fusion.1) | copy-start | bytes 12292
  28.9 3.1 %copy-start = (bf16[8,2,128,128]{3,2,1,0:T(8,128)(2,1)}, bf16[8,2,128,128]{3,2,1,0:T(8,128)(2,1)S(1)}, u32[]{:S(2)}) copy-start(bf16[8,2,128,128]{3,2,1,0:T(8,128)(2,1)S(1)} %all-to-all-done.rows_ref.pair_ref) | copy-start | bytes 1572868
  32.0 9.6 %collective-permute-start = (f32[2,128,128]{2,1,0:T(8,128)S(1)}, f32[2,128,128]{2,1,0:T(8,128)S(1)}, u32[]{:S(2)}, u32[]{:S(2)}) collective-permute-start(f32[2,128,128]{2,1,0:T(8,128)S(1)} %get-tuple-element.39), channel_id=1, source_target_pairs={{0,8},{4,12},{8,16},{12,20},{16,24},{20,28},{24,32},{28,36},{32,40... | collective-permute-start | bytes 393224 | tf_op jit(solution)/shard_map/ppermute | solution.py:33
  34.0 15.4 %collective-permute-start.8 = (f32[2,128,128]{2,1,0:T(8,128)S(1)}, f32[2,128,128]{2,1,0:T(8,128)S(1)}, u32[]{:S(2)}, u32[]{:S(2)}) collective-permute-start(f32[2,128,128]{2,1,0:T(8,128)S(1)} %get-tuple-element.40), channel_id=1, source_target_pairs={{0,120},{4,124},{8,0},{12,4},{16,8},{20,12},{24,16},{28,20},{32,24... | collective-permute-start | bytes 393224 | tf_op jit(solution)/shard_map/ppermute | solution.py:33
  41.7 7.7 %collective-permute-start.1 = (f32[2,128,128]{2,1,0:T(8,128)S(1)}, f32[2,128,128]{2,1,0:T(8,128)S(1)}, u32[]{:S(2)}, u32[]{:S(2)}) collective-permute-start(f32[2,128,128]{2,1,0:T(8,128)S(1)} %bitcast_add_fusion.12), channel_id=1, source_target_pairs={{0,8},{4,12},{8,16},{12,20},{16,24},{20,28},{24,32},{28,36},{32,40... | collective-permute-start | bytes 393224 | tf_op jit(solution)/shard_map/ppermute | solution.py:33
  43.6 63.1 %all-to-all-start.1 = ((bf16[8,11,128,128]{3,2,1,0:T(8,128)(2,1)}), bf16[8,11,128,128]{3,2,1,0:T(8,128)(2,1)}, u32[]{:S(2)}, u32[]{:S(2)}) async-start(bf16[8,11,128,128]{3,2,1,0:T(8,128)(2,1)} %shard_map.130), calls=%async_computation.1 | async-start | bytes 5767168 | tf_op jit(solution)/shard_map/all_to_all | solution.py:235
  49.4 147.2 %reduce-scatter.2.cloned.1.call-start = ((), (), s32[]{:S(2)}) async-start(), calls=%async_computation.5 | async-start | bytes 6127616 | tf_op jit(solution)/shard_map/reduce_scatter | solution.py:241
  49.4 7.6 %collective-permute-start.2 = (f32[2,128,128]{2,1,0:T(8,128)S(1)}, f32[2,128,128]{2,1,0:T(8,128)S(1)}, u32[]{:S(2)}, u32[]{:S(2)}) collective-permute-start(f32[2,128,128]{2,1,0:T(8,128)S(1)} %get-tuple-element.37), channel_id=1, source_target_pairs={{0,8},{4,12},{8,16},{12,20},{16,24},{20,28},{24,32},{28,36},{32,40... | collective-permute-start | bytes 393224 | tf_op jit(solution)/shard_map/ppermute | solution.py:33
  51.4 6.8 %collective-permute-start.9 = (f32[2,128,128]{2,1,0:T(8,128)S(1)}, f32[2,128,128]{2,1,0:T(8,128)S(1)}, u32[]{:S(2)}, u32[]{:S(2)}) collective-permute-start(f32[2,128,128]{2,1,0:T(8,128)S(1)} %get-tuple-element.38), channel_id=1, source_target_pairs={{0,120},{4,124},{8,0},{12,4},{16,8},{20,12},{24,16},{28,20},{32,24... | collective-permute-start | bytes 393224 | tf_op jit(solution)/shard_map/ppermute | solution.py:33
  58.2 8.1 %collective-permute-start.3 = (f32[2,128,128]{2,1,0:T(8,128)S(1)}, f32[2,128,128]{2,1,0:T(8,128)S(1)}, u32[]{:S(2)}, u32[]{:S(2)}) collective-permute-start(f32[2,128,128]{2,1,0:T(8,128)S(1)} %get-tuple-element.35), channel_id=1, source_target_pairs={{0,8},{4,12},{8,16},{12,20},{16,24},{20,28},{24,32},{28,36},{32,40... | collective-permute-start | bytes 393224 | tf_op jit(solution)/shard_map/ppermute | solution.py:33
  60.1 7.3 %collective-permute-start.10 = (f32[2,128,128]{2,1,0:T(8,128)S(1)}, f32[2,128,128]{2,1,0:T(8,128)S(1)}, u32[]{:S(2)}, u32[]{:S(2)}) collective-permute-start(f32[2,128,128]{2,1,0:T(8,128)S(1)} %get-tuple-element.36), channel_id=1, source_target_pairs={{0,120},{4,124},{8,0},{12,4},{16,8},{20,12},{24,16},{28,20},{32,24... | collective-permute-start | bytes 393224 | tf_op jit(solution)/shard_map/ppermute | solution.py:33
  67.5 8.1 %collective-permute-start.4 = (f32[2,128,128]{2,1,0:T(8,128)S(1)}, f32[2,128,128]{2,1,0:T(8,128)S(1)}, u32[]{:S(2)}, u32[]{:S(2)}) collective-permute-start(f32[2,128,128]{2,1,0:T(8,128)S(1)} %get-tuple-element.33), channel_id=1, source_target_pairs={{0,8},{4,12},{8,16},{12,20},{16,24},{20,28},{24,32},{28,36},{32,40... | collective-permute-start | bytes 393224 | tf_op jit(solution)/shard_map/ppermute | solution.py:33
  69.4 7.3 %collective-permute-start.11 = (f32[2,128,128]{2,1,0:T(8,128)S(1)}, f32[2,128,128]{2,1,0:T(8,128)S(1)}, u32[]{:S(2)}, u32[]{:S(2)}) collective-permute-start(f32[2,128,128]{2,1,0:T(8,128)S(1)} %get-tuple-element.34), channel_id=1, source_target_pairs={{0,120},{4,124},{8,0},{12,4},{16,8},{20,12},{24,16},{28,20},{32,24... | collective-permute-start | bytes 393224 | tf_op jit(solution)/shard_map/ppermute | solution.py:33
  76.8 7.7 %collective-permute-start.5 = (f32[2,128,128]{2,1,0:T(8,128)S(1)}, f32[2,128,128]{2,1,0:T(8,128)S(1)}, u32[]{:S(2)}, u32[]{:S(2)}) collective-permute-start(f32[2,128,128]{2,1,0:T(8,128)S(1)} %get-tuple-element.31), channel_id=1, source_target_pairs={{0,8},{4,12},{8,16},{12,20},{16,24},{20,28},{24,32},{28,36},{32,40... | collective-permute-start | bytes 393224 | tf_op jit(solution)/shard_map/ppermute | solution.py:33
  81.2 5.7 %collective-permute-start.12 = (f32[2,128,128]{2,1,0:T(8,128)S(1)}, f32[2,128,128]{2,1,0:T(8,128)S(1)}, u32[]{:S(2)}, u32[]{:S(2)}) collective-permute-start(f32[2,128,128]{2,1,0:T(8,128)S(1)} %get-tuple-element.32), channel_id=1, source_target_pairs={{0,120},{4,124},{8,0},{12,4},{16,8},{20,12},{24,16},{28,20},{32,24... | collective-permute-start | bytes 393224 | tf_op jit(solution)/shard_map/ppermute | solution.py:33
  86.9 6.9 %collective-permute-start.6 = (f32[2,128,128]{2,1,0:T(8,128)S(1)}, f32[2,128,128]{2,1,0:T(8,128)S(1)}, u32[]{:S(2)}, u32[]{:S(2)}) collective-permute-start(f32[2,128,128]{2,1,0:T(8,128)S(1)} %get-tuple-element.29), channel_id=1, source_target_pairs={{0,8},{4,12},{8,16},{12,20},{16,24},{20,28},{24,32},{28,36},{32,40... | collective-permute-start | bytes 393224 | tf_op jit(solution)/shard_map/ppermute | solution.py:33
  91.5 5.7 %collective-permute-start.13 = (f32[2,128,128]{2,1,0:T(8,128)S(1)}, f32[2,128,128]{2,1,0:T(8,128)S(1)}, u32[]{:S(2)}, u32[]{:S(2)}) collective-permute-start(f32[2,128,128]{2,1,0:T(8,128)S(1)} %get-tuple-element.30), channel_id=1, source_target_pairs={{0,120},{4,124},{8,0},{12,4},{16,8},{20,12},{24,16},{28,20},{32,24... | collective-permute-start | bytes 393224 | tf_op jit(solution)/shard_map/ppermute | solution.py:33
  97.3 6.9 %collective-permute-start.7 = (f32[2,128,128]{2,1,0:T(8,128)S(1)}, f32[2,128,128]{2,1,0:T(8,128)S(1)}, u32[]{:S(2)}, u32[]{:S(2)}) collective-permute-start(f32[2,128,128]{2,1,0:T(8,128)S(1)} %get-tuple-element.27), channel_id=1, source_target_pairs={{0,8},{4,12},{8,16},{12,20},{16,24},{20,28},{24,32},{28,36},{32,40... | collective-permute-start | bytes 393224 | tf_op jit(solution)/shard_map/ppermute | solution.py:33
  100.9 5.7 %collective-permute-start.14 = (f32[2,128,128]{2,1,0:T(8,128)S(1)}, f32[2,128,128]{2,1,0:T(8,128)S(1)}, u32[]{:S(2)}, u32[]{:S(2)}) collective-permute-start(f32[2,128,128]{2,1,0:T(8,128)S(1)} %get-tuple-element.28), channel_id=1, source_target_pairs={{0,120},{4,124},{8,0},{12,4},{16,8},{20,12},{24,16},{28,20},{32,24... | collective-permute-start | bytes 393224 | tf_op jit(solution)/shard_map/ppermute | solution.py:33
  117.7 0.7 copy-start.7
  117.7 1.0 copy-start.2
  117.7 29.7 %copy-start.6 = (s32[55]{0:T(128)S(1)}, s32[55]{0:T(128)}, u32[]{:S(2)}) copy-start(s32[55]{0:T(128)} %constant.205) | copy-start | bytes 664
  136.0 21.8 %all-to-all-start.2 = ((f32[8,2,16,128]{3,2,1,0:T(8,128)}), f32[8,2,16,128]{3,2,1,0:T(8,128)S(1)}, u32[]{:S(2)}, u32[]{:S(2)}) async-start(f32[8,2,16,128]{3,2,1,0:T(8,128)} %copy.25), calls=%async_computation.2 | async-start | bytes 262144 | tf_op jit(solution)/shard_map/all_to_all | solution.py:235
  149.8 4.0 %copy-start.5 = (s32[55]{0:T(128)S(1)}, s32[55]{0:T(128)}, u32[]{:S(2)}) copy-start(s32[55]{0:T(128)} %constant.204) | copy-start | bytes 664
  196.6 20.9 %all-to-all-start.3 = ((bf16[8,11,16,128]{3,2,1,0:T(8,128)(2,1)}), bf16[8,11,16,128]{3,2,1,0:T(8,128)(2,1)S(1)}, u32[]{:S(2)}, u32[]{:S(2)}) async-start(bf16[8,11,16,128]{3,2,1,0:T(8,128)(2,1)} %bitcast.429), calls=%async_computation.4 | async-start | bytes 720896 | tf_op jit(solution)/shard_map/all_to_all | solution.py:235
Sparse Core Ops, SparseCore 0:
  117.9 78.6 reduce-scatter.1

commit v3 on v2

v3 whole, which is shorter than its diff:
```python
import jax
import jax.numpy as jnp
import numpy as np
from jax import lax
from jax.experimental import pallas as pl
from jax.experimental.pallas import tpu as pltpu
from jax.sharding import PartitionSpec as P

TGT_DEV = 16
NDIAG = 11
Z_DEV = 8

XS, ZS, CS = 4, 16, 2
PLANE = XS * CS
QROWS = PLANE * TGT_DEV


def place(x, z, c):
    return ((x % XS) * ZS + z % ZS) * CS + c % CS


plane_groups = [[place(x, z, c) for x in range(XS) for c in range(CS)] for z in range(ZS)]
PAIR = 2
STATIONS = ZS // PAIR
WIDE = PLANE * PAIR
wide_groups = [
    [place(x, h * PAIR + p, c) for x in range(XS) for p in range(PAIR) for c in range(CS)]
    for h in range(STATIONS)
]
ring_groups = [[place(x, z, c) for z in range(ZS)] for x in range(XS) for c in range(CS)]


def ring_step(values, step):
    pairs = [
        (place(x, z, c), place(x, z + step * PAIR, c))
        for x in range(XS)
        for z in range(ZS)
        for c in range(CS)
    ]
    return lax.ppermute(values, "tgt", pairs)


pair_first, pair_second = np.triu_indices(10)


def solve_normal(matrix, right_side):
    basis_count = right_side.shape[0]
    rows_of = [[None] * basis_count for column in range(basis_count)]
    for p in range(len(pair_first)):
        b = int(pair_first[p])
        c = int(pair_second[p])
        rows_of[b][c] = matrix[p]
        rows_of[c][b] = matrix[p]
    vector = [right_side[b] for b in range(basis_count)]
    for k in range(basis_count):
        inverse = 1.0 / rows_of[k][k]
        for r in range(k + 1, basis_count):
            factor = rows_of[r][k] * inverse
            for c in range(k + 1, basis_count):
                rows_of[r][c] = rows_of[r][c] - factor * rows_of[k][c]
            vector[r] = vector[r] - factor * vector[k]
    answer = [None] * basis_count
    for k in reversed(range(basis_count)):
        running = vector[k]
        for c in range(k + 1, basis_count):
            running = running - rows_of[k][c] * answer[c]
        answer[k] = running / rows_of[k][k]
    gain_total = right_side[0] * answer[0]
    for b in range(1, basis_count):
        gain_total = gain_total + right_side[b] * answer[b]
    return gain_total


def basis_windows(rest_basis, shifts, first_wave, length):

    def one_shift(shift_value):
        return lax.dynamic_slice_in_dim(rest_basis, first_wave + shift_value, length, axis=1)

    return jax.vmap(one_shift)(shifts)


def normal_terms(weight_sum, flux_sum, windows):
    products = windows[:, pair_first, :] * windows[:, pair_second, :]
    matrix = jnp.einsum("ti,zpi->ztp", weight_sum, products, precision=lax.Precision.HIGHEST)
    right_side = jnp.einsum("ti,zbi->ztb", flux_sum, windows, precision=lax.Precision.HIGHEST)
    return (matrix, right_side)


def fit_from(matrix, right_side):
    pairs = jnp.transpose(matrix, (2, 0, 1)).reshape(matrix.shape[2], -1)
    sides = jnp.transpose(right_side, (2, 0, 1)).reshape(right_side.shape[2], -1)
    gain = solve_normal(pairs, sides).reshape(matrix.shape[0], matrix.shape[1])
    return gain.T


GROUP = 4


def split_kernel(ivar_ref, res_ref, out_ref):
    lanes = out_ref.shape[-1]
    for part in range(PLANE):
        columns = slice(part * lanes, (part + 1) * lanes)
        out_ref[part, 0] = ivar_ref[:, columns]
        out_ref[part, 1:] = res_ref[:, :, columns]


def split_lanes(ivar, res):
    diagonals, row_count, wave_dev = res.shape
    lanes = wave_dev // PLANE
    return pl.pallas_call(
        split_kernel,
        out_shape=jax.ShapeDtypeStruct((PLANE, diagonals + 1, row_count, lanes), res.dtype),
        compiler_params=pltpu.CompilerParams(vmem_limit_bytes=40 << 20),
        cost_estimate=pl.CostEstimate(
            flops=0, bytes_accessed=4 * (diagonals + 1) * row_count * wave_dev, transcendentals=0
        ),
    )(ivar, res)


def members(target_ref, step):
    per_x = CS * TGT_DEV
    local = lax.broadcasted_iota(jnp.int32, (GROUP * QROWS, 1), 0)
    q = local % QROWS
    plane_z = step * GROUP + local // QROWS
    wanted = (q // per_x) * (ZS * per_x) + plane_z * per_x + q % per_x
    return jnp.where(target_ref[...] == wanted, 1.0, 0.0).astype(jnp.bfloat16)


def res_kernel(target_ref, rows_ref, res_ref, terms):
    sources, planes, row_count, lanes = rows_ref.shape
    step = pl.program_id(0)

    @pl.when(step == 0)
    def fill_terms():
        def one_source(source, carry):
            rows = pl.ds(pl.multiple_of(source * row_count, row_count), row_count)
            weight = rows_ref[source, 0].astype(jnp.float32)
            for plane in range(1, planes):
                product = weight * rows_ref[source, plane].astype(jnp.float32)
                terms[rows, (plane - 1) * lanes : plane * lanes] = product.astype(jnp.bfloat16)
            return carry

        lax.fori_loop(0, sources, one_source, 0)

    sums = jnp.dot(members(target_ref, step), terms[...], preferred_element_type=jnp.float32)
    for g in range(GROUP):
        for owner in range(PLANE):
            first = g * QROWS + owner * TGT_DEV
            block = sums[first : first + TGT_DEV].astype(jnp.bfloat16)
            for diagonal in range(planes - 1):
                res_ref[g, owner, diagonal] = block[:, diagonal * lanes : (diagonal + 1) * lanes]


def coadd_res_rows(targets, rows):
    sources, planes, row_count, lanes = rows.shape
    out_shape = (ZS, PLANE, planes - 1, TGT_DEV, lanes)
    return pl.pallas_call(
        res_kernel,
        out_shape=jax.ShapeDtypeStruct(out_shape, jnp.bfloat16),
        grid=(ZS // GROUP,),
        in_specs=[
            pl.BlockSpec((1, sources * row_count), lambda i: (0, 0)),
            pl.BlockSpec(rows.shape, lambda i: (0, 0, 0, 0)),
        ],
        out_specs=pl.BlockSpec((GROUP,) + out_shape[1:], lambda i: (i, 0, 0, 0, 0)),
        scratch_shapes=[pltpu.VMEM((sources * row_count, (planes - 1) * lanes), jnp.bfloat16)],
        compiler_params=pltpu.CompilerParams(vmem_limit_bytes=56 << 20),
        cost_estimate=pl.CostEstimate(
            flops=2 * ZS * QROWS * sources * row_count * (planes - 1) * lanes,
            bytes_accessed=2 * (rows.size + ZS * QROWS * planes * lanes),
            transcendentals=0,
        ),
    )(targets, rows)


def half_swap(values):
    return pltpu.roll(values, values.shape[-1] // 2, 1)


def mix_kernel(ivar_ref, flux_ref, out_ref):
    row_count, lanes = out_ref.shape[1:]
    first = lax.broadcasted_iota(jnp.int32, (row_count, lanes), 1) < lanes // 2
    for tile in range(WIDE // 2):
        columns = slice(tile * lanes, (tile + 1) * lanes)
        ivar = ivar_ref[:, columns].astype(jnp.float32)
        flux = flux_ref[:, columns].astype(jnp.float32)
        low = jnp.where(first, ivar, half_swap(flux))
        high = jnp.where(first, half_swap(ivar), flux)
        out_ref[2 * tile] = low.astype(out_ref.dtype)
        out_ref[2 * tile + 1] = high.astype(out_ref.dtype)


def mix_pair(ivar, flux):
    row_count, wave_dev = ivar.shape
    return pl.pallas_call(
        mix_kernel,
        out_shape=jax.ShapeDtypeStruct((WIDE, row_count, 2 * wave_dev // WIDE), ivar.dtype),
        cost_estimate=pl.CostEstimate(
            flops=0, bytes_accessed=8 * row_count * wave_dev, transcendentals=0
        ),
    )(ivar, flux)


BATCH = 2


def mix_sum_kernel(target_ref, rows_ref, sums_ref, terms):
    sources, row_count, lanes = rows_ref.shape
    block_rows = WIDE * TGT_DEV
    step = pl.program_id(0)

    @pl.when(step == 0)
    def fill_terms():
        first = lax.broadcasted_iota(jnp.int32, (row_count, lanes), 1) < lanes // 2
        for source in range(sources):
            rows = slice(source * row_count, (source + 1) * row_count)
            values = rows_ref[source].astype(jnp.float32)
            product = jnp.where(first, values, values * half_swap(values))
            rounded = product.astype(jnp.bfloat16)
            terms[rows, 0:lanes] = rounded
            rest = product - rounded.astype(jnp.float32)
            terms[rows, lanes : 2 * lanes] = rest.astype(jnp.bfloat16)

    per_x = PAIR * CS * TGT_DEV
    local = lax.broadcasted_iota(jnp.int32, (BATCH * block_rows, 1), 0)
    q = local % block_rows
    station = step * BATCH + local // block_rows
    wanted = (q // per_x) * (STATIONS * per_x) + station * per_x + q % per_x
    member = jnp.where(target_ref[...] == wanted, 1.0, 0.0).astype(jnp.bfloat16)
    sums = jnp.dot(member, terms[...], preferred_element_type=jnp.float32)
    total = sums[:, 0:lanes] + sums[:, lanes : 2 * lanes]
    for b in range(BATCH):
        sums_ref[b] = total[b * block_rows : (b + 1) * block_rows]


def mix_sum(targets, rows):
    sources, row_count, lanes = rows.shape
    block_rows = WIDE * TGT_DEV
    return pl.pallas_call(
        mix_sum_kernel,
        out_shape=jax.ShapeDtypeStruct((STATIONS, block_rows, lanes), jnp.float32),
        grid=(STATIONS // BATCH,),
        in_specs=[
            pl.BlockSpec((1, sources * row_count), lambda i: (0, 0)),
            pl.BlockSpec(rows.shape, lambda i: (0, 0, 0)),
        ],
        out_specs=pl.BlockSpec((BATCH, block_rows, lanes), lambda i: (i, 0, 0)),
        scratch_shapes=[pltpu.VMEM((sources * row_count, 2 * lanes), jnp.bfloat16)],
        compiler_params=pltpu.CompilerParams(vmem_limit_bytes=40 << 20),
        cost_estimate=pl.CostEstimate(
            flops=4 * STATIONS * block_rows * sources * row_count * lanes,
            bytes_accessed=2 * rows.size + 4 * STATIONS * block_rows * lanes,
            transcendentals=0,
        ),
    )(targets, rows)


def ring_sum(parts, station):
    def part(offset):
        return lax.dynamic_index_in_dim(parts, (station + offset) % STATIONS, 0, keepdims=False)

    half = STATIONS // 2
    up, down = part(half), part(half + 1)
    for s in range(half):
        up = ring_step(up, 1)
        if s < half - 1:
            up = up + part(half - 1 - s)
            down = ring_step(down, -1)
            if s < half - 2:
                down = down + part(half + 2 + s)
    return part(0) + up + down


def exchange(values, groups):
    return lax.all_to_all(
        values, "tgt", split_axis=0, concat_axis=0, axis_index_groups=groups, tiled=True
    )


def scatter_sum(values):
    return lax.psum_scatter(
        values, "tgt", scatter_dimension=0, axis_index_groups=ring_groups, tiled=False
    )


def shards(
    exposure_flux,
    exposure_ivar,
    exposure_res,
    target_of_row,
    valid_of_row,
    rest_basis,
    redshift_shift,
):
    device = lax.axis_index("tgt")
    my_z = (device // CS) % ZS
    row_count, wave_dev = exposure_flux.shape
    masked = jnp.where(valid_of_row == 1, target_of_row, -1)
    targets = lax.dynamic_index_in_dim(
        masked.reshape(XS, ZS, CS * row_count), my_z, 1, keepdims=False
    ).reshape(1, -1)
    wide_targets = lax.dynamic_index_in_dim(
        masked.reshape(XS, STATIONS, PAIR * CS * row_count), my_z // PAIR, 1, keepdims=False
    ).reshape(1, -1)

    mixed = exchange(mix_pair(exposure_ivar, exposure_flux), wide_groups)
    packed = split_lanes(exposure_ivar, jnp.transpose(exposure_res, (1, 0, 2)))
    packed, mixed = lax.optimization_barrier((packed, mixed))
    rows = exchange(packed, plane_groups)
    sums = ring_sum(mix_sum(wide_targets, mixed), my_z // PAIR)
    rows, sums = lax.optimization_barrier((rows, sums))
    res_sum = scatter_sum(coadd_res_rows(targets, rows))

    own = exchange(sums.reshape(WIDE, TGT_DEV, -1), wide_groups)
    own = jnp.transpose(own.reshape(WIDE, TGT_DEV, 2, wave_dev // WIDE), (2, 1, 0, 3))
    own = own.reshape(2, TGT_DEV, wave_dev)
    everything = lax.all_gather(own.astype(jnp.bfloat16), "band", axis=2, tiled=True)
    everything = everything.astype(jnp.float32)
    coadd_flux = own[1] / own[0]
    band_index = lax.axis_index("band")
    shifts = lax.dynamic_slice_in_dim(redshift_shift, band_index * Z_DEV, Z_DEV)
    windows = basis_windows(rest_basis, shifts, 0, everything.shape[2])
    fit_gain = fit_from(*normal_terms(everything[0], everything[1], windows))

    back = exchange(res_sum, plane_groups)
    own_res = jnp.transpose(back, (1, 2, 0, 3)).reshape(NDIAG, TGT_DEV, wave_dev)
    coadd_res = (own_res.astype(jnp.float32) / own[0][None]).astype(jnp.bfloat16)
    return (coadd_flux, jnp.transpose(coadd_res, (1, 0, 2)), fit_gain)


def solution(mesh):
    in_specs = (P("tgt", "band"), P("tgt", "band"), P("tgt", None, "band"), P(), P(), P(), P())
    out_specs = (P("tgt", "band"), P("tgt", None, "band"), P("tgt", "band"))
    return jax.shard_map(shards, mesh=mesh, in_specs=in_specs, out_specs=out_specs, check_vma=False)
```

time: 226 us -> 206 us (0.912)
  starting transfers between devices: 92.5 us -> 66.6 us
  waiting for transfers between devices: 42.7 us -> 56.6 us
  Pallas kernels: 23.6 us -> 18.6 us
  local copies, waits for them, and re-layouts: 28.6 us -> 24.5 us
    ppermute x15 -> x7, starting transfers between devices: 51.8 us -> 29.1 us  [ring_step(): return lax.ppermute(values, 'tgt', pairs)]
    reduce_scatter x1, waiting for transfers between devices: 18.1 us -> 30.3 us  [scatter_sum(): lax.psum_scatter(values, 'tgt', scatter_dimension=0, axis_index_groups=ri...]
    gather x24, local copies, waits for them, and re-layouts: 16.6 us -> 10.9 us
    pallas_call x4, Pallas kernels: 23.6 us -> 18.6 us  [the longest x1 11 us: coadd_res_rows(): pl.pallas_call(res_kernel, out_shape=jax.ShapeDtypeStruct(out_shape, jnp....]
    all_to_all x4, starting transfers between devices: 40.7 us -> 37.5 us  [exchange(): lax.all_to_all(values, 'tgt', split_axis=0, concat_axis=0, axis_index_gro...]
    all_to_all x4, waiting for transfers between devices: 8.14 us -> 10.7 us  [exchange(): lax.all_to_all(values, 'tgt', split_axis=0, concat_axis=0, axis_index_gro...]
    unnamed x17 -> x16, local copies, waits for them, and re-layouts: 0.89 us -> 3.4 us
    ppermute x15 -> x7, waiting for transfers between devices: 16.4 us -> 15.6 us  [ring_step(): return lax.ppermute(values, 'tgt', pairs)]
  transfers between devices with their start and end apart: 20 -> 12, of which waited for: 16 -> 9; matrix products, arithmetic and copies ran while one was open for 17% -> 16% of each run, Pallas kernels for 3% -> 3%
where the time goes in v3:
time: 206 us; the launch traced here: 205 us
  starting transfers between devices  66.6 us (32%)
  waiting for transfers between devices  56.6 us (27%)
  local copies, waits for them, and re-layouts  24.5 us (12%)
  Pallas kernels  18.6 us (9%)
  between operations  14.5 us (7%)
  blocking collectives  12.3 us (6%)
  matrix products  8.25 us (4%)
  other arithmetic  3.18 us (2%)
    all_to_all x4, starting transfers between devices, exchange(): lax.all_to_all(values, 'tgt', split_axis=0, concat_axis=0, axis_index_gro...  37.5 us
    reduce_scatter x1, waiting for transfers between devices, scatter_sum(): lax.psum_scatter(values, 'tgt', scatter_dimension=0, axis_index_groups=ri...  30.3 us
    ppermute x7, starting transfers between devices, ring_step(): return lax.ppermute(values, 'tgt', pairs)  29.1 us
    ppermute x7, waiting for transfers between devices, ring_step(): return lax.ppermute(values, 'tgt', pairs)  15.6 us
    all_gather x1, blocking collectives, shards(): lax.all_gather(own.astype(jnp.bfloat16), 'band', axis=2, tiled=True)  12.3 us
    pallas_call x1, Pallas kernels, coadd_res_rows(): pl.pallas_call(res_kernel, out_shape=jax.ShapeDtypeStruct(out_shape, jnp....  11 us
    gather x24, local copies, waits for them, and re-layouts  10.9 us
    all_to_all x4, waiting for transfers between devices, exchange(): lax.all_to_all(values, 'tgt', split_axis=0, concat_axis=0, axis_index_gro...  10.7 us
  transfers between devices with their start and end apart: 12, of which 9 were waited for; matrix products, arithmetic and copies ran while one was open for 16% of the time, Pallas kernels for 3%

profile of v3, /device:TPU:1, one launch (start us, length us, event | category | flops | bytes accessed | tf_op | source)
XLA Modules:
  0.0 204.8 jit_solution(7857491704180872257)
XLA Ops:
  7.2 2.1 %shard_map.131 = bf16[16,128,128]{2,1,0:T(8,128)(2,1)} custom-call(bf16[128,1024]{1,0:T(8,128)(2,1)} %ivar_ref.3, bf16[128,1024]{1,0:T(8,128)(2,1)} %flux_ref.1), custom_call_target="tpu_custom_call" | custom-call | bytes 1048576 | tf_op jit(solution)/shard_map/pallas_call | solution.py:195
  9.2 10.2 %all-to-all-start = ((bf16[16,128,128]{2,1,0:T(8,128)(2,1)}), bf16[16,128,128]{2,1,0:T(8,128)(2,1)S(1)}, u32[]{:S(2)}, u32[]{:S(2)}) async-start(bf16[16,128,128]{2,1,0:T(8,128)(2,1)} %shard_map.131), calls=%async_computation | async-start | bytes 1048576 | tf_op jit(solution)/shard_map/all_to_all | solution.py:275
  19.5 1.8 copy-done
  21.3 0.9 copy-done.1
  22.2 2.4 %shard_map.130 = bf16[8,12,128,128]{3,2,1,0:T(8,128)(2,1)} custom-call(bf16[128,1024]{1,0:T(8,128)(2,1)S(1)} %copy-done.1, bf16[11,128,1024]{2,1,0:T(8,128)(2,1)S(1)} %bitcast.394), custom_call_target="tpu_custom_call" | custom-call | bytes 6291456 | tf_op jit(solution)/shard_map/pallas_call | solution.py:110
  24.6 4.7 %all-to-all-done.rows_ref = bf16[16,128,128]{2,1,0:T(8,128)(2,1)S(1)} async-done(((bf16[16,128,128]{2,1,0:T(8,128)(2,1)}), bf16[16,128,128]{2,1,0:T(8,128)(2,1)S(1)}, u32[]{:S(2)}, u32[]{:S(2)}) %all-to-all-start) | async-done | bytes 524320 | tf_op jit(solution)/shard_map/all_to_all | solution.py:275
  29.4 5.5 %all-to-all-start.1 = ((bf16[8,12,128,128]{3,2,1,0:T(8,128)(2,1)}), bf16[8,12,128,128]{3,2,1,0:T(8,128)(2,1)}, u32[]{:S(2)}, u32[]{:S(2)}) async-start(bf16[8,12,128,128]{3,2,1,0:T(8,128)(2,1)} %shard_map.130), calls=%async_computation.1 | async-start | bytes 6291456 | tf_op jit(solution)/shard_map/all_to_all | solution.py:275
  34.9 3.2 %shard_map.132 = f32[8,256,128]{2,1,0:T(8,128)S(1)} custom-call(s32[1,2048]{1,0:T(1,128)S(1)} %bitcast.395, bf16[16,128,128]{2,1,0:T(8,128)(2,1)S(1)} %all-to-all-done.rows_ref), custom_call_target="tpu_custom_call" | custom-call | flops 2147483648 | bytes 1572864 | tf_op jit(solution)/shard_map/pallas_call | solution.py:239
  38.2 1.9 collective-permute-start
  40.2 7.5 %collective-permute-start.4 = (f32[256,128]{1,0:T(8,128)S(1)}, f32[256,128]{1,0:T(8,128)S(1)}, u32[]{:S(2)}, u32[]{:S(2)}) collective-permute-start(f32[256,128]{1,0:T(8,128)S(1)} %get-tuple-element.32), channel_id=1, source_target_pairs={{0,112},{4,116},{8,120},{12,124},{16,0},{20,4},{24,8},{28,12},{32,... | collective-permute-start | bytes 393224 | tf_op jit(solution)/shard_map/ppermute | solution.py:40
  47.7 2.5 %collective-permute-done = f32[256,128]{1,0:T(8,128)S(1)} collective-permute-done((f32[256,128]{1,0:T(8,128)S(1)}, f32[256,128]{1,0:T(8,128)S(1)}, u32[]{:S(2)}, u32[]{:S(2)}) %collective-permute-start) | collective-permute-done | bytes 131104 | tf_op jit(solution)/shard_map/ppermute | solution.py:40
  50.3 1.9 collective-permute-start.1
  52.2 0.6 collective-permute-done.4
  52.8 7.3 %collective-permute-done.1 = f32[256,128]{1,0:T(8,128)S(1)} collective-permute-done((f32[256,128]{1,0:T(8,128)S(1)}, f32[256,128]{1,0:T(8,128)S(1)}, u32[]{:S(2)}, u32[]{:S(2)}) %collective-permute-start.1) | collective-permute-done | bytes 131104 | tf_op jit(solution)/shard_map/ppermute | solution.py:40
  60.2 1.9 collective-permute-start.2
  62.1 6.8 %collective-permute-start.5 = (f32[256,128]{1,0:T(8,128)S(1)}, f32[256,128]{1,0:T(8,128)S(1)}, u32[]{:S(2)}, u32[]{:S(2)}) collective-permute-start(f32[256,128]{1,0:T(8,128)S(1)} %get-tuple-element.30), channel_id=1, source_target_pairs={{0,112},{4,116},{8,120},{12,124},{16,0},{20,4},{24,8},{28,12},{32,... | collective-permute-start | bytes 393224 | tf_op jit(solution)/shard_map/ppermute | solution.py:40
  68.9 2.6 %collective-permute-done.2 = f32[256,128]{1,0:T(8,128)S(1)} collective-permute-done((f32[256,128]{1,0:T(8,128)S(1)}, f32[256,128]{1,0:T(8,128)S(1)}, u32[]{:S(2)}, u32[]{:S(2)}) %collective-permute-start.2) | collective-permute-done | bytes 131104 | tf_op jit(solution)/shard_map/ppermute | solution.py:40
  71.5 3.1 %collective-permute-start.3 = (f32[256,128]{1,0:T(8,128)S(1)}, f32[256,128]{1,0:T(8,128)S(1)}, u32[]{:S(2)}, u32[]{:S(2)}) collective-permute-start(f32[256,128]{1,0:T(8,128)S(1)} %get-tuple-element.27), channel_id=1, source_target_pairs={{0,16},{4,20},{8,24},{12,28},{16,32},{20,36},{24,40},{28,44},{32,4... | collective-permute-start | bytes 393224 | tf_op jit(solution)/shard_map/ppermute | solution.py:40
  74.6 6.0 %collective-permute-start.6 = (f32[256,128]{1,0:T(8,128)S(1)}, f32[256,128]{1,0:T(8,128)S(1)}, u32[]{:S(2)}, u32[]{:S(2)}) collective-permute-start(f32[256,128]{1,0:T(8,128)S(1)} %get-tuple-element.28), channel_id=1, source_target_pairs={{0,112},{4,116},{8,120},{12,124},{16,0},{20,4},{24,8},{28,12},{32,... | collective-permute-start | bytes 393224 | tf_op jit(solution)/shard_map/ppermute | solution.py:40
  80.7 0.6 constant_dynamic-slice_fusion.1
  81.3 1.0 collective-permute-done.3
  82.3 1.6 collective-permute-done.6
  83.9 0.7 fusion.8
  84.5 11.0 %shard_map.133 = bf16[16,8,11,16,128]{4,3,2,1,0:T(8,128)(2,1)} custom-call(s32[1,1024]{1,0:T(1,128)} %bitcast.408, bf16[8,12,128,128]{3,2,1,0:T(8,128)(2,1)} %all-to-all-done.1.rows_ref), custom_call_target="tpu_custom_call" | custom-call | flops 5905580032 | bytes 9437184 | tf_op jit(solution)/shard_map/pallas_call | solution.py:157
  95.5 0.6 copy-done.7
  96.2 0.1 fusion.73
  96.2 8.7 %all-to-all-start.2 = ((f32[16,16,128]{2,1,0:T(8,128)}), f32[16,16,128]{2,1,0:T(8,128)S(1)}, u32[]{:S(2)}, u32[]{:S(2)}) async-start(f32[16,16,128]{2,1,0:T(8,128)} %bitcast.10), calls=%async_computation.2 | async-start | bytes 262144 | tf_op jit(solution)/shard_map/all_to_all | solution.py:275
  105.0 11.1 %while.1 = (s32[]{:T(128)}, f32[10,4608]{1,0:T(8,128)S(1)}, s32[8,2]{0,1:T(2,128)S(1)}, f32[8,10,4096]{2,1,0:T(8,128)S(1)}, s32[]{:T(128)}) while((s32[]{:T(128)}, f32[10,4608]{1,0:T(8,128)S(1)}, s32[8,2]{0,1:T(2,128)S(1)}, f32[8,10,4096]{2,1,0:T(8,128)S(1)}, s32[]{:T(128)}) %tuple.42), condition=%wide.while_cond, body=%wide.while_body.sunk | while | flops 2 | bytes 524393 | solution.py:77
  105.0 0.1 constant_dynamic-slice_fusion.4
  105.0 0.5 slice.757
  105.6 0.8 bitcast_dynamic-update-slice_fusion.2
  106.4 0.5 slice.757
  106.9 0.8 bitcast_dynamic-update-slice_fusion.2
  107.8 0.5 slice.757
  108.3 0.8 bitcast_dynamic-update-slice_fusion.2
  109.2 0.5 slice.757
  109.7 0.8 bitcast_dynamic-update-slice_fusion.2
  110.5 0.1 constant_dynamic-slice_fusion.4
  110.6 0.5 slice.757
  111.1 0.8 bitcast_dynamic-update-slice_fusion.2
  112.0 0.5 slice.757
  112.5 0.8 bitcast_dynamic-update-slice_fusion.2
  113.4 0.5 slice.757
  113.9 0.8 bitcast_dynamic-update-slice_fusion.2
  114.7 0.5 slice.757
  115.3 0.8 bitcast_dynamic-update-slice_fusion.2
  116.0 0.8 copy.23
  116.8 4.0 %gather_fusion.1 = f32[55,8,4096]{2,1,0:T(8,128)} fusion(f32[8,10,4096]{2,0,1:T(8,128)S(1)} %copy.23, s32[1024]{0:T(1024)S(1)} %pad_clamp_fusion), kind=kCustom, calls=%fused_computation.1 | custom fusion | bytes 14418140 | tf_op jit(solution)/shard_map/gather | solution.py:83
  120.8 3.9 %gather_fusion = f32[55,8,4096]{2,1,0:T(8,128)} fusion(f32[8,10,4096]{2,0,1:T(8,128)S(1)} %copy.23, s32[1024]{0:T(1024)S(1)} %pad_clamp_fusion.1), kind=kCustom, calls=%fused_computation | custom fusion | bytes 14418140 | tf_op jit(solution)/shard_map/gather | solution.py:83
  124.8 0.2 reshape.237
  125.0 0.1 bitcast_convert_fusion
  125.1 0.1 convert_element_type.24
  125.3 12.3 %all_gather.3 = bf16[2,16,4096]{2,1,0:T(8,128)(2,1)S(1)} all-gather(bf16[2,16,1024]{2,1,0:T(8,128)(2,1)S(1)} %convert_element_type.24), channel_id=1, replica_groups=mesh['tgt'=128,'band'=4] {'band'}, dimensions={2}, use_global_device_ids=true | all-gather | bytes 327680 | tf_op jit(solution)/shard_map/all_gather | solution.py:317
  137.6 0.2 fusion.74
  137.8 1.1 convolution_bitcast_fusion
  138.9 7.2 %fusion.3 = f32[55,8,16]{2,1,0:T(8,128)S(1)} fusion(f32[55,8,4096]{2,1,0:T(8,128)} %gather_fusion, f32[55,8,4096]{2,1,0:T(8,128)} %gather_fusion.1, bf16[2,16,4096]{2,1,0:T(8,128)(2,1)S(1)} %all_gather.3), kind=kOutput, calls=%fused_computation.7 | convolution fusion | flops 347832320 | bytes 14577152 | tf_op jit(solution)/shard_map/ti,zpi->ztp/dot_general | solution.py:84
  146.1 30.3 %reduce-scatter.2.cloned.1.call-done = bf16[1,8,11,16,128]{4,3,2,1,0:T(8,128)(2,1)} async-done(((bf16[16,8,11,16,128]{4,3,2,1,0:T(8,128)(2,1)}), bf16[1,8,11,16,128]{4,3,2,1,0:T(8,128)(2,1)}) %reduce-scatter.2.cloned.1.call-update) | async-done | bytes 360464 | tf_op jit(solution)/shard_map/reduce_scatter | solution.py:281
  176.3 13.1 %all-to-all-start.3 = ((bf16[8,11,16,128]{3,2,1,0:T(8,128)(2,1)}), bf16[8,11,16,128]{3,2,1,0:T(8,128)(2,1)S(1)}, u32[]{:S(2)}, u32[]{:S(2)}) async-start(bf16[8,11,16,128]{3,2,1,0:T(8,128)(2,1)} %bitcast.397), calls=%async_computation.4 | async-start | bytes 720896 | tf_op jit(solution)/shard_map/all_to_all | solution.py:275
  189.5 0.1 squeeze.300
  189.6 0.1 squeeze.299
  189.7 0.6 div.109
  190.4 0.8 add_bitcast_fusion
  191.2 6.0 %all-to-all-done.3 = bf16[8,11,16,128]{3,2,1,0:T(8,128)(2,1)S(1)} async-done(((bf16[8,11,16,128]{3,2,1,0:T(8,128)(2,1)}), bf16[8,11,16,128]{3,2,1,0:T(8,128)(2,1)S(1)}, u32[]{:S(2)}, u32[]{:S(2)}) %all-to-all-start.3) | async-done | bytes 360480 | tf_op jit(solution)/shard_map/all_to_all | solution.py:275
  197.1 0.8 fusion.7
  (40 shorter events, 0.8 us)
Async XLA Ops:
  9.2 20.1 %all-to-all-start = ((bf16[16,128,128]{2,1,0:T(8,128)(2,1)}), bf16[16,128,128]{2,1,0:T(8,128)(2,1)S(1)}, u32[]{:S(2)}, u32[]{:S(2)}) async-start(bf16[16,128,128]{2,1,0:T(8,128)(2,1)} %shard_map.131), calls=%async_computation | async-start | bytes 1048576 | tf_op jit(solution)/shard_map/all_to_all | solution.py:275
  19.5 1.8 copy-start
  21.3 0.9 copy-start.1
  24.6 10.3 %copy-start.3 = (s32[16384]{0:T(1024)S(1)}, s32[16384]{0:T(1024)}, u32[]{:S(2)}) copy-start(s32[16384]{0:T(1024)} %param.14) | copy-start | bytes 196612
  24.6 10.3 %copy-start.4 = (s32[16384]{0:T(1024)S(1)}, s32[16384]{0:T(1024)}, u32[]{:S(2)}) copy-start(s32[16384]{0:T(1024)} %param.15) | copy-start | bytes 196612
  29.4 55.2 %all-to-all-start.1 = ((bf16[8,12,128,128]{3,2,1,0:T(8,128)(2,1)}), bf16[8,12,128,128]{3,2,1,0:T(8,128)(2,1)}, u32[]{:S(2)}, u32[]{:S(2)}) async-start(bf16[8,12,128,128]{3,2,1,0:T(8,128)(2,1)} %shard_map.130), calls=%async_computation.1 | async-start | bytes 6291456 | tf_op jit(solution)/shard_map/all_to_all | solution.py:275
  34.9 141.5 %reduce-scatter.2.cloned.1.call-start = ((), (), s32[]{:S(2)}) async-start(), calls=%async_computation.5 | async-start | bytes 6127616 | tf_op jit(solution)/shard_map/reduce_scatter | solution.py:281
  38.2 12.0 %collective-permute-start = (f32[256,128]{1,0:T(8,128)S(1)}, f32[256,128]{1,0:T(8,128)S(1)}, u32[]{:S(2)}, u32[]{:S(2)}) collective-permute-start(f32[256,128]{1,0:T(8,128)S(1)} %get-tuple-element.31), channel_id=1, source_target_pairs={{0,16},{4,20},{8,24},{12,28},{16,32},{20,36},{24,40},{28,44},{32,4... | collective-permute-start | bytes 393224 | tf_op jit(solution)/shard_map/ppermute | solution.py:40
  40.2 12.6 %collective-permute-start.4 = (f32[256,128]{1,0:T(8,128)S(1)}, f32[256,128]{1,0:T(8,128)S(1)}, u32[]{:S(2)}, u32[]{:S(2)}) collective-permute-start(f32[256,128]{1,0:T(8,128)S(1)} %get-tuple-element.32), channel_id=1, source_target_pairs={{0,112},{4,116},{8,120},{12,124},{16,0},{20,4},{24,8},{28,12},{32,... | collective-permute-start | bytes 393224 | tf_op jit(solution)/shard_map/ppermute | solution.py:40
  50.3 9.9 %collective-permute-start.1 = (f32[256,128]{1,0:T(8,128)S(1)}, f32[256,128]{1,0:T(8,128)S(1)}, u32[]{:S(2)}, u32[]{:S(2)}) collective-permute-start(f32[256,128]{1,0:T(8,128)S(1)} %bitcast_add_fusion.4), channel_id=1, source_target_pairs={{0,16},{4,20},{8,24},{12,28},{16,32},{20,36},{24,40},{28,44},{32,4... | collective-permute-start | bytes 393224 | tf_op jit(solution)/shard_map/ppermute | solution.py:40
  60.2 11.3 %collective-permute-start.2 = (f32[256,128]{1,0:T(8,128)S(1)}, f32[256,128]{1,0:T(8,128)S(1)}, u32[]{:S(2)}, u32[]{:S(2)}) collective-permute-start(f32[256,128]{1,0:T(8,128)S(1)} %get-tuple-element.29), channel_id=1, source_target_pairs={{0,16},{4,20},{8,24},{12,28},{16,32},{20,36},{24,40},{28,44},{32,4... | collective-permute-start | bytes 393224 | tf_op jit(solution)/shard_map/ppermute | solution.py:40
  62.1 9.4 %collective-permute-start.5 = (f32[256,128]{1,0:T(8,128)S(1)}, f32[256,128]{1,0:T(8,128)S(1)}, u32[]{:S(2)}, u32[]{:S(2)}) collective-permute-start(f32[256,128]{1,0:T(8,128)S(1)} %get-tuple-element.30), channel_id=1, source_target_pairs={{0,112},{4,116},{8,120},{12,124},{16,0},{20,4},{24,8},{28,12},{32,... | collective-permute-start | bytes 393224 | tf_op jit(solution)/shard_map/ppermute | solution.py:40
  71.5 10.7 %collective-permute-start.3 = (f32[256,128]{1,0:T(8,128)S(1)}, f32[256,128]{1,0:T(8,128)S(1)}, u32[]{:S(2)}, u32[]{:S(2)}) collective-permute-start(f32[256,128]{1,0:T(8,128)S(1)} %get-tuple-element.27), channel_id=1, source_target_pairs={{0,16},{4,20},{8,24},{12,28},{16,32},{20,36},{24,40},{28,44},{32,4... | collective-permute-start | bytes 393224 | tf_op jit(solution)/shard_map/ppermute | solution.py:40
  74.6 9.3 %collective-permute-start.6 = (f32[256,128]{1,0:T(8,128)S(1)}, f32[256,128]{1,0:T(8,128)S(1)}, u32[]{:S(2)}, u32[]{:S(2)}) collective-permute-start(f32[256,128]{1,0:T(8,128)S(1)} %get-tuple-element.28), channel_id=1, source_target_pairs={{0,112},{4,116},{8,120},{12,124},{16,0},{20,4},{24,8},{28,12},{32,... | collective-permute-start | bytes 393224 | tf_op jit(solution)/shard_map/ppermute | solution.py:40
  95.5 0.7 copy-start.7
  95.5 9.4 %copy-start.2 = (f32[10,4608]{1,0:T(8,128)S(1)}, f32[10,4608]{1,0:T(8,128)}, u32[]{:S(2)}) copy-start(f32[10,4608]{1,0:T(8,128)} %param.16) | copy-start | bytes 552964
  96.2 28.5 %all-to-all-start.2 = ((f32[16,16,128]{2,1,0:T(8,128)}), f32[16,16,128]{2,1,0:T(8,128)S(1)}, u32[]{:S(2)}, u32[]{:S(2)}) async-start(f32[16,16,128]{2,1,0:T(8,128)} %bitcast.10), calls=%async_computation.2 | async-start | bytes 262144 | tf_op jit(solution)/shard_map/all_to_all | solution.py:275
  104.9 11.9 %copy-start.6 = (s32[55]{0:T(128)S(1)}, s32[55]{0:T(128)}, u32[]{:S(2)}) copy-start(s32[55]{0:T(128)} %constant.161) | copy-start | bytes 664
  116.8 4.0 %copy-start.5 = (s32[55]{0:T(128)S(1)}, s32[55]{0:T(128)}, u32[]{:S(2)}) copy-start(s32[55]{0:T(128)} %constant.160) | copy-start | bytes 664
  176.3 20.8 %all-to-all-start.3 = ((bf16[8,11,16,128]{3,2,1,0:T(8,128)(2,1)}), bf16[8,11,16,128]{3,2,1,0:T(8,128)(2,1)S(1)}, u32[]{:S(2)}, u32[]{:S(2)}) async-start(bf16[8,11,16,128]{3,2,1,0:T(8,128)(2,1)} %bitcast.397), calls=%async_computation.4 | async-start | bytes 720896 | tf_op jit(solution)/shard_map/all_to_all | solution.py:275
Sparse Core Ops, SparseCore 0:
  95.6 80.6 reduce-scatter.1

commit v4 on v3

v4 whole, which is shorter than its diff:
```python
import jax
import jax.numpy as jnp
import numpy as np
from jax import lax
from jax.experimental import pallas as pl
from jax.experimental.pallas import tpu as pltpu
from jax.sharding import PartitionSpec as P

TGT_DEV = 16
NDIAG = 11
Z_DEV = 8

XS, ZS, CS = 4, 16, 2
PLANE = XS * CS
QROWS = PLANE * TGT_DEV


def place(x, z, c):
    return ((x % XS) * ZS + z % ZS) * CS + c % CS


plane_groups = [[place(x, z, c) for x in range(XS) for c in range(CS)] for z in range(ZS)]
PAIR = 2
STATIONS = ZS // PAIR
WIDE = PLANE * PAIR
wide_groups = [
    [place(x, h * PAIR + p, c) for x in range(XS) for p in range(PAIR) for c in range(CS)]
    for h in range(STATIONS)
]
ring_groups = [[place(x, z, c) for z in range(ZS)] for x in range(XS) for c in range(CS)]


def ring_step(values, step):
    pairs = [
        (place(x, z, c), place(x, z + step * PAIR, c))
        for x in range(XS)
        for z in range(ZS)
        for c in range(CS)
    ]
    return lax.ppermute(values, "tgt", pairs)


pair_first, pair_second = np.triu_indices(10)


def solve_normal(matrix, right_side):
    basis_count = right_side.shape[0]
    rows_of = [[None] * basis_count for column in range(basis_count)]
    for p in range(len(pair_first)):
        b = int(pair_first[p])
        c = int(pair_second[p])
        rows_of[b][c] = matrix[p]
        rows_of[c][b] = matrix[p]
    vector = [right_side[b] for b in range(basis_count)]
    for k in range(basis_count):
        inverse = 1.0 / rows_of[k][k]
        for r in range(k + 1, basis_count):
            factor = rows_of[r][k] * inverse
            for c in range(k + 1, basis_count):
                rows_of[r][c] = rows_of[r][c] - factor * rows_of[k][c]
            vector[r] = vector[r] - factor * vector[k]
    answer = [None] * basis_count
    for k in reversed(range(basis_count)):
        running = vector[k]
        for c in range(k + 1, basis_count):
            running = running - rows_of[k][c] * answer[c]
        answer[k] = running / rows_of[k][k]
    gain_total = right_side[0] * answer[0]
    for b in range(1, basis_count):
        gain_total = gain_total + right_side[b] * answer[b]
    return gain_total


def basis_windows(rest_basis, shifts, first_wave, length):

    def one_shift(shift_value):
        return lax.dynamic_slice_in_dim(rest_basis, first_wave + shift_value, length, axis=1)

    return jax.vmap(one_shift)(shifts)


def normal_terms(weight_sum, flux_sum, windows):
    products = windows[:, pair_first, :] * windows[:, pair_second, :]
    matrix = jnp.einsum("ti,zpi->ztp", weight_sum, products, precision=lax.Precision.HIGHEST)
    right_side = jnp.einsum("ti,zbi->ztb", flux_sum, windows, precision=lax.Precision.HIGHEST)
    return (matrix, right_side)


def fit_from(matrix, right_side):
    pairs = jnp.transpose(matrix, (2, 0, 1)).reshape(matrix.shape[2], -1)
    sides = jnp.transpose(right_side, (2, 0, 1)).reshape(right_side.shape[2], -1)
    gain = solve_normal(pairs, sides).reshape(matrix.shape[0], matrix.shape[1])
    return gain.T


def half_swap(values):
    return pltpu.roll(values, values.shape[-1] // 2, 1)


def mix_kernel(ivar_ref, flux_ref, out_ref):
    row_count, lanes = out_ref.shape[1:]
    first = lax.broadcasted_iota(jnp.int32, (row_count, lanes), 1) < lanes // 2
    for tile in range(WIDE // 2):
        columns = slice(tile * lanes, (tile + 1) * lanes)
        ivar = ivar_ref[:, columns].astype(jnp.float32)
        flux = flux_ref[:, columns].astype(jnp.float32)
        low = jnp.where(first, ivar, half_swap(flux))
        high = jnp.where(first, half_swap(ivar), flux)
        out_ref[2 * tile] = low.astype(out_ref.dtype)
        out_ref[2 * tile + 1] = high.astype(out_ref.dtype)


def mix_pair(ivar, flux):
    row_count, wave_dev = ivar.shape
    return pl.pallas_call(
        mix_kernel,
        out_shape=jax.ShapeDtypeStruct((WIDE, row_count, 2 * wave_dev // WIDE), ivar.dtype),
        cost_estimate=pl.CostEstimate(
            flops=0, bytes_accessed=8 * row_count * wave_dev, transcendentals=0
        ),
    )(ivar, flux)


FOLDS = (NDIAG + 1) // 2


def mix_res_kernel(res_ref, out_ref):
    row_count, lanes = out_ref.shape[2:]
    first = lax.broadcasted_iota(jnp.int32, (row_count, lanes), 1) < lanes // 2
    for fold in range(FOLDS):
        for tile in range(WIDE // 2):
            columns = slice(tile * lanes, (tile + 1) * lanes)
            one = res_ref[2 * fold, :, columns].astype(jnp.float32)
            if 2 * fold + 1 < NDIAG:
                two = res_ref[2 * fold + 1, :, columns].astype(jnp.float32)
            else:
                two = jnp.zeros_like(one)
            low = jnp.where(first, one, half_swap(two))
            high = jnp.where(first, half_swap(one), two)
            out_ref[2 * tile, fold] = low.astype(out_ref.dtype)
            out_ref[2 * tile + 1, fold] = high.astype(out_ref.dtype)


def mix_res(res):
    diagonals, row_count, wave_dev = res.shape
    return pl.pallas_call(
        mix_res_kernel,
        out_shape=jax.ShapeDtypeStruct(
            (WIDE, FOLDS, row_count, 2 * wave_dev // WIDE), res.dtype
        ),
        compiler_params=pltpu.CompilerParams(vmem_limit_bytes=40 << 20),
        cost_estimate=pl.CostEstimate(
            flops=0, bytes_accessed=4 * (diagonals + 1) * row_count * wave_dev, transcendentals=0
        ),
    )(res)


BATCH = 2


def members(target_ref):
    block_rows = WIDE * TGT_DEV
    per_x = PAIR * CS * TGT_DEV
    local = lax.broadcasted_iota(jnp.int32, (BATCH * block_rows, 1), 0)
    q = local % block_rows
    station = pl.program_id(0) * BATCH + local // block_rows
    wanted = (q // per_x) * (STATIONS * per_x) + station * per_x + q % per_x
    return jnp.where(target_ref[...] == wanted, 1.0, 0.0).astype(jnp.bfloat16)


def mix_sum_kernel(target_ref, rows_ref, sums_ref, terms):
    sources, row_count, lanes = rows_ref.shape
    block_rows = WIDE * TGT_DEV

    @pl.when(pl.program_id(0) == 0)
    def fill_terms():
        first = lax.broadcasted_iota(jnp.int32, (row_count, lanes), 1) < lanes // 2
        for source in range(sources):
            rows = slice(source * row_count, (source + 1) * row_count)
            values = rows_ref[source].astype(jnp.float32)
            product = jnp.where(first, values, values * half_swap(values))
            rounded = product.astype(jnp.bfloat16)
            terms[rows, 0:lanes] = rounded
            rest = product - rounded.astype(jnp.float32)
            terms[rows, lanes : 2 * lanes] = rest.astype(jnp.bfloat16)

    sums = jnp.dot(members(target_ref), terms[...], preferred_element_type=jnp.float32)
    total = sums[:, 0:lanes] + sums[:, lanes : 2 * lanes]
    for b in range(BATCH):
        sums_ref[b] = total[b * block_rows : (b + 1) * block_rows]


def mix_sum(targets, rows):
    sources, row_count, lanes = rows.shape
    block_rows = WIDE * TGT_DEV
    return pl.pallas_call(
        mix_sum_kernel,
        out_shape=jax.ShapeDtypeStruct((STATIONS, block_rows, lanes), jnp.float32),
        grid=(STATIONS // BATCH,),
        in_specs=[
            pl.BlockSpec((1, sources * row_count), lambda i: (0, 0)),
            pl.BlockSpec(rows.shape, lambda i: (0, 0, 0)),
        ],
        out_specs=pl.BlockSpec((BATCH, block_rows, lanes), lambda i: (i, 0, 0)),
        scratch_shapes=[pltpu.VMEM((sources * row_count, 2 * lanes), jnp.bfloat16)],
        compiler_params=pltpu.CompilerParams(vmem_limit_bytes=40 << 20),
        cost_estimate=pl.CostEstimate(
            flops=4 * STATIONS * block_rows * sources * row_count * lanes,
            bytes_accessed=2 * rows.size + 4 * STATIONS * block_rows * lanes,
            transcendentals=0,
        ),
    )(targets, rows)


STREAMS = 2


def res_sum_kernel(target_ref, mixed_ref, rows_ref, *refs):
    sums_refs, terms = refs[:STREAMS], refs[STREAMS]
    sources, folds, row_count, lanes = rows_ref.shape
    block_rows = WIDE * TGT_DEV

    @pl.when(pl.program_id(0) == 0)
    def fill_terms():
        first = lax.broadcasted_iota(jnp.int32, (row_count, lanes), 1) < lanes // 2

        def one_source(source, carry):
            rows = pl.ds(pl.multiple_of(source * row_count, row_count), row_count)
            values = mixed_ref[source].astype(jnp.float32)
            weight = jnp.where(first, values, half_swap(values))
            for fold in range(folds):
                product = weight * rows_ref[source, fold].astype(jnp.float32)
                terms[rows, fold * lanes : (fold + 1) * lanes] = product.astype(jnp.bfloat16)
            return carry

        lax.fori_loop(0, sources, one_source, 0)

    sums = jnp.dot(members(target_ref), terms[...], preferred_element_type=jnp.float32)
    each = folds // STREAMS
    for b in range(BATCH):
        for owner in range(WIDE):
            start = b * block_rows + owner * TGT_DEV
            block = sums[start : start + TGT_DEV].astype(jnp.bfloat16)
            for fold in range(folds):
                piece = block[:, fold * lanes : (fold + 1) * lanes]
                sums_refs[fold // each][b, owner, fold % each] = piece


def res_sums(targets, mixed, rows):
    sources, folds, row_count, lanes = rows.shape
    tail = (WIDE, folds // STREAMS, TGT_DEV, lanes)
    return pl.pallas_call(
        res_sum_kernel,
        out_shape=[jax.ShapeDtypeStruct((STATIONS,) + tail, jnp.bfloat16)] * STREAMS,
        grid=(STATIONS // BATCH,),
        in_specs=[
            pl.BlockSpec((1, sources * row_count), lambda i: (0, 0)),
            pl.BlockSpec(mixed.shape, lambda i: (0, 0, 0)),
            pl.BlockSpec(rows.shape, lambda i: (0, 0, 0, 0)),
        ],
        out_specs=[pl.BlockSpec((BATCH,) + tail, lambda i: (i, 0, 0, 0, 0))] * STREAMS,
        scratch_shapes=[pltpu.VMEM((sources * row_count, folds * lanes), jnp.bfloat16)],
        compiler_params=pltpu.CompilerParams(vmem_limit_bytes=48 << 20),
        cost_estimate=pl.CostEstimate(
            flops=2 * STATIONS * WIDE * TGT_DEV * sources * row_count * folds * lanes,
            bytes_accessed=2 * (rows.size + STATIONS * WIDE * TGT_DEV * folds * lanes),
            transcendentals=0,
        ),
    )(targets, mixed, rows)


def unfold(low, high, first):
    one = jnp.where(first, low, half_swap(high))
    two = jnp.where(first, half_swap(low), high)
    return one, two


def own_kernel(sums_ref, weight_ref, coadd_ref, both_ref):
    lanes = sums_ref.shape[-1]
    first = lax.broadcasted_iota(jnp.int32, (TGT_DEV, lanes), 1) < lanes // 2
    for tile in range(WIDE // 2):
        columns = slice(tile * lanes, (tile + 1) * lanes)
        weight, flux = unfold(sums_ref[2 * tile], sums_ref[2 * tile + 1], first)
        weight_ref[:, columns] = weight
        coadd_ref[:, columns] = flux / weight
        both_ref[0, :, columns] = weight.astype(jnp.bfloat16)
        both_ref[1, :, columns] = flux.astype(jnp.bfloat16)


def own_sums(sums):
    wave_dev = WIDE * sums.shape[-1] // 2
    whole = jax.ShapeDtypeStruct((TGT_DEV, wave_dev), jnp.float32)
    both = jax.ShapeDtypeStruct((2, TGT_DEV, wave_dev), jnp.bfloat16)
    return pl.pallas_call(own_kernel, out_shape=(whole, whole, both))(sums)


def finish_kernel(weight_ref, *refs):
    sums_refs, out_ref = refs[:STREAMS], refs[STREAMS]
    each, lanes = sums_refs[0].shape[1], sums_refs[0].shape[-1]
    first = lax.broadcasted_iota(jnp.int32, (TGT_DEV, lanes), 1) < lanes // 2
    for tile in range(WIDE // 2):
        columns = slice(tile * lanes, (tile + 1) * lanes)
        weight = weight_ref[:, columns]
        for fold in range(FOLDS):
            low = sums_refs[fold // each][2 * tile, fold % each].astype(jnp.float32)
            high = sums_refs[fold // each][2 * tile + 1, fold % each].astype(jnp.float32)
            one, two = unfold(low, high, first)
            out_ref[2 * fold, :, columns] = (one / weight).astype(jnp.bfloat16)
            if 2 * fold + 1 < NDIAG:
                out_ref[2 * fold + 1, :, columns] = (two / weight).astype(jnp.bfloat16)


def finish(weight, sums):
    out = jax.ShapeDtypeStruct((NDIAG,) + weight.shape, jnp.bfloat16)
    return pl.pallas_call(finish_kernel, out_shape=out)(weight, *sums)


def ring_start(parts, station):
    def part(offset):
        return lax.dynamic_index_in_dim(parts, (station + offset) % STATIONS, 0, keepdims=False)

    return part, part(STATIONS // 2), part(STATIONS // 2 + 1)


def ring_turn(state, s):
    half = STATIONS // 2
    part, up, down = state
    up = ring_step(up, 1)
    if s < half - 1:
        up = up + part(half - 1 - s)
        down = ring_step(down, -1)
        if s < half - 2:
            down = down + part(half + 2 + s)
    return part, up, down


def ring_end(state):
    part, up, down = state
    total = part(0).astype(jnp.float32) + up.astype(jnp.float32) + down.astype(jnp.float32)
    return total.astype(up.dtype)


def exchange(values, groups):
    return lax.all_to_all(
        values, "tgt", split_axis=0, concat_axis=0, axis_index_groups=groups, tiled=True
    )


def shards(
    exposure_flux,
    exposure_ivar,
    exposure_res,
    target_of_row,
    valid_of_row,
    rest_basis,
    redshift_shift,
):
    device = lax.axis_index("tgt")
    my_z = (device // CS) % ZS
    row_count, wave_dev = exposure_flux.shape
    masked = jnp.where(valid_of_row == 1, target_of_row, -1)
    station = my_z // PAIR
    targets = lax.dynamic_index_in_dim(
        masked.reshape(XS, STATIONS, PAIR * CS * row_count), station, 1, keepdims=False
    ).reshape(1, -1)

    mixed = exchange(mix_pair(exposure_ivar, exposure_flux), wide_groups)
    packed = mix_res(jnp.transpose(exposure_res, (1, 0, 2)))
    packed, mixed = lax.optimization_barrier((packed, mixed))
    rows = exchange(packed, wide_groups)
    turns = STATIONS // 2
    part, up, down = ring_start(mix_sum(targets, mixed), station)
    for s in range(turns - 1):
        part, up, down = ring_turn((part, up, down), s)
    rows, up, down = lax.optimization_barrier((rows, up, down))
    sums = ring_end(ring_turn((part, up, down), turns - 1))

    streams = [ring_start(parts, station) for parts in res_sums(targets, mixed, rows)]
    for s in range(turns):
        streams = [ring_turn(state, s) for state in streams]
    back = [exchange(ring_end(state), wide_groups) for state in streams]

    weight_sum, coadd_flux, both = own_sums(
        exchange(sums.reshape(WIDE, TGT_DEV, -1), wide_groups)
    )
    everything = lax.all_gather(both, "band", axis=2, tiled=True).astype(jnp.float32)
    band_index = lax.axis_index("band")
    shifts = lax.dynamic_slice_in_dim(redshift_shift, band_index * Z_DEV, Z_DEV)
    windows = basis_windows(rest_basis, shifts, 0, everything.shape[2])
    fit_gain = fit_from(*normal_terms(everything[0], everything[1], windows))

    coadd_res = jnp.transpose(finish(weight_sum, back), (1, 0, 2))
    return (coadd_flux, coadd_res, fit_gain)


def solution(mesh):
    in_specs = (P("tgt", "band"), P("tgt", "band"), P("tgt", None, "band"), P(), P(), P(), P())
    out_specs = (P("tgt", "band"), P("tgt", None, "band"), P("tgt", "band"))
    return jax.shard_map(shards, mesh=mesh, in_specs=in_specs, out_specs=out_specs, check_vma=False)
```

time: 206 us -> 274 us (1.33)
  starting transfers between devices: 66.6 us -> 119 us
  between operations: 14.5 us -> 1.33 us
  other arithmetic: 3.18 us -> 14.5 us
  local copies, waits for them, and re-layouts: 24.5 us -> 35.4 us
  Pallas kernels: 18.6 us -> 22.7 us
    ppermute x7 -> x21, starting transfers between devices: 29.1 us -> 73.2 us  [ring_step(): return lax.ppermute(values, 'tgt', pairs)]
    ppermute x7 -> x21, waiting for transfers between devices: 15.6 us -> 50.2 us  [ring_step(): return lax.ppermute(values, 'tgt', pairs)]
    reduce_scatter x1 -> x0, waiting for transfers between devices: 30.3 us -> none  [scatter_sum(): lax.psum_scatter(values, 'tgt', scatter_dimension=0, axis_index_groups=ri...]
    add x4 -> x10, other arithmetic: 0.75 us -> 9.99 us  [the longest x7 5.52 us: ring_turn(): up = up + part(half - 1 - s)]
    all_to_all x4 -> x5, starting transfers between devices: 37.5 us -> 46.1 us  [exchange(): lax.all_to_all(values, 'tgt', split_axis=0, concat_axis=0, axis_index_gro...]
    gather x24, local copies, waits for them, and re-layouts: 10.9 us -> 18.5 us
    pallas_call x2 -> x4, Pallas kernels: 13.3 us -> 17.4 us  [the longest x1 11 us: res_sums(): pl.pallas_call(res_sum_kernel, out_shape=[jax.ShapeDtypeStruct((STATIONS,...]
    convert_element_type x1 -> x2, other arithmetic: 0.09 us -> 3.58 us  [ring_end(): return total.astype(up.dtype)]
  transfers between devices with their start and end apart: 12 -> 26, of which waited for: 9 -> 6; matrix products, arithmetic and copies ran while one was open for 16% -> 20% of each run, Pallas kernels for 3% -> 7%
where the time goes in v4:
time: 274 us; the launch traced here: 273 us
  starting transfers between devices  119 us (43%)
  waiting for transfers between devices  58.7 us (21%)
  local copies, waits for them, and re-layouts  35.4 us (13%)
  Pallas kernels  22.7 us (8%)
  other arithmetic  14.5 us (5%)
  blocking collectives  10.9 us (4%)
  matrix products  9.64 us (4%)
    ppermute x21, starting transfers between devices, ring_step(): return lax.ppermute(values, 'tgt', pairs)  73.2 us
    ppermute x21, waiting for transfers between devices, ring_step(): return lax.ppermute(values, 'tgt', pairs)  50.2 us
    all_to_all x5, starting transfers between devices, exchange(): lax.all_to_all(values, 'tgt', split_axis=0, concat_axis=0, axis_index_gro...  46.1 us
    gather x24, local copies, waits for them, and re-layouts  18.5 us
    pallas_call x1, Pallas kernels, res_sums(): pl.pallas_call(res_sum_kernel, out_shape=[jax.ShapeDtypeStruct((STATIONS,...  11 us
    all_gather x1, blocking collectives, shards(): lax.all_gather(both, 'band', axis=2, tiled=True).astype(jnp.float32)  10.9 us
    all_to_all x5, waiting for transfers between devices, exchange(): lax.all_to_all(values, 'tgt', split_axis=0, concat_axis=0, axis_index_gro...  8.44 us
    gather x2, local copies, waits for them, and re-layouts, normal_terms(): products = windows[:, pair_first, :] * windows[:, pair_second, :]  7.95 us
  transfers between devices with their start and end apart: 26, of which 6 were waited for; matrix products, arithmetic and copies ran while one was open for 20% of the time, Pallas kernels for 7%

profile of v4, /device:TPU:1, one launch (start us, length us, event | category | flops | bytes accessed | tf_op | source)
XLA Modules:
  0.0 272.6 jit_solution(3339432486017563426)
XLA Ops:
  0.6 2.0 shard_map.131
  2.7 10.2 %all-to-all-start = ((bf16[16,128,128]{2,1,0:T(8,128)(2,1)}), bf16[16,128,128]{2,1,0:T(8,128)(2,1)S(1)}, u32[]{:S(2)}, u32[]{:S(2)}) async-start(bf16[16,128,128]{2,1,0:T(8,128)(2,1)} %shard_map.131), calls=%async_computation | async-start | bytes 1048576 | tf_op jit(solution)/shard_map/all_to_all | solution.py:344
  12.9 1.8 copy-done
  14.7 2.8 %shard_map.130 = bf16[16,6,128,128]{3,2,1,0:T(8,128)(2,1)} custom-call(bf16[11,128,1024]{2,1,0:T(8,128)(2,1)S(1)} %bitcast.92), custom_call_target="tpu_custom_call" | custom-call | bytes 6291456 | tf_op jit(solution)/shard_map/pallas_call | solution.py:146
  17.5 5.3 %all-to-all-done.rows_ref.mixed_ref = bf16[16,128,128]{2,1,0:T(8,128)(2,1)S(1)} async-done(((bf16[16,128,128]{2,1,0:T(8,128)(2,1)}), bf16[16,128,128]{2,1,0:T(8,128)(2,1)S(1)}, u32[]{:S(2)}, u32[]{:S(2)}) %all-to-all-start) | async-done | bytes 524320 | tf_op jit(solution)/shard_map/all_to_all | solution.py:344
  22.8 5.4 %all-to-all-start.1 = ((bf16[16,6,128,128]{3,2,1,0:T(8,128)(2,1)}), bf16[16,6,128,128]{3,2,1,0:T(8,128)(2,1)}, u32[]{:S(2)}, u32[]{:S(2)}) async-start(bf16[16,6,128,128]{3,2,1,0:T(8,128)(2,1)} %shard_map.130), calls=%async_computation.1 | async-start | bytes 6291456 | tf_op jit(solution)/shard_map/all_to_all | solution.py:344
  28.3 3.2 %shard_map.132 = f32[8,256,128]{2,1,0:T(8,128)S(1)} custom-call(s32[1,2048]{1,0:T(1,128)S(1)} %bitcast.93, bf16[16,128,128]{2,1,0:T(8,128)(2,1)S(1)} %all-to-all-done.rows_ref.mixed_ref), custom_call_target="tpu_custom_call" | custom-call | flops 2147483648 | bytes 1572864 | tf_op jit(solution)/shard_map/pallas_call | solution.py:196
  31.6 1.9 collective-permute-start
  33.5 7.5 %collective-permute-start.3 = (f32[256,128]{1,0:T(8,128)S(1)}, f32[256,128]{1,0:T(8,128)}, u32[]{:S(2)}, u32[]{:S(2)}) collective-permute-start(f32[256,128]{1,0:T(8,128)S(1)} %get-tuple-element.110), channel_id=1, source_target_pairs={{0,112},{4,116},{8,120},{12,124},{16,0},{20,4},{24,8},{28,12},{32,... | collective-permute-start | bytes 393224 | tf_op jit(solution)/shard_map/ppermute | solution.py:40
  41.1 38.2 %collective-permute-done = f32[256,128]{1,0:T(8,128)S(1)} collective-permute-done((f32[256,128]{1,0:T(8,128)S(1)}, f32[256,128]{1,0:T(8,128)S(1)}, u32[]{:S(2)}, u32[]{:S(2)}) %collective-permute-start) | collective-permute-done | bytes 131104 | tf_op jit(solution)/shard_map/ppermute | solution.py:40
  79.3 1.9 collective-permute-start.1
  81.4 6.5 %collective-permute-done.1 = f32[256,128]{1,0:T(8,128)} collective-permute-done((f32[256,128]{1,0:T(8,128)S(1)}, f32[256,128]{1,0:T(8,128)}, u32[]{:S(2)}, u32[]{:S(2)}) %collective-permute-start.1) | collective-permute-done | bytes 131104 | tf_op jit(solution)/shard_map/ppermute | solution.py:40
  87.9 1.0 bitcast_add_fusion.11
  88.9 2.0 collective-permute-start.4
  90.9 4.2 %collective-permute-start.2 = (f32[256,128]{1,0:T(8,128)S(1)}, f32[256,128]{1,0:T(8,128)}, u32[]{:S(2)}, u32[]{:S(2)}) collective-permute-start(f32[256,128]{1,0:T(8,128)S(1)} %get-tuple-element.109), channel_id=1, source_target_pairs={{0,16},{4,20},{8,24},{12,28},{16,32},{20,36},{24,40},{28,44},{32,4... | collective-permute-start | bytes 393224 | tf_op jit(solution)/shard_map/ppermute | solution.py:40
  95.1 18.7 %while.1 = (s32[]{:T(128)}, f32[10,4608]{1,0:T(8,128)}, s32[8,2]{0,1:T(2,128)S(1)}, f32[8,10,4096]{2,1,0:T(8,128)S(1)}, s32[]{:T(128)}) while((s32[]{:T(128)}, f32[10,4608]{1,0:T(8,128)}, s32[8,2]{0,1:T(2,128)S(1)}, f32[8,10,4096]{2,1,0:T(8,128)S(1)}, s32[]{:T(128)}) %tuple.94), condition=%wide.while_cond, body=%wide.while_body.sunk | while | flops 2 | bytes 426089 | solution.py:77
  95.7 1.7 bitcast_dynamic-update-slice_fusion.2
  98.0 1.7 bitcast_dynamic-update-slice_fusion.2
  100.4 1.7 bitcast_dynamic-update-slice_fusion.2
  102.7 1.7 bitcast_dynamic-update-slice_fusion.2
  105.1 1.7 bitcast_dynamic-update-slice_fusion.2
  107.4 1.7 bitcast_dynamic-update-slice_fusion.2
  109.7 1.7 bitcast_dynamic-update-slice_fusion.2
  112.1 1.7 bitcast_dynamic-update-slice_fusion.2
  113.9 1.8 bitcast_add_fusion.10
  115.7 3.2 %collective-permute-start.5 = (f32[256,128]{1,0:T(8,128)}, f32[256,128]{1,0:T(8,128)S(1)}, u32[]{:S(2)}, u32[]{:S(2)}) collective-permute-start(f32[256,128]{1,0:T(8,128)} %get-tuple-element.106), channel_id=1, source_target_pairs={{0,112},{4,116},{8,120},{12,124},{16,0},{20,4},{24,8},{28,12},{32,... | collective-permute-start | bytes 393224 | tf_op jit(solution)/shard_map/ppermute | solution.py:40
  119.8 4.0 %gather_fusion.1 = f32[55,8,4096]{2,1,0:T(8,128)} fusion(f32[8,10,4096]{2,0,1:T(8,128)S(1)} %copy.14, s32[1024]{0:T(1024)S(1)} %pad_clamp_fusion), kind=kCustom, calls=%fused_computation.1 | custom fusion | bytes 14418140 | tf_op jit(solution)/shard_map/gather | solution.py:83
  123.8 4.0 %gather_fusion = f32[55,8,4096]{2,1,0:T(8,128)} fusion(f32[8,10,4096]{2,0,1:T(8,128)S(1)} %copy.14, s32[1024]{0:T(1024)S(1)} %pad_clamp_fusion.1), kind=kCustom, calls=%fused_computation | custom fusion | bytes 14418140 | tf_op jit(solution)/shard_map/gather | solution.py:83
  127.8 2.9 %collective-permute-start.6 = (f32[256,128]{1,0:T(8,128)}, f32[256,128]{1,0:T(8,128)S(1)}, u32[]{:S(2)}, u32[]{:S(2)}) collective-permute-start(f32[256,128]{1,0:T(8,128)} %get-tuple-element.15), channel_id=1, source_target_pairs={{0,16},{4,20},{8,24},{12,28},{16,32},{20,36},{24,40},{28,44},{32,4... | collective-permute-start | bytes 393224 | tf_op jit(solution)/shard_map/ppermute | solution.py:40
  130.7 1.0 copy-done.3
  131.8 11.0 %shard_map.134 = (bf16[8,16,3,16,128]{4,3,2,1,0:T(8,128)(2,1)S(1)}, bf16[8,16,3,16,128]{4,3,2,1,0:T(8,128)(2,1)S(1)}) custom-call(s32[1,2048]{1,0:T(1,128)S(1)} %bitcast.94, bf16[16,128,128]{2,1,0:T(8,128)(2,1)S(1)} %copy-done.3, bf16[16,6,128,128]{3,2,1,0:T(8,128)(2,1)} %all-to-all-done.1.rows_ref), custom_call_target="tpu_custom_call" | custom-call | flops 6442450944 | bytes 6291456 | tf_op jit(solution)/shard_map/pallas_call | solution.py:252
  143.6 3.3 %collective-permute-start.7 = (bf16[16,3,16,128]{3,2,1,0:T(8,128)(2,1)}, bf16[16,3,16,128]{3,2,1,0:T(8,128)(2,1)}, u32[]{:S(2)}, u32[]{:S(2)}) collective-permute-start(bf16[16,3,16,128]{3,2,1,0:T(8,128)(2,1)} %get-tuple-element.104), channel_id=1, source_target_pairs={{0,16},{4,20},{8,24},{12,28},{16,32},{20,36},{24,40},{28,44},{32,4... | collective-permute-start | bytes 589832 | tf_op jit(solution)/shard_map/ppermute | solution.py:40
  146.9 4.1 %collective-permute-start.11 = (bf16[16,3,16,128]{3,2,1,0:T(8,128)(2,1)}, bf16[16,3,16,128]{3,2,1,0:T(8,128)(2,1)}, u32[]{:S(2)}, u32[]{:S(2)}) collective-permute-start(bf16[16,3,16,128]{3,2,1,0:T(8,128)(2,1)} %get-tuple-element.105), channel_id=1, source_target_pairs={{0,112},{4,116},{8,120},{12,124},{16,0},{20,4},{24,8},{28,12},{32,... | collective-permute-start | bytes 589832 | tf_op jit(solution)/shard_map/ppermute | solution.py:40
  151.7 2.1 collective-permute-start.14
  153.8 5.3 %collective-permute-start.18 = (bf16[16,3,16,128]{3,2,1,0:T(8,128)(2,1)S(1)}, bf16[16,3,16,128]{3,2,1,0:T(8,128)(2,1)}, u32[]{:S(2)}, u32[]{:S(2)}) collective-permute-start(bf16[16,3,16,128]{3,2,1,0:T(8,128)(2,1)S(1)} %get-tuple-element.99), channel_id=1, source_target_pairs={{0,112},{4,116},{8,120},{12,124},{16,0},{20,4},{24,8},{28,12},{32,... | collective-permute-start | bytes 589832 | tf_op jit(solution)/shard_map/ppermute | solution.py:40
  159.1 1.7 fusion.7
  160.8 10.3 %all-to-all-start.2 = ((f32[16,16,128]{2,1,0:T(8,128)}), f32[16,16,128]{2,1,0:T(8,128)S(1)}, u32[]{:S(2)}, u32[]{:S(2)}) async-start(f32[16,16,128]{2,1,0:T(8,128)} %bitcast.10), calls=%async_computation.2 | async-start | bytes 262144 | tf_op jit(solution)/shard_map/all_to_all | solution.py:344
  171.0 1.0 bitcast_add_fusion.9
  172.0 1.9 collective-permute-start.8
  173.9 1.0 bitcast_add_fusion.4
  174.9 2.6 collective-permute-start.15
  177.5 5.1 %collective-permute-done.8 = bf16[16,3,16,128]{3,2,1,0:T(8,128)(2,1)S(1)} collective-permute-done((bf16[16,3,16,128]{3,2,1,0:T(8,128)(2,1)S(1)}, bf16[16,3,16,128]{3,2,1,0:T(8,128)(2,1)S(1)}, u32[]{:S(2)}, u32[]{:S(2)}) %collective-permute-start.8) | collective-permute-done | bytes 196640 | tf_op jit(solution)/shard_map/ppermute | solution.py:40
  182.6 1.0 bitcast_add_fusion.8
  183.6 1.9 collective-permute-start.9
  185.5 5.5 %collective-permute-start.12 = (bf16[16,3,16,128]{3,2,1,0:T(8,128)(2,1)S(1)}, bf16[16,3,16,128]{3,2,1,0:T(8,128)(2,1)S(1)}, u32[]{:S(2)}, u32[]{:S(2)}) collective-permute-start(bf16[16,3,16,128]{3,2,1,0:T(8,128)(2,1)S(1)} %get-tuple-element.103), channel_id=1, source_target_pairs={{0,112},{4,116},{8,120},{12,124},{16,0},{20,4},{24,8},{28,12},{32,... | collective-permute-start | bytes 589832 | tf_op jit(solution)/shard_map/ppermute | solution.py:40
  191.4 1.0 bitcast_add_fusion.3
  192.4 1.9 collective-permute-start.16
  194.3 5.5 %collective-permute-start.19 = (bf16[16,3,16,128]{3,2,1,0:T(8,128)(2,1)S(1)}, bf16[16,3,16,128]{3,2,1,0:T(8,128)(2,1)S(1)}, u32[]{:S(2)}, u32[]{:S(2)}) collective-permute-start(bf16[16,3,16,128]{3,2,1,0:T(8,128)(2,1)S(1)} %get-tuple-element.97), channel_id=1, source_target_pairs={{0,112},{4,116},{8,120},{12,124},{16,0},{20,4},{24,8},{28,12},{32,... | collective-permute-start | bytes 589832 | tf_op jit(solution)/shard_map/ppermute | solution.py:40
  200.6 1.9 collective-permute-start.10
  202.5 5.6 %collective-permute-start.13 = (bf16[16,3,16,128]{3,2,1,0:T(8,128)(2,1)}, bf16[16,3,16,128]{3,2,1,0:T(8,128)(2,1)}, u32[]{:S(2)}, u32[]{:S(2)}) collective-permute-start(bf16[16,3,16,128]{3,2,1,0:T(8,128)(2,1)} %get-tuple-element.101), channel_id=1, source_target_pairs={{0,112},{4,116},{8,120},{12,124},{16,0},{20,4},{24,8},{28,12},{32,... | collective-permute-start | bytes 589832 | tf_op jit(solution)/shard_map/ppermute | solution.py:40
  208.1 0.8 bitcast_add_fusion.2
  209.0 3.2 %collective-permute-start.17 = (bf16[16,3,16,128]{3,2,1,0:T(8,128)(2,1)}, bf16[16,3,16,128]{3,2,1,0:T(8,128)(2,1)}, u32[]{:S(2)}, u32[]{:S(2)}) collective-permute-start(bf16[16,3,16,128]{3,2,1,0:T(8,128)(2,1)} %get-tuple-element.94), channel_id=1, source_target_pairs={{0,16},{4,20},{8,24},{12,28},{16,32},{20,36},{24,40},{28,44},{32,4... | collective-permute-start | bytes 589832 | tf_op jit(solution)/shard_map/ppermute | solution.py:40
  212.2 4.7 %collective-permute-start.20 = (bf16[16,3,16,128]{3,2,1,0:T(8,128)(2,1)}, bf16[16,3,16,128]{3,2,1,0:T(8,128)(2,1)}, u32[]{:S(2)}, u32[]{:S(2)}) collective-permute-start(bf16[16,3,16,128]{3,2,1,0:T(8,128)(2,1)} %get-tuple-element.95), channel_id=1, source_target_pairs={{0,112},{4,116},{8,120},{12,124},{16,0},{20,4},{24,8},{28,12},{32,... | collective-permute-start | bytes 589832 | tf_op jit(solution)/shard_map/ppermute | solution.py:40
  217.5 1.6 shard_map.133
  219.2 10.9 %all_gather.3 = bf16[2,16,4096]{2,1,0:T(8,128)(2,1)S(1)} all-gather(bf16[2,16,1024]{2,1,0:T(8,128)(2,1)} %get-tuple-element.22), channel_id=1, replica_groups=mesh['tgt'=128,'band'=4] {'band'}, dimensions={2}, use_global_device_ids=true | all-gather | bytes 327680 | tf_op jit(solution)/shard_map/all_gather | solution.py:386
  230.1 1.8 fusion.6
  231.9 14.5 %all-to-all-start.3 = ((bf16[16,3,16,128]{3,2,1,0:T(8,128)(2,1)}), bf16[16,3,16,128]{3,2,1,0:T(8,128)(2,1)S(1)}, u32[]{:S(2)}, u32[]{:S(2)}) async-start(bf16[16,3,16,128]{3,2,1,0:T(8,128)(2,1)} %fusion.6), calls=%async_computation.3 | async-start | bytes 393216 | tf_op jit(solution)/shard_map/all_to_all | solution.py:344
  246.3 7.0 %fusion = f32[8,55,16]{2,0,1:T(8,128)S(1)} fusion(f32[55,8,4096]{2,1,0:T(8,128)} %gather_fusion, f32[55,8,4096]{2,1,0:T(8,128)} %gather_fusion.1, bf16[2,16,4096]{2,1,0:T(8,128)(2,1)S(1)} %all_gather.3), kind=kOutput, calls=%fused_computation.4 | convolution fusion | flops 347832320 | bytes 14577152 | tf_op jit(solution)/shard_map/ti,zpi->ztp/dot_general | solution.py:84
  255.7 1.8 fusion.4
  257.5 5.7 %all-to-all-start.4 = ((bf16[16,3,16,128]{3,2,1,0:T(8,128)(2,1)}), bf16[16,3,16,128]{3,2,1,0:T(8,128)(2,1)S(1)}, u32[]{:S(2)}, u32[]{:S(2)}) async-start(bf16[16,3,16,128]{3,2,1,0:T(8,128)(2,1)} %fusion.4), calls=%async_computation.4 | async-start | bytes 393216 | tf_op jit(solution)/shard_map/all_to_all | solution.py:344
  263.2 2.6 convolution_bitcast_fusion
  265.9 0.9 add_bitcast_fusion
  266.8 3.1 %all-to-all-done.4.refs_1_ = bf16[16,3,16,128]{3,2,1,0:T(8,128)(2,1)S(1)} async-done(((bf16[16,3,16,128]{3,2,1,0:T(8,128)(2,1)}), bf16[16,3,16,128]{3,2,1,0:T(8,128)(2,1)S(1)}, u32[]{:S(2)}, u32[]{:S(2)}) %all-to-all-start.4) | async-done | bytes 196640 | tf_op jit(solution)/shard_map/all_to_all | solution.py:344
  270.6 2.0 shard_map.135
  (82 shorter events, 12.1 us)
Async XLA Ops:
  2.7 20.1 %all-to-all-start = ((bf16[16,128,128]{2,1,0:T(8,128)(2,1)}), bf16[16,128,128]{2,1,0:T(8,128)(2,1)S(1)}, u32[]{:S(2)}, u32[]{:S(2)}) async-start(bf16[16,128,128]{2,1,0:T(8,128)(2,1)} %shard_map.131), calls=%async_computation | async-start | bytes 1048576 | tf_op jit(solution)/shard_map/all_to_all | solution.py:344
  12.9 1.8 copy-start
  17.5 10.7 %copy-start.9 = (s32[16384]{0:T(1024)S(1)}, s32[16384]{0:T(1024)}, u32[]{:S(2)}) copy-start(s32[16384]{0:T(1024)} %param.14) | copy-start | bytes 196612
  17.5 10.7 %copy-start.10 = (s32[16384]{0:T(1024)S(1)}, s32[16384]{0:T(1024)}, u32[]{:S(2)}) copy-start(s32[16384]{0:T(1024)} %param.15) | copy-start | bytes 196612
  22.8 5.5 %copy-start.2 = (bf16[16,128,128]{2,1,0:T(8,128)(2,1)}, bf16[16,128,128]{2,1,0:T(8,128)(2,1)S(1)}, u32[]{:S(2)}) copy-start(bf16[16,128,128]{2,1,0:T(8,128)(2,1)S(1)} %all-to-all-done.rows_ref.mixed_ref) | copy-start | bytes 1572868
  22.8 105.0 %all-to-all-start.1 = ((bf16[16,6,128,128]{3,2,1,0:T(8,128)(2,1)}), bf16[16,6,128,128]{3,2,1,0:T(8,128)(2,1)}, u32[]{:S(2)}, u32[]{:S(2)}) async-start(bf16[16,6,128,128]{3,2,1,0:T(8,128)(2,1)} %shard_map.130), calls=%async_computation.1 | async-start | bytes 6291456 | tf_op jit(solution)/shard_map/all_to_all | solution.py:344
  28.3 53.0 %copy-start.13 = (s32[32]{0:T(128)S(1)}, s32[32]{0:T(128)}, u32[]{:S(2)}) copy-start(s32[32]{0:T(128)} %param.17) | copy-start | bytes 388
  31.5 82.4 %copy-start.1 = (f32[8,256,128]{2,1,0:T(8,128)}, f32[8,256,128]{2,1,0:T(8,128)S(1)}, u32[]{:S(2)}) copy-start(f32[8,256,128]{2,1,0:T(8,128)S(1)} %shard_map.132) | copy-start | bytes 3145732
  31.6 47.7 %collective-permute-start = (f32[256,128]{1,0:T(8,128)S(1)}, f32[256,128]{1,0:T(8,128)S(1)}, u32[]{:S(2)}, u32[]{:S(2)}) collective-permute-start(f32[256,128]{1,0:T(8,128)S(1)} %get-tuple-element.111), channel_id=1, source_target_pairs={{0,16},{4,20},{8,24},{12,28},{16,32},{20,36},{24,40},{28,44},{32,4... | collective-permute-start | bytes 393224 | tf_op jit(solution)/shard_map/ppermute | solution.py:40
  33.5 47.8 %collective-permute-start.3 = (f32[256,128]{1,0:T(8,128)S(1)}, f32[256,128]{1,0:T(8,128)}, u32[]{:S(2)}, u32[]{:S(2)}) collective-permute-start(f32[256,128]{1,0:T(8,128)S(1)} %get-tuple-element.110), channel_id=1, source_target_pairs={{0,112},{4,116},{8,120},{12,124},{16,0},{20,4},{24,8},{28,12},{32,... | collective-permute-start | bytes 393224 | tf_op jit(solution)/shard_map/ppermute | solution.py:40
  79.3 8.6 %collective-permute-start.1 = (f32[256,128]{1,0:T(8,128)S(1)}, f32[256,128]{1,0:T(8,128)}, u32[]{:S(2)}, u32[]{:S(2)}) collective-permute-start(f32[256,128]{1,0:T(8,128)S(1)} %bitcast_add_fusion.14), channel_id=1, source_target_pairs={{0,16},{4,20},{8,24},{12,28},{16,32},{20,36},{24,40},{28,44},{32,4... | collective-permute-start | bytes 393224 | tf_op jit(solution)/shard_map/ppermute | solution.py:40
  81.4 37.6 %copy-start.12 = (s32[55]{0:T(128)S(1)}, s32[55]{0:T(128)}, u32[]{:S(2)}) copy-start(s32[55]{0:T(128)} %constant.221) | copy-start | bytes 664
  88.9 25.0 %collective-permute-start.4 = (f32[256,128]{1,0:T(8,128)S(1)}, f32[256,128]{1,0:T(8,128)S(1)}, u32[]{:S(2)}, u32[]{:S(2)}) collective-permute-start(f32[256,128]{1,0:T(8,128)S(1)} %get-tuple-element.108), channel_id=1, source_target_pairs={{0,112},{4,116},{8,120},{12,124},{16,0},{20,4},{24,8},{28,12},{32,... | collective-permute-start | bytes 393224 | tf_op jit(solution)/shard_map/ppermute | solution.py:40
  90.9 23.0 %collective-permute-start.2 = (f32[256,128]{1,0:T(8,128)S(1)}, f32[256,128]{1,0:T(8,128)}, u32[]{:S(2)}, u32[]{:S(2)}) collective-permute-start(f32[256,128]{1,0:T(8,128)S(1)} %get-tuple-element.109), channel_id=1, source_target_pairs={{0,16},{4,20},{8,24},{12,28},{16,32},{20,36},{24,40},{28,44},{32,4... | collective-permute-start | bytes 393224 | tf_op jit(solution)/shard_map/ppermute | solution.py:40
  113.8 6.0 %copy-start.4 = (f32[8,10,4096]{2,1,0:T(8,128)}, f32[8,10,4096]{2,1,0:T(8,128)S(1)}, u32[]{:S(2)}) copy-start(f32[8,10,4096]{2,1,0:T(8,128)S(1)} %get-tuple-element.30) | copy-start | bytes 3932164
  115.7 12.0 %collective-permute-start.5 = (f32[256,128]{1,0:T(8,128)}, f32[256,128]{1,0:T(8,128)S(1)}, u32[]{:S(2)}, u32[]{:S(2)}) collective-permute-start(f32[256,128]{1,0:T(8,128)} %get-tuple-element.106), channel_id=1, source_target_pairs={{0,112},{4,116},{8,120},{12,124},{16,0},{20,4},{24,8},{28,12},{32,... | collective-permute-start | bytes 393224 | tf_op jit(solution)/shard_map/ppermute | solution.py:40
  119.8 4.0 %copy-start.11 = (s32[55]{0:T(128)S(1)}, s32[55]{0:T(128)}, u32[]{:S(2)}) copy-start(s32[55]{0:T(128)} %constant.220) | copy-start | bytes 664
  127.8 15.0 %copy-start.8 = (f32[256,128]{1,0:T(8,128)}, f32[256,128]{1,0:T(8,128)S(1)}, u32[]{:S(2)}) copy-start(f32[256,128]{1,0:T(8,128)S(1)} %collective-permute-done.5) | copy-start | bytes 393220
  127.8 31.3 %collective-permute-start.6 = (f32[256,128]{1,0:T(8,128)}, f32[256,128]{1,0:T(8,128)S(1)}, u32[]{:S(2)}, u32[]{:S(2)}) collective-permute-start(f32[256,128]{1,0:T(8,128)} %get-tuple-element.15), channel_id=1, source_target_pairs={{0,16},{4,20},{8,24},{12,28},{16,32},{20,36},{24,40},{28,44},{32,4... | collective-permute-start | bytes 393224 | tf_op jit(solution)/shard_map/ppermute | solution.py:40
  130.7 1.0 copy-start.3
  143.6 27.4 %collective-permute-start.7 = (bf16[16,3,16,128]{3,2,1,0:T(8,128)(2,1)}, bf16[16,3,16,128]{3,2,1,0:T(8,128)(2,1)}, u32[]{:S(2)}, u32[]{:S(2)}) collective-permute-start(bf16[16,3,16,128]{3,2,1,0:T(8,128)(2,1)} %get-tuple-element.104), channel_id=1, source_target_pairs={{0,16},{4,20},{8,24},{12,28},{16,32},{20,36},{24,40},{28,44},{32,4... | collective-permute-start | bytes 589832 | tf_op jit(solution)/shard_map/ppermute | solution.py:40
  146.9 30.6 %collective-permute-start.11 = (bf16[16,3,16,128]{3,2,1,0:T(8,128)(2,1)}, bf16[16,3,16,128]{3,2,1,0:T(8,128)(2,1)}, u32[]{:S(2)}, u32[]{:S(2)}) collective-permute-start(bf16[16,3,16,128]{3,2,1,0:T(8,128)(2,1)} %get-tuple-element.105), channel_id=1, source_target_pairs={{0,112},{4,116},{8,120},{12,124},{16,0},{20,4},{24,8},{28,12},{32,... | collective-permute-start | bytes 589832 | tf_op jit(solution)/shard_map/ppermute | solution.py:40
  151.7 22.2 %collective-permute-start.14 = (bf16[16,3,16,128]{3,2,1,0:T(8,128)(2,1)}, bf16[16,3,16,128]{3,2,1,0:T(8,128)(2,1)}, u32[]{:S(2)}, u32[]{:S(2)}) collective-permute-start(bf16[16,3,16,128]{3,2,1,0:T(8,128)(2,1)} %get-tuple-element.98), channel_id=1, source_target_pairs={{0,16},{4,20},{8,24},{12,28},{16,32},{20,36},{24,40},{28,44},{32,4... | collective-permute-start | bytes 589832 | tf_op jit(solution)/shard_map/ppermute | solution.py:40
  153.8 37.2 %collective-permute-start.18 = (bf16[16,3,16,128]{3,2,1,0:T(8,128)(2,1)S(1)}, bf16[16,3,16,128]{3,2,1,0:T(8,128)(2,1)}, u32[]{:S(2)}, u32[]{:S(2)}) collective-permute-start(bf16[16,3,16,128]{3,2,1,0:T(8,128)(2,1)S(1)} %get-tuple-element.99), channel_id=1, source_target_pairs={{0,112},{4,116},{8,120},{12,124},{16,0},{20,4},{24,8},{28,12},{32,... | collective-permute-start | bytes 589832 | tf_op jit(solution)/shard_map/ppermute | solution.py:40
  160.8 56.1 %all-to-all-start.2 = ((f32[16,16,128]{2,1,0:T(8,128)}), f32[16,16,128]{2,1,0:T(8,128)S(1)}, u32[]{:S(2)}, u32[]{:S(2)}) async-start(f32[16,16,128]{2,1,0:T(8,128)} %bitcast.10), calls=%async_computation.2 | async-start | bytes 262144 | tf_op jit(solution)/shard_map/all_to_all | solution.py:344
  172.0 10.6 %collective-permute-start.8 = (bf16[16,3,16,128]{3,2,1,0:T(8,128)(2,1)S(1)}, bf16[16,3,16,128]{3,2,1,0:T(8,128)(2,1)S(1)}, u32[]{:S(2)}, u32[]{:S(2)}) collective-permute-start(bf16[16,3,16,128]{3,2,1,0:T(8,128)(2,1)S(1)} %bitcast_add_fusion.9), channel_id=1, source_target_pairs={{0,16},{4,20},{8,24},{12,28},{16,32},{20,36},{24,40},{28,44},{32,4... | collective-permute-start | bytes 589832 | tf_op jit(solution)/shard_map/ppermute | solution.py:40
  174.9 16.5 %collective-permute-start.15 = (bf16[16,3,16,128]{3,2,1,0:T(8,128)(2,1)S(1)}, bf16[16,3,16,128]{3,2,1,0:T(8,128)(2,1)S(1)}, u32[]{:S(2)}, u32[]{:S(2)}) collective-permute-start(bf16[16,3,16,128]{3,2,1,0:T(8,128)(2,1)S(1)} %bitcast_add_fusion.4), channel_id=1, source_target_pairs={{0,16},{4,20},{8,24},{12,28},{16,32},{20,36},{24,40},{28,44},{32,4... | collective-permute-start | bytes 589832 | tf_op jit(solution)/shard_map/ppermute | solution.py:40
  183.6 16.2 %collective-permute-start.9 = (bf16[16,3,16,128]{3,2,1,0:T(8,128)(2,1)S(1)}, bf16[16,3,16,128]{3,2,1,0:T(8,128)(2,1)S(1)}, u32[]{:S(2)}, u32[]{:S(2)}) collective-permute-start(bf16[16,3,16,128]{3,2,1,0:T(8,128)(2,1)S(1)} %get-tuple-element.102), channel_id=1, source_target_pairs={{0,16},{4,20},{8,24},{12,28},{16,32},{20,36},{24,40},{28,44},{32,4... | collective-permute-start | bytes 589832 | tf_op jit(solution)/shard_map/ppermute | solution.py:40
  185.5 14.3 %collective-permute-start.12 = (bf16[16,3,16,128]{3,2,1,0:T(8,128)(2,1)S(1)}, bf16[16,3,16,128]{3,2,1,0:T(8,128)(2,1)S(1)}, u32[]{:S(2)}, u32[]{:S(2)}) collective-permute-start(bf16[16,3,16,128]{3,2,1,0:T(8,128)(2,1)S(1)} %get-tuple-element.103), channel_id=1, source_target_pairs={{0,112},{4,116},{8,120},{12,124},{16,0},{20,4},{24,8},{28,12},{32,... | collective-permute-start | bytes 589832 | tf_op jit(solution)/shard_map/ppermute | solution.py:40
  192.4 15.7 %collective-permute-start.16 = (bf16[16,3,16,128]{3,2,1,0:T(8,128)(2,1)S(1)}, bf16[16,3,16,128]{3,2,1,0:T(8,128)(2,1)S(1)}, u32[]{:S(2)}, u32[]{:S(2)}) collective-permute-start(bf16[16,3,16,128]{3,2,1,0:T(8,128)(2,1)S(1)} %get-tuple-element.96), channel_id=1, source_target_pairs={{0,16},{4,20},{8,24},{12,28},{16,32},{20,36},{24,40},{28,44},{32,4... | collective-permute-start | bytes 589832 | tf_op jit(solution)/shard_map/ppermute | solution.py:40
  194.3 13.8 %collective-permute-start.19 = (bf16[16,3,16,128]{3,2,1,0:T(8,128)(2,1)S(1)}, bf16[16,3,16,128]{3,2,1,0:T(8,128)(2,1)S(1)}, u32[]{:S(2)}, u32[]{:S(2)}) collective-permute-start(bf16[16,3,16,128]{3,2,1,0:T(8,128)(2,1)S(1)} %get-tuple-element.97), channel_id=1, source_target_pairs={{0,112},{4,116},{8,120},{12,124},{16,0},{20,4},{24,8},{28,12},{32,... | collective-permute-start | bytes 589832 | tf_op jit(solution)/shard_map/ppermute | solution.py:40
  200.6 29.5 %collective-permute-start.10 = (bf16[16,3,16,128]{3,2,1,0:T(8,128)(2,1)}, bf16[16,3,16,128]{3,2,1,0:T(8,128)(2,1)}, u32[]{:S(2)}, u32[]{:S(2)}) collective-permute-start(bf16[16,3,16,128]{3,2,1,0:T(8,128)(2,1)} %get-tuple-element.100), channel_id=1, source_target_pairs={{0,16},{4,20},{8,24},{12,28},{16,32},{20,36},{24,40},{28,44},{32,4... | collective-permute-start | bytes 589832 | tf_op jit(solution)/shard_map/ppermute | solution.py:40
  202.5 27.5 %collective-permute-start.13 = (bf16[16,3,16,128]{3,2,1,0:T(8,128)(2,1)}, bf16[16,3,16,128]{3,2,1,0:T(8,128)(2,1)}, u32[]{:S(2)}, u32[]{:S(2)}) collective-permute-start(bf16[16,3,16,128]{3,2,1,0:T(8,128)(2,1)} %get-tuple-element.101), channel_id=1, source_target_pairs={{0,112},{4,116},{8,120},{12,124},{16,0},{20,4},{24,8},{28,12},{32,... | collective-permute-start | bytes 589832 | tf_op jit(solution)/shard_map/ppermute | solution.py:40
  209.0 46.7 %collective-permute-start.17 = (bf16[16,3,16,128]{3,2,1,0:T(8,128)(2,1)}, bf16[16,3,16,128]{3,2,1,0:T(8,128)(2,1)}, u32[]{:S(2)}, u32[]{:S(2)}) collective-permute-start(bf16[16,3,16,128]{3,2,1,0:T(8,128)(2,1)} %get-tuple-element.94), channel_id=1, source_target_pairs={{0,16},{4,20},{8,24},{12,28},{16,32},{20,36},{24,40},{28,44},{32,4... | collective-permute-start | bytes 589832 | tf_op jit(solution)/shard_map/ppermute | solution.py:40
  212.2 43.5 %collective-permute-start.20 = (bf16[16,3,16,128]{3,2,1,0:T(8,128)(2,1)}, bf16[16,3,16,128]{3,2,1,0:T(8,128)(2,1)}, u32[]{:S(2)}, u32[]{:S(2)}) collective-permute-start(bf16[16,3,16,128]{3,2,1,0:T(8,128)(2,1)} %get-tuple-element.95), channel_id=1, source_target_pairs={{0,112},{4,116},{8,120},{12,124},{16,0},{20,4},{24,8},{28,12},{32,... | collective-permute-start | bytes 589832 | tf_op jit(solution)/shard_map/ppermute | solution.py:40
  216.9 0.6 copy-start.7
  231.9 25.6 %all-to-all-start.3 = ((bf16[16,3,16,128]{3,2,1,0:T(8,128)(2,1)}), bf16[16,3,16,128]{3,2,1,0:T(8,128)(2,1)S(1)}, u32[]{:S(2)}, u32[]{:S(2)}) async-start(bf16[16,3,16,128]{3,2,1,0:T(8,128)(2,1)} %fusion.6), calls=%async_computation.3 | async-start | bytes 393216 | tf_op jit(solution)/shard_map/all_to_all | solution.py:344
  257.5 12.4 %copy-start.5 = (bf16[16,3,16,128]{3,2,1,0:T(8,128)(2,1)}, bf16[16,3,16,128]{3,2,1,0:T(8,128)(2,1)S(1)}, u32[]{:S(2)}) copy-start(bf16[16,3,16,128]{3,2,1,0:T(8,128)(2,1)S(1)} %all-to-all-done.3.refs_0_) | copy-start | bytes 589828
  257.5 12.4 %all-to-all-start.4 = ((bf16[16,3,16,128]{3,2,1,0:T(8,128)(2,1)}), bf16[16,3,16,128]{3,2,1,0:T(8,128)(2,1)S(1)}, u32[]{:S(2)}, u32[]{:S(2)}) async-start(bf16[16,3,16,128]{3,2,1,0:T(8,128)(2,1)} %fusion.4), calls=%async_computation.4 | async-start | bytes 393216 | tf_op jit(solution)/shard_map/all_to_all | solution.py:344
  269.9 0.7 copy-start.6

commit v5 on v3

--- a/solution.py
+++ b/solution.py
@@ -255,20 +255,23 @@
     )(targets, rows)
 
 
-def ring_sum(parts, station):
+def ring_start(parts, station):
     def part(offset):
         return lax.dynamic_index_in_dim(parts, (station + offset) % STATIONS, 0, keepdims=False)
 
+    return part, part(STATIONS // 2), part(STATIONS // 2 + 1)
+
+
+def ring_turn(state, s):
     half = STATIONS // 2
-    up, down = part(half), part(half + 1)
-    for s in range(half):
-        up = ring_step(up, 1)
-        if s < half - 1:
-            up = up + part(half - 1 - s)
-            down = ring_step(down, -1)
-            if s < half - 2:
-                down = down + part(half + 2 + s)
-    return part(0) + up + down
+    part, up, down = state
+    up = ring_step(up, 1)
+    if s < half - 1:
+        up = up + part(half - 1 - s)
+        down = ring_step(down, -1)
+        if s < half - 2:
+            down = down + part(half + 2 + s)
+    return part, up, down
 
 
 def exchange(values, groups):
@@ -307,8 +310,14 @@
     packed = split_lanes(exposure_ivar, jnp.transpose(exposure_res, (1, 0, 2)))
     packed, mixed = lax.optimization_barrier((packed, mixed))
     rows = exchange(packed, plane_groups)
-    sums = ring_sum(mix_sum(wide_targets, mixed), my_z // PAIR)
-    rows, sums = lax.optimization_barrier((rows, sums))
+    turns = STATIONS // 2
+    part, up, down = ring_start(mix_sum(wide_targets, mixed), my_z // PAIR)
+    for s in range(turns - 1):
+        part, up, down = ring_turn((part, up, down), s)
+        up, down = lax.optimization_barrier((up, down))
+    rows, up, down = lax.optimization_barrier((rows, up, down))
+    part, up, down = ring_turn((part, up, down), turns - 1)
+    sums = part(0) + up + down
     res_sum = scatter_sum(coadd_res_rows(targets, rows))
 
     own = exchange(sums.reshape(WIDE, TGT_DEV, -1), wide_groups)

time: 206 us -> 199 us (0.966)
  waiting for transfers between devices: 56.6 us -> 37.7 us
  local copies, waits for them, and re-layouts: 24.5 us -> 31.6 us
  starting transfers between devices: 66.6 us -> 72.6 us
    reduce_scatter x1, waiting for transfers between devices: 30.3 us -> 12.4 us  [scatter_sum(): lax.psum_scatter(values, 'tgt', scatter_dimension=0, axis_index_groups=ri...]
    gather x24, local copies, waits for them, and re-layouts: 10.9 us -> 18.6 us
    all_to_all x4, starting transfers between devices: 37.5 us -> 43.5 us  [exchange(): lax.all_to_all(values, 'tgt', split_axis=0, concat_axis=0, axis_index_gro...]
  transfers between devices with their start and end apart: 12 -> 12, of which waited for: 9 -> 10; matrix products, arithmetic and copies ran while one was open for 16% -> 20% of each run, Pallas kernels for 3% -> 3%
where the time goes in v5:
time: 199 us; the launch traced here: 198 us
  starting transfers between devices  72.6 us (36%)
  waiting for transfers between devices  37.7 us (19%)
  local copies, waits for them, and re-layouts  31.6 us (16%)
  Pallas kernels  18.6 us (9%)
  between operations  14.5 us (7%)
  blocking collectives  11.1 us (6%)
  matrix products  8.25 us (4%)
  other arithmetic  3.18 us (2%)
    all_to_all x4, starting transfers between devices, exchange(): lax.all_to_all(values, 'tgt', split_axis=0, concat_axis=0, axis_index_gro...  43.5 us
    ppermute x7, starting transfers between devices, ring_step(): return lax.ppermute(values, 'tgt', pairs)  29.1 us
    gather x24, local copies, waits for them, and re-layouts  18.6 us
    ppermute x7, waiting for transfers between devices, ring_step(): return lax.ppermute(values, 'tgt', pairs)  14.5 us
    reduce_scatter x1, waiting for transfers between devices, scatter_sum(): lax.psum_scatter(values, 'tgt', scatter_dimension=0, axis_index_groups=ri...  12.4 us
    all_gather x1, blocking collectives, shards(): lax.all_gather(own.astype(jnp.bfloat16), 'band', axis=2, tiled=True)  11.1 us
    pallas_call x1, Pallas kernels, coadd_res_rows(): pl.pallas_call(res_kernel, out_shape=jax.ShapeDtypeStruct(out_shape, jnp....  10.9 us
    all_to_all x4, waiting for transfers between devices, exchange(): lax.all_to_all(values, 'tgt', split_axis=0, concat_axis=0, axis_index_gro...  10.7 us
  transfers between devices with their start and end apart: 12, of which 10 were waited for; matrix products, arithmetic and copies ran while one was open for 20% of the time, Pallas kernels for 3%

profile of v5, /device:TPU:1, one launch (start us, length us, event | category | flops | bytes accessed | tf_op | source)
XLA Modules:
  0.0 197.7 jit_solution(12065363436101559028)
XLA Ops:
  7.2 2.1 %shard_map.131 = bf16[16,128,128]{2,1,0:T(8,128)(2,1)} custom-call(bf16[128,1024]{1,0:T(8,128)(2,1)} %ivar_ref.3, bf16[128,1024]{1,0:T(8,128)(2,1)} %flux_ref.1), custom_call_target="tpu_custom_call" | custom-call | bytes 1048576 | tf_op jit(solution)/shard_map/pallas_call | solution.py:195
  9.2 10.2 %all-to-all-start = ((bf16[16,128,128]{2,1,0:T(8,128)(2,1)}), bf16[16,128,128]{2,1,0:T(8,128)(2,1)S(1)}, u32[]{:S(2)}, u32[]{:S(2)}) async-start(bf16[16,128,128]{2,1,0:T(8,128)(2,1)} %shard_map.131), calls=%async_computation | async-start | bytes 1048576 | tf_op jit(solution)/shard_map/all_to_all | solution.py:278
  19.5 1.8 copy-done
  21.3 0.9 copy-done.1
  22.2 2.4 %shard_map.130 = bf16[8,12,128,128]{3,2,1,0:T(8,128)(2,1)} custom-call(bf16[128,1024]{1,0:T(8,128)(2,1)S(1)} %copy-done.1, bf16[11,128,1024]{2,1,0:T(8,128)(2,1)S(1)} %bitcast.394), custom_call_target="tpu_custom_call" | custom-call | bytes 6291456 | tf_op jit(solution)/shard_map/pallas_call | solution.py:110
  24.6 4.8 %all-to-all-done.rows_ref = bf16[16,128,128]{2,1,0:T(8,128)(2,1)S(1)} async-done(((bf16[16,128,128]{2,1,0:T(8,128)(2,1)}), bf16[16,128,128]{2,1,0:T(8,128)(2,1)S(1)}, u32[]{:S(2)}, u32[]{:S(2)}) %all-to-all-start) | async-done | bytes 524320 | tf_op jit(solution)/shard_map/all_to_all | solution.py:278
  29.4 5.5 %all-to-all-start.1 = ((bf16[8,12,128,128]{3,2,1,0:T(8,128)(2,1)}), bf16[8,12,128,128]{3,2,1,0:T(8,128)(2,1)}, u32[]{:S(2)}, u32[]{:S(2)}) async-start(bf16[8,12,128,128]{3,2,1,0:T(8,128)(2,1)} %shard_map.130), calls=%async_computation.1 | async-start | bytes 6291456 | tf_op jit(solution)/shard_map/all_to_all | solution.py:278
  34.9 3.2 %shard_map.132 = f32[8,256,128]{2,1,0:T(8,128)S(1)} custom-call(s32[1,2048]{1,0:T(1,128)S(1)} %bitcast.395, bf16[16,128,128]{2,1,0:T(8,128)(2,1)S(1)} %all-to-all-done.rows_ref), custom_call_target="tpu_custom_call" | custom-call | flops 2147483648 | bytes 1572864 | tf_op jit(solution)/shard_map/pallas_call | solution.py:239
  38.2 7.5 %collective-permute-start.1 = (f32[256,128]{1,0:T(8,128)S(1)}, f32[256,128]{1,0:T(8,128)S(1)}, u32[]{:S(2)}, u32[]{:S(2)}) collective-permute-start(f32[256,128]{1,0:T(8,128)S(1)} %get-tuple-element.45), channel_id=1, source_target_pairs={{0,112},{4,116},{8,120},{12,124},{16,0},{20,4},{24,8},{28,12},{32,... | collective-permute-start | bytes 393224 | tf_op jit(solution)/shard_map/ppermute | solution.py:40
  45.8 1.9 collective-permute-start
  47.7 1.3 collective-permute-done.1
  49.1 5.3 %collective-permute-done = f32[256,128]{1,0:T(8,128)S(1)} collective-permute-done((f32[256,128]{1,0:T(8,128)S(1)}, f32[256,128]{1,0:T(8,128)S(1)}, u32[]{:S(2)}, u32[]{:S(2)}) %collective-permute-start) | collective-permute-done | bytes 131104 | tf_op jit(solution)/shard_map/ppermute | solution.py:40
  54.4 1.9 collective-permute-start.2
  56.3 5.5 %collective-permute-start.3 = (f32[256,128]{1,0:T(8,128)S(1)}, f32[256,128]{1,0:T(8,128)S(1)}, u32[]{:S(2)}, u32[]{:S(2)}) collective-permute-start(f32[256,128]{1,0:T(8,128)S(1)} %get-tuple-element.17), channel_id=1, source_target_pairs={{0,112},{4,116},{8,120},{12,124},{16,0},{20,4},{24,8},{28,12},{32,... | collective-permute-start | bytes 393224 | tf_op jit(solution)/shard_map/ppermute | solution.py:40
  61.8 0.4 collective-permute-done.2
  62.2 1.5 collective-permute-done.3
  63.8 1.9 collective-permute-start.4
  65.7 0.6 constant_dynamic-slice_fusion.1
  66.3 6.0 %collective-permute-start.5 = (f32[256,128]{1,0:T(8,128)S(1)}, f32[256,128]{1,0:T(8,128)S(1)}, u32[]{:S(2)}, u32[]{:S(2)}) collective-permute-start(f32[256,128]{1,0:T(8,128)S(1)} %get-tuple-element.19), channel_id=1, source_target_pairs={{0,112},{4,116},{8,120},{12,124},{16,0},{20,4},{24,8},{28,12},{32,... | collective-permute-start | bytes 393224 | tf_op jit(solution)/shard_map/ppermute | solution.py:40
  72.3 0.2 collective-permute-done.4
  72.5 1.7 collective-permute-done.5
  74.3 10.9 %shard_map.133 = bf16[16,8,11,16,128]{4,3,2,1,0:T(8,128)(2,1)} custom-call(s32[1,1024]{1,0:T(1,128)} %bitcast.408, bf16[8,12,128,128]{3,2,1,0:T(8,128)(2,1)} %all-to-all-done.1.rows_ref), custom_call_target="tpu_custom_call" | custom-call | flops 5905580032 | bytes 9437184 | tf_op jit(solution)/shard_map/pallas_call | solution.py:157
  85.2 4.4 %collective-permute-start.6 = (f32[256,128]{1,0:T(8,128)S(1)}, f32[256,128]{1,0:T(8,128)S(1)}, u32[]{:S(2)}, u32[]{:S(2)}) collective-permute-start(f32[256,128]{1,0:T(8,128)S(1)} %bitcast_add_fusion), channel_id=1, source_target_pairs={{0,16},{4,20},{8,24},{12,28},{16,32},{20,36},{24,40},{28,44},{32,4... | collective-permute-start | bytes 393224 | tf_op jit(solution)/shard_map/ppermute | solution.py:40
  89.6 0.1 fusion.73
  89.7 4.1 %collective-permute-done.6 = f32[256,128]{1,0:T(8,128)S(1)} collective-permute-done((f32[256,128]{1,0:T(8,128)S(1)}, f32[256,128]{1,0:T(8,128)S(1)}, u32[]{:S(2)}, u32[]{:S(2)}) %collective-permute-start.6) | collective-permute-done | bytes 131104 | tf_op jit(solution)/shard_map/ppermute | solution.py:40
  93.9 0.7 fusion.8
  94.5 15.1 %all-to-all-start.2 = ((f32[16,16,128]{2,1,0:T(8,128)}), f32[16,16,128]{2,1,0:T(8,128)S(1)}, u32[]{:S(2)}, u32[]{:S(2)}) async-start(f32[16,16,128]{2,1,0:T(8,128)} %bitcast.10), calls=%async_computation.2 | async-start | bytes 262144 | tf_op jit(solution)/shard_map/all_to_all | solution.py:278
  109.7 18.8 %while.1 = (s32[]{:T(128)}, f32[10,4608]{1,0:T(8,128)}, s32[8,2]{0,1:T(2,128)S(1)}, f32[8,10,4096]{2,1,0:T(8,128)S(1)}, s32[]{:T(128)}) while((s32[]{:T(128)}, f32[10,4608]{1,0:T(8,128)}, s32[8,2]{0,1:T(2,128)S(1)}, f32[8,10,4096]{2,1,0:T(8,128)S(1)}, s32[]{:T(128)}) %tuple.43), condition=%wide.while_cond, body=%wide.while_body.sunk | while | flops 2 | bytes 426089 | solution.py:77
  109.7 0.1 constant_dynamic-slice_fusion.4
  109.8 0.5 slice.757
  110.3 1.7 bitcast_dynamic-update-slice_fusion.2
  112.1 0.5 slice.757
  112.6 1.7 bitcast_dynamic-update-slice_fusion.2
  114.5 0.5 slice.757
  115.0 1.7 bitcast_dynamic-update-slice_fusion.2
  116.8 0.5 slice.757
  117.3 1.7 bitcast_dynamic-update-slice_fusion.2
  119.1 0.1 constant_dynamic-slice_fusion.4
  119.2 0.5 slice.757
  119.7 1.7 bitcast_dynamic-update-slice_fusion.2
  121.5 0.5 slice.757
  122.0 1.7 bitcast_dynamic-update-slice_fusion.2
  123.8 0.5 slice.757
  124.4 1.7 bitcast_dynamic-update-slice_fusion.2
  126.2 0.5 slice.757
  126.7 1.7 bitcast_dynamic-update-slice_fusion.2
  128.5 0.8 copy.23
  129.3 4.0 %gather_fusion.1 = f32[55,8,4096]{2,1,0:T(8,128)} fusion(f32[8,10,4096]{2,0,1:T(8,128)S(1)} %copy.23, s32[1024]{0:T(1024)S(1)} %pad_clamp_fusion), kind=kCustom, calls=%fused_computation.1 | custom fusion | bytes 14418140 | tf_op jit(solution)/shard_map/gather | solution.py:83
  133.2 3.9 %gather_fusion = f32[55,8,4096]{2,1,0:T(8,128)} fusion(f32[8,10,4096]{2,0,1:T(8,128)S(1)} %copy.23, s32[1024]{0:T(1024)S(1)} %pad_clamp_fusion.1), kind=kCustom, calls=%fused_computation | custom fusion | bytes 14418140 | tf_op jit(solution)/shard_map/gather | solution.py:83
  137.2 0.2 reshape.237
  137.4 0.1 bitcast_convert_fusion
  137.5 0.1 convert_element_type.24
  137.7 11.1 %all_gather.3 = bf16[2,16,4096]{2,1,0:T(8,128)(2,1)S(1)} all-gather(bf16[2,16,1024]{2,1,0:T(8,128)(2,1)S(1)} %convert_element_type.24), channel_id=1, replica_groups=mesh['tgt'=128,'band'=4] {'band'}, dimensions={2}, use_global_device_ids=true | all-gather | bytes 327680 | tf_op jit(solution)/shard_map/all_gather | solution.py:326
  148.8 0.2 fusion.74
  149.0 1.1 convolution_bitcast_fusion
  150.1 7.2 %fusion.3 = f32[55,8,16]{2,1,0:T(8,128)S(1)} fusion(f32[55,8,4096]{2,1,0:T(8,128)} %gather_fusion, f32[55,8,4096]{2,1,0:T(8,128)} %gather_fusion.1, bf16[2,16,4096]{2,1,0:T(8,128)(2,1)S(1)} %all_gather.3), kind=kOutput, calls=%fused_computation.7 | convolution fusion | flops 347832320 | bytes 14577152 | tf_op jit(solution)/shard_map/ti,zpi->ztp/dot_general | solution.py:84
  157.3 12.4 %reduce-scatter.2.cloned.1.call-done = bf16[1,8,11,16,128]{4,3,2,1,0:T(8,128)(2,1)} async-done(((bf16[16,8,11,16,128]{4,3,2,1,0:T(8,128)(2,1)}), bf16[1,8,11,16,128]{4,3,2,1,0:T(8,128)(2,1)}) %reduce-scatter.2.cloned.1.call-update) | async-done | bytes 360464 | tf_op jit(solution)/shard_map/reduce_scatter | solution.py:284
  169.7 12.7 %all-to-all-start.3 = ((bf16[8,11,16,128]{3,2,1,0:T(8,128)(2,1)}), bf16[8,11,16,128]{3,2,1,0:T(8,128)(2,1)S(1)}, u32[]{:S(2)}, u32[]{:S(2)}) async-start(bf16[8,11,16,128]{3,2,1,0:T(8,128)(2,1)} %bitcast.397), calls=%async_computation.4 | async-start | bytes 720896 | tf_op jit(solution)/shard_map/all_to_all | solution.py:278
  182.4 0.1 squeeze.300
  182.6 0.1 squeeze.299
  182.7 0.6 div.109
  183.3 0.8 add_bitcast_fusion
  184.1 6.0 %all-to-all-done.3 = bf16[8,11,16,128]{3,2,1,0:T(8,128)(2,1)S(1)} async-done(((bf16[8,11,16,128]{3,2,1,0:T(8,128)(2,1)}), bf16[8,11,16,128]{3,2,1,0:T(8,128)(2,1)S(1)}, u32[]{:S(2)}, u32[]{:S(2)}) %all-to-all-start.3) | async-done | bytes 360480 | tf_op jit(solution)/shard_map/all_to_all | solution.py:278
  190.1 0.8 fusion.7
  (38 shorter events, 0.8 us)
Async XLA Ops:
  9.2 20.1 %all-to-all-start = ((bf16[16,128,128]{2,1,0:T(8,128)(2,1)}), bf16[16,128,128]{2,1,0:T(8,128)(2,1)S(1)}, u32[]{:S(2)}, u32[]{:S(2)}) async-start(bf16[16,128,128]{2,1,0:T(8,128)(2,1)} %shard_map.131), calls=%async_computation | async-start | bytes 1048576 | tf_op jit(solution)/shard_map/all_to_all | solution.py:278
  19.5 1.8 copy-start
  21.3 0.9 copy-start.1
  24.6 10.3 %copy-start.2 = (s32[16384]{0:T(1024)S(1)}, s32[16384]{0:T(1024)}, u32[]{:S(2)}) copy-start(s32[16384]{0:T(1024)} %param.14) | copy-start | bytes 196612
  24.6 10.3 %copy-start.3 = (s32[16384]{0:T(1024)S(1)}, s32[16384]{0:T(1024)}, u32[]{:S(2)}) copy-start(s32[16384]{0:T(1024)} %param.15) | copy-start | bytes 196612
  29.4 44.9 %all-to-all-start.1 = ((bf16[8,12,128,128]{3,2,1,0:T(8,128)(2,1)}), bf16[8,12,128,128]{3,2,1,0:T(8,128)(2,1)}, u32[]{:S(2)}, u32[]{:S(2)}) async-start(bf16[8,12,128,128]{3,2,1,0:T(8,128)(2,1)} %shard_map.130), calls=%async_computation.1 | async-start | bytes 6291456 | tf_op jit(solution)/shard_map/all_to_all | solution.py:278
  34.9 134.8 %reduce-scatter.2.cloned.1.call-start = ((), (), s32[]{:S(2)}) async-start(), calls=%async_computation.5 | async-start | bytes 6127616 | tf_op jit(solution)/shard_map/reduce_scatter | solution.py:284
  38.2 10.8 %collective-permute-start.1 = (f32[256,128]{1,0:T(8,128)S(1)}, f32[256,128]{1,0:T(8,128)S(1)}, u32[]{:S(2)}, u32[]{:S(2)}) collective-permute-start(f32[256,128]{1,0:T(8,128)S(1)} %get-tuple-element.45), channel_id=1, source_target_pairs={{0,112},{4,116},{8,120},{12,124},{16,0},{20,4},{24,8},{28,12},{32,... | collective-permute-start | bytes 393224 | tf_op jit(solution)/shard_map/ppermute | solution.py:40
  45.8 8.6 %collective-permute-start = (f32[256,128]{1,0:T(8,128)S(1)}, f32[256,128]{1,0:T(8,128)S(1)}, u32[]{:S(2)}, u32[]{:S(2)}) collective-permute-start(f32[256,128]{1,0:T(8,128)S(1)} %get-tuple-element.46), channel_id=1, source_target_pairs={{0,16},{4,20},{8,24},{12,28},{16,32},{20,36},{24,40},{28,44},{32,4... | collective-permute-start | bytes 393224 | tf_op jit(solution)/shard_map/ppermute | solution.py:40
  54.4 7.8 %collective-permute-start.2 = (f32[256,128]{1,0:T(8,128)S(1)}, f32[256,128]{1,0:T(8,128)S(1)}, u32[]{:S(2)}, u32[]{:S(2)}) collective-permute-start(f32[256,128]{1,0:T(8,128)S(1)} %get-tuple-element.16), channel_id=1, source_target_pairs={{0,16},{4,20},{8,24},{12,28},{16,32},{20,36},{24,40},{28,44},{32,4... | collective-permute-start | bytes 393224 | tf_op jit(solution)/shard_map/ppermute | solution.py:40
  56.3 7.4 %collective-permute-start.3 = (f32[256,128]{1,0:T(8,128)S(1)}, f32[256,128]{1,0:T(8,128)S(1)}, u32[]{:S(2)}, u32[]{:S(2)}) collective-permute-start(f32[256,128]{1,0:T(8,128)S(1)} %get-tuple-element.17), channel_id=1, source_target_pairs={{0,112},{4,116},{8,120},{12,124},{16,0},{20,4},{24,8},{28,12},{32,... | collective-permute-start | bytes 393224 | tf_op jit(solution)/shard_map/ppermute | solution.py:40
  63.8 8.7 %collective-permute-start.4 = (f32[256,128]{1,0:T(8,128)S(1)}, f32[256,128]{1,0:T(8,128)S(1)}, u32[]{:S(2)}, u32[]{:S(2)}) collective-permute-start(f32[256,128]{1,0:T(8,128)S(1)} %get-tuple-element.18), channel_id=1, source_target_pairs={{0,16},{4,20},{8,24},{12,28},{16,32},{20,36},{24,40},{28,44},{32,4... | collective-permute-start | bytes 393224 | tf_op jit(solution)/shard_map/ppermute | solution.py:40
  66.3 7.9 %collective-permute-start.5 = (f32[256,128]{1,0:T(8,128)S(1)}, f32[256,128]{1,0:T(8,128)S(1)}, u32[]{:S(2)}, u32[]{:S(2)}) collective-permute-start(f32[256,128]{1,0:T(8,128)S(1)} %get-tuple-element.19), channel_id=1, source_target_pairs={{0,112},{4,116},{8,120},{12,124},{16,0},{20,4},{24,8},{28,12},{32,... | collective-permute-start | bytes 393224 | tf_op jit(solution)/shard_map/ppermute | solution.py:40
  85.2 4.4 %copy-start.6 = (s32[32]{0:T(128)S(1)}, s32[32]{0:T(128)}, u32[]{:S(2)}) copy-start(s32[32]{0:T(128)} %param.17) | copy-start | bytes 388
  85.2 8.6 %collective-permute-start.6 = (f32[256,128]{1,0:T(8,128)S(1)}, f32[256,128]{1,0:T(8,128)S(1)}, u32[]{:S(2)}, u32[]{:S(2)}) collective-permute-start(f32[256,128]{1,0:T(8,128)S(1)} %bitcast_add_fusion), channel_id=1, source_target_pairs={{0,16},{4,20},{8,24},{12,28},{16,32},{20,36},{24,40},{28,44},{32,4... | collective-permute-start | bytes 393224 | tf_op jit(solution)/shard_map/ppermute | solution.py:40
  94.5 42.6 %all-to-all-start.2 = ((f32[16,16,128]{2,1,0:T(8,128)}), f32[16,16,128]{2,1,0:T(8,128)S(1)}, u32[]{:S(2)}, u32[]{:S(2)}) async-start(f32[16,16,128]{2,1,0:T(8,128)} %bitcast.10), calls=%async_computation.2 | async-start | bytes 262144 | tf_op jit(solution)/shard_map/all_to_all | solution.py:278
  109.7 19.5 %copy-start.5 = (s32[55]{0:T(128)S(1)}, s32[55]{0:T(128)}, u32[]{:S(2)}) copy-start(s32[55]{0:T(128)} %constant.161) | copy-start | bytes 664
  129.2 4.0 %copy-start.4 = (s32[55]{0:T(128)S(1)}, s32[55]{0:T(128)}, u32[]{:S(2)}) copy-start(s32[55]{0:T(128)} %constant.160) | copy-start | bytes 664
  169.7 20.4 %all-to-all-start.3 = ((bf16[8,11,16,128]{3,2,1,0:T(8,128)(2,1)}), bf16[8,11,16,128]{3,2,1,0:T(8,128)(2,1)S(1)}, u32[]{:S(2)}, u32[]{:S(2)}) async-start(bf16[8,11,16,128]{3,2,1,0:T(8,128)(2,1)} %bitcast.397), calls=%async_computation.4 | async-start | bytes 720896 | tf_op jit(solution)/shard_map/all_to_all | solution.py:278
Sparse Core Ops, SparseCore 0:
  85.3 84.2 reduce-scatter.1

commit v6 on v5

--- a/solution.py
+++ b/solution.py
@@ -134,10 +134,10 @@
     def fill_terms():
         def one_source(source, carry):
             rows = pl.ds(pl.multiple_of(source * row_count, row_count), row_count)
-            weight = rows_ref[source, 0].astype(jnp.float32)
+            weight = rows_ref[source, 0]
             for plane in range(1, planes):
-                product = weight * rows_ref[source, plane].astype(jnp.float32)
-                terms[rows, (plane - 1) * lanes : plane * lanes] = product.astype(jnp.bfloat16)
+                product = weight * rows_ref[source, plane]
+                terms[rows, (plane - 1) * lanes : plane * lanes] = product
             return carry
 
         lax.fori_loop(0, sources, one_source, 0)
@@ -312,11 +312,12 @@
     rows = exchange(packed, plane_groups)
     turns = STATIONS // 2
     part, up, down = ring_start(mix_sum(wide_targets, mixed), my_z // PAIR)
-    for s in range(turns - 1):
+    for s in range(turns):
+        if s == turns // 2:
+            rows, up, down = lax.optimization_barrier((rows, up, down))
         part, up, down = ring_turn((part, up, down), s)
-        up, down = lax.optimization_barrier((up, down))
-    rows, up, down = lax.optimization_barrier((rows, up, down))
-    part, up, down = ring_turn((part, up, down), turns - 1)
+        if s < turns - 1:
+            up, down = lax.optimization_barrier((up, down))
     sums = part(0) + up + down
     res_sum = scatter_sum(coadd_res_rows(targets, rows))
 

time: 199 us -> 193 us (0.970)
  starting transfers between devices: 72.6 us -> 64.4 us
  waiting for transfers between devices: 37.7 us -> 40.9 us
    reduce_scatter x1, waiting for transfers between devices: 12.4 us -> 1.6 us  [scatter_sum(): lax.psum_scatter(values, 'tgt', scatter_dimension=0, axis_index_groups=ri...]
    all_to_all x4, starting transfers between devices: 43.5 us -> 32.7 us  [exchange(): lax.all_to_all(values, 'tgt', split_axis=0, concat_axis=0, axis_index_gro...]
    all_to_all x4, waiting for transfers between devices: 10.7 us -> 19.6 us  [exchange(): lax.all_to_all(values, 'tgt', split_axis=0, concat_axis=0, axis_index_gro...]
    ppermute x7, waiting for transfers between devices: 14.5 us -> 19.7 us  [ring_step(): return lax.ppermute(values, 'tgt', pairs)]
    ppermute x7, starting transfers between devices: 29.1 us -> 31.7 us  [ring_step(): return lax.ppermute(values, 'tgt', pairs)]
  transfers between devices with their start and end apart: 12 -> 12, of which waited for: 10 -> 10; matrix products, arithmetic and copies ran while one was open for 20% -> 21% of each run, Pallas kernels for 3% -> 3%
where the time goes in v6:
time: 193 us; the launch traced here: 192 us
  starting transfers between devices  64.4 us (33%)
  waiting for transfers between devices  40.9 us (21%)
  local copies, waits for them, and re-layouts  31.6 us (16%)
  Pallas kernels  18.5 us (10%)
  between operations  14.5 us (8%)
  blocking collectives  10.5 us (5%)
  matrix products  8.25 us (4%)
  other arithmetic  3.18 us (2%)
    all_to_all x4, starting transfers between devices, exchange(): lax.all_to_all(values, 'tgt', split_axis=0, concat_axis=0, axis_index_gro...  32.7 us
    ppermute x7, starting transfers between devices, ring_step(): return lax.ppermute(values, 'tgt', pairs)  31.7 us
    ppermute x7, waiting for transfers between devices, ring_step(): return lax.ppermute(values, 'tgt', pairs)  19.7 us
    all_to_all x4, waiting for transfers between devices, exchange(): lax.all_to_all(values, 'tgt', split_axis=0, concat_axis=0, axis_index_gro...  19.6 us
    gather x24, local copies, waits for them, and re-layouts  18.6 us
    pallas_call x1, Pallas kernels, coadd_res_rows(): pl.pallas_call(res_kernel, out_shape=jax.ShapeDtypeStruct(out_shape, jnp....  10.9 us
    all_gather x1, blocking collectives, shards(): lax.all_gather(own.astype(jnp.bfloat16), 'band', axis=2, tiled=True)  10.5 us
    gather x2, local copies, waits for them, and re-layouts, normal_terms(): products = windows[:, pair_first, :] * windows[:, pair_second, :]  7.9 us
  transfers between devices with their start and end apart: 12, of which 10 were waited for; matrix products, arithmetic and copies ran while one was open for 21% of the time, Pallas kernels for 3%

profile of v6, /device:TPU:1, one launch (start us, length us, event | category | flops | bytes accessed | tf_op | source)
XLA Modules:
  0.0 192.0 jit_solution(1478916470794383573)
XLA Ops:
  7.2 2.1 %shard_map.131 = bf16[16,128,128]{2,1,0:T(8,128)(2,1)} custom-call(bf16[128,1024]{1,0:T(8,128)(2,1)} %ivar_ref.3, bf16[128,1024]{1,0:T(8,128)(2,1)} %flux_ref.1), custom_call_target="tpu_custom_call" | custom-call | bytes 1048576 | tf_op jit(solution)/shard_map/pallas_call | solution.py:195
  9.2 10.2 %all-to-all-start = ((bf16[16,128,128]{2,1,0:T(8,128)(2,1)}), bf16[16,128,128]{2,1,0:T(8,128)(2,1)S(1)}, u32[]{:S(2)}, u32[]{:S(2)}) async-start(bf16[16,128,128]{2,1,0:T(8,128)(2,1)} %shard_map.131), calls=%async_computation | async-start | bytes 1048576 | tf_op jit(solution)/shard_map/all_to_all | solution.py:278
  19.5 1.8 copy-done
  21.3 0.9 copy-done.1
  22.2 2.4 %shard_map.130 = bf16[8,12,128,128]{3,2,1,0:T(8,128)(2,1)} custom-call(bf16[128,1024]{1,0:T(8,128)(2,1)S(1)} %copy-done.1, bf16[11,128,1024]{2,1,0:T(8,128)(2,1)S(1)} %bitcast.394), custom_call_target="tpu_custom_call" | custom-call | bytes 6291456 | tf_op jit(solution)/shard_map/pallas_call | solution.py:110
  24.6 4.8 %all-to-all-done.rows_ref = bf16[16,128,128]{2,1,0:T(8,128)(2,1)S(1)} async-done(((bf16[16,128,128]{2,1,0:T(8,128)(2,1)}), bf16[16,128,128]{2,1,0:T(8,128)(2,1)S(1)}, u32[]{:S(2)}, u32[]{:S(2)}) %all-to-all-start) | async-done | bytes 524320 | tf_op jit(solution)/shard_map/all_to_all | solution.py:278
  29.4 5.5 %all-to-all-start.1 = ((bf16[8,12,128,128]{3,2,1,0:T(8,128)(2,1)}), bf16[8,12,128,128]{3,2,1,0:T(8,128)(2,1)}, u32[]{:S(2)}, u32[]{:S(2)}) async-start(bf16[8,12,128,128]{3,2,1,0:T(8,128)(2,1)} %shard_map.130), calls=%async_computation.1 | async-start | bytes 6291456 | tf_op jit(solution)/shard_map/all_to_all | solution.py:278
  34.9 3.2 %shard_map.132 = f32[8,256,128]{2,1,0:T(8,128)S(1)} custom-call(s32[1,2048]{1,0:T(1,128)S(1)} %bitcast.395, bf16[16,128,128]{2,1,0:T(8,128)(2,1)S(1)} %all-to-all-done.rows_ref), custom_call_target="tpu_custom_call" | custom-call | flops 2147483648 | bytes 1572864 | tf_op jit(solution)/shard_map/pallas_call | solution.py:239
  38.2 7.5 %collective-permute-start.1 = (f32[256,128]{1,0:T(8,128)S(1)}, f32[256,128]{1,0:T(8,128)S(1)}, u32[]{:S(2)}, u32[]{:S(2)}) collective-permute-start(f32[256,128]{1,0:T(8,128)S(1)} %get-tuple-element.45), channel_id=1, source_target_pairs={{0,112},{4,116},{8,120},{12,124},{16,0},{20,4},{24,8},{28,12},{32,... | collective-permute-start | bytes 393224 | tf_op jit(solution)/shard_map/ppermute | solution.py:40
  45.8 1.9 %collective-permute-start = (f32[256,128]{1,0:T(8,128)S(1)}, f32[256,128]{1,0:T(8,128)S(1)}, u32[]{:S(2)}, u32[]{:S(2)}) collective-permute-start(f32[256,128]{1,0:T(8,128)S(1)} %get-tuple-element.46), channel_id=1, source_target_pairs={{0,16},{4,20},{8,24},{12,28},{16,32},{20,36},{24,40},{28,44},{32,4... | collective-permute-start | bytes 393224 | tf_op jit(solution)/shard_map/ppermute | solution.py:40
  47.7 1.3 collective-permute-done.1
  49.1 5.3 %collective-permute-done = f32[256,128]{1,0:T(8,128)S(1)} collective-permute-done((f32[256,128]{1,0:T(8,128)S(1)}, f32[256,128]{1,0:T(8,128)S(1)}, u32[]{:S(2)}, u32[]{:S(2)}) %collective-permute-start) | collective-permute-done | bytes 131104 | tf_op jit(solution)/shard_map/ppermute | solution.py:40
  54.4 1.9 %collective-permute-start.2 = (f32[256,128]{1,0:T(8,128)S(1)}, f32[256,128]{1,0:T(8,128)S(1)}, u32[]{:S(2)}, u32[]{:S(2)}) collective-permute-start(f32[256,128]{1,0:T(8,128)S(1)} %get-tuple-element.16), channel_id=1, source_target_pairs={{0,16},{4,20},{8,24},{12,28},{16,32},{20,36},{24,40},{28,44},{32,4... | collective-permute-start | bytes 393224 | tf_op jit(solution)/shard_map/ppermute | solution.py:40
  56.3 5.5 %collective-permute-start.3 = (f32[256,128]{1,0:T(8,128)S(1)}, f32[256,128]{1,0:T(8,128)S(1)}, u32[]{:S(2)}, u32[]{:S(2)}) collective-permute-start(f32[256,128]{1,0:T(8,128)S(1)} %get-tuple-element.17), channel_id=1, source_target_pairs={{0,112},{4,116},{8,120},{12,124},{16,0},{20,4},{24,8},{28,12},{32,... | collective-permute-start | bytes 393224 | tf_op jit(solution)/shard_map/ppermute | solution.py:40
  61.9 0.6 constant_dynamic-slice_fusion.1
  62.5 1.2 collective-permute-done.3
  63.8 8.8 %all-to-all-done.1.rows_ref = bf16[8,12,128,128]{3,2,1,0:T(8,128)(2,1)} async-done(((bf16[8,12,128,128]{3,2,1,0:T(8,128)(2,1)}), bf16[8,12,128,128]{3,2,1,0:T(8,128)(2,1)}, u32[]{:S(2)}, u32[]{:S(2)}) %all-to-all-start.1) | async-done | bytes 3145760 | tf_op jit(solution)/shard_map/all_to_all | solution.py:278
  72.5 10.9 %shard_map.133 = bf16[16,8,11,16,128]{4,3,2,1,0:T(8,128)(2,1)} custom-call(s32[1,1024]{1,0:T(1,128)} %bitcast.408, bf16[8,12,128,128]{3,2,1,0:T(8,128)(2,1)} %all-to-all-done.1.rows_ref), custom_call_target="tpu_custom_call" | custom-call | flops 5905580032 | bytes 9437184 | tf_op jit(solution)/shard_map/pallas_call | solution.py:157
  83.4 1.9 %collective-permute-start.4 = (f32[256,128]{1,0:T(8,128)S(1)}, f32[256,128]{1,0:T(8,128)S(1)}, u32[]{:S(2)}, u32[]{:S(2)}) collective-permute-start(f32[256,128]{1,0:T(8,128)S(1)} %get-tuple-element.20), channel_id=1, source_target_pairs={{0,16},{4,20},{8,24},{12,28},{16,32},{20,36},{24,40},{28,44},{32,4... | collective-permute-start | bytes 393224 | tf_op jit(solution)/shard_map/ppermute | solution.py:40
  85.4 7.5 %collective-permute-start.5 = (f32[256,128]{1,0:T(8,128)S(1)}, f32[256,128]{1,0:T(8,128)S(1)}, u32[]{:S(2)}, u32[]{:S(2)}) collective-permute-start(f32[256,128]{1,0:T(8,128)S(1)} %get-tuple-element.21), channel_id=1, source_target_pairs={{0,112},{4,116},{8,120},{12,124},{16,0},{20,4},{24,8},{28,12},{32,... | collective-permute-start | bytes 393224 | tf_op jit(solution)/shard_map/ppermute | solution.py:40
  92.9 1.9 collective-permute-done.4
  94.8 3.1 %collective-permute-done.5 = f32[256,128]{1,0:T(8,128)S(1)} collective-permute-done((f32[256,128]{1,0:T(8,128)S(1)}, f32[256,128]{1,0:T(8,128)S(1)}, u32[]{:S(2)}, u32[]{:S(2)}) %collective-permute-start.5) | collective-permute-done | bytes 131104 | tf_op jit(solution)/shard_map/ppermute | solution.py:40
  97.9 5.4 %collective-permute-start.6 = (f32[256,128]{1,0:T(8,128)S(1)}, f32[256,128]{1,0:T(8,128)S(1)}, u32[]{:S(2)}, u32[]{:S(2)}) collective-permute-start(f32[256,128]{1,0:T(8,128)S(1)} %bitcast_add_fusion), channel_id=1, source_target_pairs={{0,16},{4,20},{8,24},{12,28},{16,32},{20,36},{24,40},{28,44},{32,4... | collective-permute-start | bytes 393224 | tf_op jit(solution)/shard_map/ppermute | solution.py:40
  103.4 0.1 fusion.73
  103.5 6.9 %collective-permute-done.6 = f32[256,128]{1,0:T(8,128)S(1)} collective-permute-done((f32[256,128]{1,0:T(8,128)S(1)}, f32[256,128]{1,0:T(8,128)S(1)}, u32[]{:S(2)}, u32[]{:S(2)}) %collective-permute-start.6) | collective-permute-done | bytes 131104 | tf_op jit(solution)/shard_map/ppermute | solution.py:40
  110.4 0.7 fusion.8
  111.1 7.1 %all-to-all-start.2 = ((f32[16,16,128]{2,1,0:T(8,128)}), f32[16,16,128]{2,1,0:T(8,128)S(1)}, u32[]{:S(2)}, u32[]{:S(2)}) async-start(f32[16,16,128]{2,1,0:T(8,128)} %bitcast.10), calls=%async_computation.2 | async-start | bytes 262144 | tf_op jit(solution)/shard_map/all_to_all | solution.py:278
  118.2 18.8 %while.1 = (s32[]{:T(128)}, f32[10,4608]{1,0:T(8,128)}, s32[8,2]{0,1:T(2,128)S(1)}, f32[8,10,4096]{2,1,0:T(8,128)S(1)}, s32[]{:T(128)}) while((s32[]{:T(128)}, f32[10,4608]{1,0:T(8,128)}, s32[8,2]{0,1:T(2,128)S(1)}, f32[8,10,4096]{2,1,0:T(8,128)S(1)}, s32[]{:T(128)}) %tuple.43), condition=%wide.while_cond, body=%wide.while_body.sunk | while | flops 2 | bytes 426089 | solution.py:77
  118.2 0.1 constant_dynamic-slice_fusion.4
  118.3 0.5 slice.757
  118.8 1.7 bitcast_dynamic-update-slice_fusion.2
  120.6 0.1 constant_dynamic-slice_fusion.4
  120.6 0.5 slice.757
  121.2 1.7 bitcast_dynamic-update-slice_fusion.2
  123.0 0.5 slice.757
  123.5 1.7 bitcast_dynamic-update-slice_fusion.2
  125.3 0.5 slice.757
  125.8 1.7 bitcast_dynamic-update-slice_fusion.2
  127.7 0.5 slice.757
  128.2 1.7 bitcast_dynamic-update-slice_fusion.2
  130.0 0.5 slice.757
  130.5 1.7 bitcast_dynamic-update-slice_fusion.2
  132.4 0.5 slice.757
  132.9 1.7 bitcast_dynamic-update-slice_fusion.2
  134.7 0.5 slice.757
  135.2 1.7 bitcast_dynamic-update-slice_fusion.2
  137.0 0.8 copy.23
  137.8 4.0 %gather_fusion.1 = f32[55,8,4096]{2,1,0:T(8,128)} fusion(f32[8,10,4096]{2,0,1:T(8,128)S(1)} %copy.23, s32[1024]{0:T(1024)S(1)} %pad_clamp_fusion), kind=kCustom, calls=%fused_computation.1 | custom fusion | bytes 14418140 | tf_op jit(solution)/shard_map/gather | solution.py:83
  141.8 3.9 %gather_fusion = f32[55,8,4096]{2,1,0:T(8,128)} fusion(f32[8,10,4096]{2,0,1:T(8,128)S(1)} %copy.23, s32[1024]{0:T(1024)S(1)} %pad_clamp_fusion.1), kind=kCustom, calls=%fused_computation | custom fusion | bytes 14418140 | tf_op jit(solution)/shard_map/gather | solution.py:83
  145.7 0.2 reshape.237
  145.9 0.1 bitcast_convert_fusion
  146.1 0.1 convert_element_type.24
  146.2 10.5 %all_gather.3 = bf16[2,16,4096]{2,1,0:T(8,128)(2,1)S(1)} all-gather(bf16[2,16,1024]{2,1,0:T(8,128)(2,1)S(1)} %convert_element_type.24), channel_id=1, replica_groups=mesh['tgt'=128,'band'=4] {'band'}, dimensions={2}, use_global_device_ids=true | all-gather | bytes 327680 | tf_op jit(solution)/shard_map/all_gather | solution.py:327
  156.7 0.2 fusion.74
  156.9 1.1 convolution_bitcast_fusion
  158.0 7.2 %fusion.3 = f32[55,8,16]{2,1,0:T(8,128)S(1)} fusion(f32[55,8,4096]{2,1,0:T(8,128)} %gather_fusion, f32[55,8,4096]{2,1,0:T(8,128)} %gather_fusion.1, bf16[2,16,4096]{2,1,0:T(8,128)(2,1)S(1)} %all_gather.3), kind=kOutput, calls=%fused_computation.7 | convolution fusion | flops 347832320 | bytes 14577152 | tf_op jit(solution)/shard_map/ti,zpi->ztp/dot_general | solution.py:84
  165.2 1.6 reduce-scatter.2.cloned.1.call-done
  166.8 9.9 %all-to-all-start.3 = ((bf16[8,11,16,128]{3,2,1,0:T(8,128)(2,1)}), bf16[8,11,16,128]{3,2,1,0:T(8,128)(2,1)S(1)}, u32[]{:S(2)}, u32[]{:S(2)}) async-start(bf16[8,11,16,128]{3,2,1,0:T(8,128)(2,1)} %bitcast.397), calls=%async_computation.4 | async-start | bytes 720896 | tf_op jit(solution)/shard_map/all_to_all | solution.py:278
  176.7 0.1 squeeze.300
  176.9 0.1 squeeze.299
  177.0 0.6 div.109
  177.6 0.8 add_bitcast_fusion
  178.4 6.0 %all-to-all-done.3 = bf16[8,11,16,128]{3,2,1,0:T(8,128)(2,1)S(1)} async-done(((bf16[8,11,16,128]{3,2,1,0:T(8,128)(2,1)}), bf16[8,11,16,128]{3,2,1,0:T(8,128)(2,1)S(1)}, u32[]{:S(2)}, u32[]{:S(2)}) %all-to-all-start.3) | async-done | bytes 360480 | tf_op jit(solution)/shard_map/all_to_all | solution.py:278
  184.4 0.8 fusion.7
  (38 shorter events, 0.8 us)
Async XLA Ops:
  9.2 20.1 %all-to-all-start = ((bf16[16,128,128]{2,1,0:T(8,128)(2,1)}), bf16[16,128,128]{2,1,0:T(8,128)(2,1)S(1)}, u32[]{:S(2)}, u32[]{:S(2)}) async-start(bf16[16,128,128]{2,1,0:T(8,128)(2,1)} %shard_map.131), calls=%async_computation | async-start | bytes 1048576 | tf_op jit(solution)/shard_map/all_to_all | solution.py:278
  19.5 1.8 copy-start
  21.3 0.9 copy-start.1
  24.6 10.3 %copy-start.2 = (s32[16384]{0:T(1024)S(1)}, s32[16384]{0:T(1024)}, u32[]{:S(2)}) copy-start(s32[16384]{0:T(1024)} %param.14) | copy-start | bytes 196612
  24.6 10.3 %copy-start.3 = (s32[16384]{0:T(1024)S(1)}, s32[16384]{0:T(1024)}, u32[]{:S(2)}) copy-start(s32[16384]{0:T(1024)} %param.15) | copy-start | bytes 196612
  29.4 43.2 %all-to-all-start.1 = ((bf16[8,12,128,128]{3,2,1,0:T(8,128)(2,1)}), bf16[8,12,128,128]{3,2,1,0:T(8,128)(2,1)}, u32[]{:S(2)}, u32[]{:S(2)}) async-start(bf16[8,12,128,128]{3,2,1,0:T(8,128)(2,1)} %shard_map.130), calls=%async_computation.1 | async-start | bytes 6291456 | tf_op jit(solution)/shard_map/all_to_all | solution.py:278
  34.9 131.9 %reduce-scatter.2.cloned.1.call-start = ((), (), s32[]{:S(2)}) async-start(), calls=%async_computation.5 | async-start | bytes 6127616 | tf_op jit(solution)/shard_map/reduce_scatter | solution.py:284
  38.2 10.8 %collective-permute-start.1 = (f32[256,128]{1,0:T(8,128)S(1)}, f32[256,128]{1,0:T(8,128)S(1)}, u32[]{:S(2)}, u32[]{:S(2)}) collective-permute-start(f32[256,128]{1,0:T(8,128)S(1)} %get-tuple-element.45), channel_id=1, source_target_pairs={{0,112},{4,116},{8,120},{12,124},{16,0},{20,4},{24,8},{28,12},{32,... | collective-permute-start | bytes 393224 | tf_op jit(solution)/shard_map/ppermute | solution.py:40
  45.8 8.6 %collective-permute-start = (f32[256,128]{1,0:T(8,128)S(1)}, f32[256,128]{1,0:T(8,128)S(1)}, u32[]{:S(2)}, u32[]{:S(2)}) collective-permute-start(f32[256,128]{1,0:T(8,128)S(1)} %get-tuple-element.46), channel_id=1, source_target_pairs={{0,16},{4,20},{8,24},{12,28},{16,32},{20,36},{24,40},{28,44},{32,4... | collective-permute-start | bytes 393224 | tf_op jit(solution)/shard_map/ppermute | solution.py:40
  54.4 8.1 %collective-permute-start.2 = (f32[256,128]{1,0:T(8,128)S(1)}, f32[256,128]{1,0:T(8,128)S(1)}, u32[]{:S(2)}, u32[]{:S(2)}) collective-permute-start(f32[256,128]{1,0:T(8,128)S(1)} %get-tuple-element.16), channel_id=1, source_target_pairs={{0,16},{4,20},{8,24},{12,28},{16,32},{20,36},{24,40},{28,44},{32,4... | collective-permute-start | bytes 393224 | tf_op jit(solution)/shard_map/ppermute | solution.py:40
  56.3 7.4 %collective-permute-start.3 = (f32[256,128]{1,0:T(8,128)S(1)}, f32[256,128]{1,0:T(8,128)S(1)}, u32[]{:S(2)}, u32[]{:S(2)}) collective-permute-start(f32[256,128]{1,0:T(8,128)S(1)} %get-tuple-element.17), channel_id=1, source_target_pairs={{0,112},{4,116},{8,120},{12,124},{16,0},{20,4},{24,8},{28,12},{32,... | collective-permute-start | bytes 393224 | tf_op jit(solution)/shard_map/ppermute | solution.py:40
  83.4 19.9 %copy-start.6 = (s32[32]{0:T(128)S(1)}, s32[32]{0:T(128)}, u32[]{:S(2)}) copy-start(s32[32]{0:T(128)} %param.17) | copy-start | bytes 388
  83.4 11.4 %collective-permute-start.4 = (f32[256,128]{1,0:T(8,128)S(1)}, f32[256,128]{1,0:T(8,128)S(1)}, u32[]{:S(2)}, u32[]{:S(2)}) collective-permute-start(f32[256,128]{1,0:T(8,128)S(1)} %get-tuple-element.20), channel_id=1, source_target_pairs={{0,16},{4,20},{8,24},{12,28},{16,32},{20,36},{24,40},{28,44},{32,4... | collective-permute-start | bytes 393224 | tf_op jit(solution)/shard_map/ppermute | solution.py:40
  85.4 12.5 %collective-permute-start.5 = (f32[256,128]{1,0:T(8,128)S(1)}, f32[256,128]{1,0:T(8,128)S(1)}, u32[]{:S(2)}, u32[]{:S(2)}) collective-permute-start(f32[256,128]{1,0:T(8,128)S(1)} %get-tuple-element.21), channel_id=1, source_target_pairs={{0,112},{4,116},{8,120},{12,124},{16,0},{20,4},{24,8},{28,12},{32,... | collective-permute-start | bytes 393224 | tf_op jit(solution)/shard_map/ppermute | solution.py:40
  97.9 12.5 %collective-permute-start.6 = (f32[256,128]{1,0:T(8,128)S(1)}, f32[256,128]{1,0:T(8,128)S(1)}, u32[]{:S(2)}, u32[]{:S(2)}) collective-permute-start(f32[256,128]{1,0:T(8,128)S(1)} %bitcast_add_fusion), channel_id=1, source_target_pairs={{0,16},{4,20},{8,24},{12,28},{16,32},{20,36},{24,40},{28,44},{32,4... | collective-permute-start | bytes 393224 | tf_op jit(solution)/shard_map/ppermute | solution.py:40
  111.1 34.6 %all-to-all-start.2 = ((f32[16,16,128]{2,1,0:T(8,128)}), f32[16,16,128]{2,1,0:T(8,128)S(1)}, u32[]{:S(2)}, u32[]{:S(2)}) async-start(f32[16,16,128]{2,1,0:T(8,128)} %bitcast.10), calls=%async_computation.2 | async-start | bytes 262144 | tf_op jit(solution)/shard_map/all_to_all | solution.py:278
  118.2 19.6 %copy-start.5 = (s32[55]{0:T(128)S(1)}, s32[55]{0:T(128)}, u32[]{:S(2)}) copy-start(s32[55]{0:T(128)} %constant.161) | copy-start | bytes 664
  137.8 4.0 %copy-start.4 = (s32[55]{0:T(128)S(1)}, s32[55]{0:T(128)}, u32[]{:S(2)}) copy-start(s32[55]{0:T(128)} %constant.160) | copy-start | bytes 664
  166.8 17.6 %all-to-all-start.3 = ((bf16[8,11,16,128]{3,2,1,0:T(8,128)(2,1)}), bf16[8,11,16,128]{3,2,1,0:T(8,128)(2,1)S(1)}, u32[]{:S(2)}, u32[]{:S(2)}) async-start(bf16[8,11,16,128]{3,2,1,0:T(8,128)(2,1)} %bitcast.397), calls=%async_computation.4 | async-start | bytes 720896 | tf_op jit(solution)/shard_map/all_to_all | solution.py:278
Sparse Core Ops, SparseCore 0:
  83.6 83.1 reduce-scatter.1

commit v7 on v6

--- a/solution.py
+++ b/solution.py
@@ -100,8 +100,9 @@
     lanes = out_ref.shape[-1]
     for part in range(PLANE):
         columns = slice(part * lanes, (part + 1) * lanes)
-        out_ref[part, 0] = ivar_ref[:, columns]
-        out_ref[part, 1:] = res_ref[:, :, columns]
+        weight = ivar_ref[:, columns]
+        for diagonal in range(NDIAG):
+            out_ref[part, diagonal] = weight * res_ref[diagonal, :, columns]
 
 
 def split_lanes(ivar, res):
@@ -109,10 +110,12 @@
     lanes = wave_dev // PLANE
     return pl.pallas_call(
         split_kernel,
-        out_shape=jax.ShapeDtypeStruct((PLANE, diagonals + 1, row_count, lanes), res.dtype),
+        out_shape=jax.ShapeDtypeStruct((PLANE, diagonals, row_count, lanes), res.dtype),
         compiler_params=pltpu.CompilerParams(vmem_limit_bytes=40 << 20),
         cost_estimate=pl.CostEstimate(
-            flops=0, bytes_accessed=4 * (diagonals + 1) * row_count * wave_dev, transcendentals=0
+            flops=diagonals * row_count * wave_dev,
+            bytes_accessed=4 * (diagonals + 1) * row_count * wave_dev,
+            transcendentals=0,
         ),
     )(ivar, res)
 
@@ -134,10 +137,8 @@
     def fill_terms():
         def one_source(source, carry):
             rows = pl.ds(pl.multiple_of(source * row_count, row_count), row_count)
-            weight = rows_ref[source, 0]
-            for plane in range(1, planes):
-                product = weight * rows_ref[source, plane]
-                terms[rows, (plane - 1) * lanes : plane * lanes] = product
+            for plane in range(planes):
+                terms[rows, plane * lanes : (plane + 1) * lanes] = rows_ref[source, plane]
             return carry
 
         lax.fori_loop(0, sources, one_source, 0)
@@ -147,13 +148,13 @@
         for owner in range(PLANE):
             first = g * QROWS + owner * TGT_DEV
             block = sums[first : first + TGT_DEV].astype(jnp.bfloat16)
-            for diagonal in range(planes - 1):
+            for diagonal in range(planes):
                 res_ref[g, owner, diagonal] = block[:, diagonal * lanes : (diagonal + 1) * lanes]
 
 
 def coadd_res_rows(targets, rows):
     sources, planes, row_count, lanes = rows.shape
-    out_shape = (ZS, PLANE, planes - 1, TGT_DEV, lanes)
+    out_shape = (ZS, PLANE, planes, TGT_DEV, lanes)
     return pl.pallas_call(
         res_kernel,
         out_shape=jax.ShapeDtypeStruct(out_shape, jnp.bfloat16),
@@ -163,10 +164,10 @@
             pl.BlockSpec(rows.shape, lambda i: (0, 0, 0, 0)),
         ],
         out_specs=pl.BlockSpec((GROUP,) + out_shape[1:], lambda i: (i, 0, 0, 0, 0)),
-        scratch_shapes=[pltpu.VMEM((sources * row_count, (planes - 1) * lanes), jnp.bfloat16)],
+        scratch_shapes=[pltpu.VMEM((sources * row_count, planes * lanes), jnp.bfloat16)],
         compiler_params=pltpu.CompilerParams(vmem_limit_bytes=56 << 20),
         cost_estimate=pl.CostEstimate(
-            flops=2 * ZS * QROWS * sources * row_count * (planes - 1) * lanes,
+            flops=2 * ZS * QROWS * sources * row_count * planes * lanes,
             bytes_accessed=2 * (rows.size + ZS * QROWS * planes * lanes),
             transcendentals=0,
         ),

time: 193 us -> 190 us (0.984)
  waiting for transfers between devices: 40.9 us -> 37.7 us
    all_to_all x4, waiting for transfers between devices: 19.6 us -> 16.7 us  [exchange(): lax.all_to_all(values, 'tgt', split_axis=0, concat_axis=0, axis_index_gro...]
where the time goes in v7:
time: 190 us; the launch traced here: 189 us
  starting transfers between devices  63.3 us (33%)
  waiting for transfers between devices  37.7 us (20%)
  local copies, waits for them, and re-layouts  31.6 us (17%)
  Pallas kernels  18.4 us (10%)
  between operations  14.5 us (8%)
  blocking collectives  12 us (6%)
  matrix products  8.23 us (4%)
  other arithmetic  3.18 us (2%)
    ppermute x7, starting transfers between devices, ring_step(): return lax.ppermute(values, 'tgt', pairs)  31.7 us
    all_to_all x4, starting transfers between devices, exchange(): lax.all_to_all(values, 'tgt', split_axis=0, concat_axis=0, axis_index_gro...  31.6 us
    ppermute x7, waiting for transfers between devices, ring_step(): return lax.ppermute(values, 'tgt', pairs)  20.1 us
    gather x24, local copies, waits for them, and re-layouts  18.6 us
    all_to_all x4, waiting for transfers between devices, exchange(): lax.all_to_all(values, 'tgt', split_axis=0, concat_axis=0, axis_index_gro...  16.7 us
    all_gather x1, blocking collectives, shards(): lax.all_gather(own.astype(jnp.bfloat16), 'band', axis=2, tiled=True)  12 us
    pallas_call x1, Pallas kernels, coadd_res_rows(): pl.pallas_call(res_kernel, out_shape=jax.ShapeDtypeStruct(out_shape, jnp....  10.8 us
    gather x2, local copies, waits for them, and re-layouts, normal_terms(): products = windows[:, pair_first, :] * windows[:, pair_second, :]  7.9 us
  transfers between devices with their start and end apart: 12, of which 10 were waited for; matrix products, arithmetic and copies ran while one was open for 21% of the time, Pallas kernels for 3%

profile of v7, /device:TPU:1, one launch (start us, length us, event | category | flops | bytes accessed | tf_op | source)
XLA Modules:
  0.0 189.1 jit_solution(2194568011747172368)
XLA Ops:
  7.2 2.1 %shard_map.131 = bf16[16,128,128]{2,1,0:T(8,128)(2,1)} custom-call(bf16[128,1024]{1,0:T(8,128)(2,1)} %ivar_ref.3, bf16[128,1024]{1,0:T(8,128)(2,1)} %flux_ref.1), custom_call_target="tpu_custom_call" | custom-call | bytes 1048576 | tf_op jit(solution)/shard_map/pallas_call | solution.py:196
  9.2 10.2 %all-to-all-start = ((bf16[16,128,128]{2,1,0:T(8,128)(2,1)}), bf16[16,128,128]{2,1,0:T(8,128)(2,1)S(1)}, u32[]{:S(2)}, u32[]{:S(2)}) async-start(bf16[16,128,128]{2,1,0:T(8,128)(2,1)} %shard_map.131), calls=%async_computation | async-start | bytes 1048576 | tf_op jit(solution)/shard_map/all_to_all | solution.py:279
  19.5 1.8 copy-done
  21.3 0.9 copy-done.1
  22.2 2.4 %shard_map.130 = bf16[8,11,128,128]{3,2,1,0:T(8,128)(2,1)} custom-call(bf16[128,1024]{1,0:T(8,128)(2,1)S(1)} %copy-done.1, bf16[11,128,1024]{2,1,0:T(8,128)(2,1)S(1)} %bitcast.394), custom_call_target="tpu_custom_call" | custom-call | flops 1441792 | bytes 6291456 | tf_op jit(solution)/shard_map/pallas_call | solution.py:111
  24.6 4.8 %all-to-all-done.rows_ref = bf16[16,128,128]{2,1,0:T(8,128)(2,1)S(1)} async-done(((bf16[16,128,128]{2,1,0:T(8,128)(2,1)}), bf16[16,128,128]{2,1,0:T(8,128)(2,1)S(1)}, u32[]{:S(2)}, u32[]{:S(2)}) %all-to-all-start) | async-done | bytes 524320 | tf_op jit(solution)/shard_map/all_to_all | solution.py:279
  29.4 5.5 %all-to-all-start.1 = ((bf16[8,11,128,128]{3,2,1,0:T(8,128)(2,1)}), bf16[8,11,128,128]{3,2,1,0:T(8,128)(2,1)}, u32[]{:S(2)}, u32[]{:S(2)}) async-start(bf16[8,11,128,128]{3,2,1,0:T(8,128)(2,1)} %shard_map.130), calls=%async_computation.1 | async-start | bytes 5767168 | tf_op jit(solution)/shard_map/all_to_all | solution.py:279
  34.9 3.2 %shard_map.132 = f32[8,256,128]{2,1,0:T(8,128)S(1)} custom-call(s32[1,2048]{1,0:T(1,128)S(1)} %bitcast.395, bf16[16,128,128]{2,1,0:T(8,128)(2,1)S(1)} %all-to-all-done.rows_ref), custom_call_target="tpu_custom_call" | custom-call | flops 2147483648 | bytes 1572864 | tf_op jit(solution)/shard_map/pallas_call | solution.py:240
  38.2 7.5 %collective-permute-start.1 = (f32[256,128]{1,0:T(8,128)S(1)}, f32[256,128]{1,0:T(8,128)S(1)}, u32[]{:S(2)}, u32[]{:S(2)}) collective-permute-start(f32[256,128]{1,0:T(8,128)S(1)} %get-tuple-element.45), channel_id=1, source_target_pairs={{0,112},{4,116},{8,120},{12,124},{16,0},{20,4},{24,8},{28,12},{32,... | collective-permute-start | bytes 393224 | tf_op jit(solution)/shard_map/ppermute | solution.py:40
  45.7 1.9 %collective-permute-start = (f32[256,128]{1,0:T(8,128)S(1)}, f32[256,128]{1,0:T(8,128)S(1)}, u32[]{:S(2)}, u32[]{:S(2)}) collective-permute-start(f32[256,128]{1,0:T(8,128)S(1)} %get-tuple-element.46), channel_id=1, source_target_pairs={{0,16},{4,20},{8,24},{12,28},{16,32},{20,36},{24,40},{28,44},{32,4... | collective-permute-start | bytes 393224 | tf_op jit(solution)/shard_map/ppermute | solution.py:40
  47.7 1.3 collective-permute-done.1
  49.0 5.3 %collective-permute-done = f32[256,128]{1,0:T(8,128)S(1)} collective-permute-done((f32[256,128]{1,0:T(8,128)S(1)}, f32[256,128]{1,0:T(8,128)S(1)}, u32[]{:S(2)}, u32[]{:S(2)}) %collective-permute-start) | collective-permute-done | bytes 131104 | tf_op jit(solution)/shard_map/ppermute | solution.py:40
  54.4 1.9 %collective-permute-start.2 = (f32[256,128]{1,0:T(8,128)S(1)}, f32[256,128]{1,0:T(8,128)S(1)}, u32[]{:S(2)}, u32[]{:S(2)}) collective-permute-start(f32[256,128]{1,0:T(8,128)S(1)} %get-tuple-element.16), channel_id=1, source_target_pairs={{0,16},{4,20},{8,24},{12,28},{16,32},{20,36},{24,40},{28,44},{32,4... | collective-permute-start | bytes 393224 | tf_op jit(solution)/shard_map/ppermute | solution.py:40
  56.3 5.5 %collective-permute-start.3 = (f32[256,128]{1,0:T(8,128)S(1)}, f32[256,128]{1,0:T(8,128)S(1)}, u32[]{:S(2)}, u32[]{:S(2)}) collective-permute-start(f32[256,128]{1,0:T(8,128)S(1)} %get-tuple-element.17), channel_id=1, source_target_pairs={{0,112},{4,116},{8,120},{12,124},{16,0},{20,4},{24,8},{28,12},{32,... | collective-permute-start | bytes 393224 | tf_op jit(solution)/shard_map/ppermute | solution.py:40
  61.9 0.6 constant_dynamic-slice_fusion.1
  62.5 1.2 collective-permute-done.3
  63.7 6.0 %all-to-all-done.1.rows_ref = bf16[8,11,128,128]{3,2,1,0:T(8,128)(2,1)} async-done(((bf16[8,11,128,128]{3,2,1,0:T(8,128)(2,1)}), bf16[8,11,128,128]{3,2,1,0:T(8,128)(2,1)}, u32[]{:S(2)}, u32[]{:S(2)}) %all-to-all-start.1) | async-done | bytes 2883616 | tf_op jit(solution)/shard_map/all_to_all | solution.py:279
  69.7 10.8 %shard_map.133 = bf16[16,8,11,16,128]{4,3,2,1,0:T(8,128)(2,1)} custom-call(s32[1,1024]{1,0:T(1,128)} %bitcast.408, bf16[8,11,128,128]{3,2,1,0:T(8,128)(2,1)} %all-to-all-done.1.rows_ref), custom_call_target="tpu_custom_call" | custom-call | flops 5905580032 | bytes 8650752 | tf_op jit(solution)/shard_map/pallas_call | solution.py:158
  80.5 1.9 %collective-permute-start.4 = (f32[256,128]{1,0:T(8,128)S(1)}, f32[256,128]{1,0:T(8,128)S(1)}, u32[]{:S(2)}, u32[]{:S(2)}) collective-permute-start(f32[256,128]{1,0:T(8,128)S(1)} %get-tuple-element.20), channel_id=1, source_target_pairs={{0,16},{4,20},{8,24},{12,28},{16,32},{20,36},{24,40},{28,44},{32,4... | collective-permute-start | bytes 393224 | tf_op jit(solution)/shard_map/ppermute | solution.py:40
  82.5 7.5 %collective-permute-start.5 = (f32[256,128]{1,0:T(8,128)S(1)}, f32[256,128]{1,0:T(8,128)S(1)}, u32[]{:S(2)}, u32[]{:S(2)}) collective-permute-start(f32[256,128]{1,0:T(8,128)S(1)} %get-tuple-element.21), channel_id=1, source_target_pairs={{0,112},{4,116},{8,120},{12,124},{16,0},{20,4},{24,8},{28,12},{32,... | collective-permute-start | bytes 393224 | tf_op jit(solution)/shard_map/ppermute | solution.py:40
  90.0 1.9 collective-permute-done.4
  91.9 3.1 %collective-permute-done.5 = f32[256,128]{1,0:T(8,128)S(1)} collective-permute-done((f32[256,128]{1,0:T(8,128)S(1)}, f32[256,128]{1,0:T(8,128)S(1)}, u32[]{:S(2)}, u32[]{:S(2)}) %collective-permute-start.5) | collective-permute-done | bytes 131104 | tf_op jit(solution)/shard_map/ppermute | solution.py:40
  95.0 5.4 %collective-permute-start.6 = (f32[256,128]{1,0:T(8,128)S(1)}, f32[256,128]{1,0:T(8,128)S(1)}, u32[]{:S(2)}, u32[]{:S(2)}) collective-permute-start(f32[256,128]{1,0:T(8,128)S(1)} %bitcast_add_fusion), channel_id=1, source_target_pairs={{0,16},{4,20},{8,24},{12,28},{16,32},{20,36},{24,40},{28,44},{32,4... | collective-permute-start | bytes 393224 | tf_op jit(solution)/shard_map/ppermute | solution.py:40
  100.4 0.1 fusion.73
  100.5 7.3 %collective-permute-done.6 = f32[256,128]{1,0:T(8,128)S(1)} collective-permute-done((f32[256,128]{1,0:T(8,128)S(1)}, f32[256,128]{1,0:T(8,128)S(1)}, u32[]{:S(2)}, u32[]{:S(2)}) %collective-permute-start.6) | collective-permute-done | bytes 131104 | tf_op jit(solution)/shard_map/ppermute | solution.py:40
  107.8 0.7 fusion.8
  108.5 5.8 %all-to-all-start.2 = ((f32[16,16,128]{2,1,0:T(8,128)}), f32[16,16,128]{2,1,0:T(8,128)S(1)}, u32[]{:S(2)}, u32[]{:S(2)}) async-start(f32[16,16,128]{2,1,0:T(8,128)} %bitcast.10), calls=%async_computation.2 | async-start | bytes 262144 | tf_op jit(solution)/shard_map/all_to_all | solution.py:279
  114.3 18.8 %while.1 = (s32[]{:T(128)}, f32[10,4608]{1,0:T(8,128)}, s32[8,2]{0,1:T(2,128)S(1)}, f32[8,10,4096]{2,1,0:T(8,128)S(1)}, s32[]{:T(128)}) while((s32[]{:T(128)}, f32[10,4608]{1,0:T(8,128)}, s32[8,2]{0,1:T(2,128)S(1)}, f32[8,10,4096]{2,1,0:T(8,128)S(1)}, s32[]{:T(128)}) %tuple.43), condition=%wide.while_cond, body=%wide.while_body.sunk | while | flops 2 | bytes 426089 | solution.py:77
  114.3 0.1 constant_dynamic-slice_fusion.4
  114.4 0.5 slice.757
  114.9 1.7 bitcast_dynamic-update-slice_fusion.2
  116.7 0.1 constant_dynamic-slice_fusion.4
  116.8 0.5 slice.757
  117.3 1.7 bitcast_dynamic-update-slice_fusion.2
  119.1 0.5 slice.757
  119.6 1.7 bitcast_dynamic-update-slice_fusion.2
  121.5 0.5 slice.757
  122.0 1.7 bitcast_dynamic-update-slice_fusion.2
  123.8 0.5 slice.757
  124.3 1.7 bitcast_dynamic-update-slice_fusion.2
  126.2 0.5 slice.757
  126.7 1.7 bitcast_dynamic-update-slice_fusion.2
  128.5 0.5 slice.757
  129.0 1.7 bitcast_dynamic-update-slice_fusion.2
  130.8 0.5 slice.757
  131.4 1.7 bitcast_dynamic-update-slice_fusion.2
  133.1 0.8 copy.23
  133.9 4.0 %gather_fusion.1 = f32[55,8,4096]{2,1,0:T(8,128)} fusion(f32[8,10,4096]{2,0,1:T(8,128)S(1)} %copy.23, s32[1024]{0:T(1024)S(1)} %pad_clamp_fusion), kind=kCustom, calls=%fused_computation.1 | custom fusion | bytes 14418140 | tf_op jit(solution)/shard_map/gather | solution.py:83
  137.9 3.9 %gather_fusion = f32[55,8,4096]{2,1,0:T(8,128)} fusion(f32[8,10,4096]{2,0,1:T(8,128)S(1)} %copy.23, s32[1024]{0:T(1024)S(1)} %pad_clamp_fusion.1), kind=kCustom, calls=%fused_computation | custom fusion | bytes 14418140 | tf_op jit(solution)/shard_map/gather | solution.py:83
  141.8 0.2 reshape.237
  142.0 0.1 bitcast_convert_fusion
  142.2 0.1 convert_element_type.24
  142.3 12.0 %all_gather.3 = bf16[2,16,4096]{2,1,0:T(8,128)(2,1)S(1)} all-gather(bf16[2,16,1024]{2,1,0:T(8,128)(2,1)S(1)} %convert_element_type.24), channel_id=1, replica_groups=mesh['tgt'=128,'band'=4] {'band'}, dimensions={2}, use_global_device_ids=true | all-gather | bytes 327680 | tf_op jit(solution)/shard_map/all_gather | solution.py:328
  154.3 0.2 fusion.74
  154.5 1.1 convolution_bitcast_fusion
  155.6 7.2 %fusion.3 = f32[55,8,16]{2,1,0:T(8,128)S(1)} fusion(f32[55,8,4096]{2,1,0:T(8,128)} %gather_fusion, f32[55,8,4096]{2,1,0:T(8,128)} %gather_fusion.1, bf16[2,16,4096]{2,1,0:T(8,128)(2,1)S(1)} %all_gather.3), kind=kOutput, calls=%fused_computation.7 | convolution fusion | flops 347832320 | bytes 14577152 | tf_op jit(solution)/shard_map/ti,zpi->ztp/dot_general | solution.py:84
  162.8 0.9 reduce-scatter.2.cloned.1.call-done
  163.6 10.0 %all-to-all-start.3 = ((bf16[8,11,16,128]{3,2,1,0:T(8,128)(2,1)}), bf16[8,11,16,128]{3,2,1,0:T(8,128)(2,1)S(1)}, u32[]{:S(2)}, u32[]{:S(2)}) async-start(bf16[8,11,16,128]{3,2,1,0:T(8,128)(2,1)} %bitcast.397), calls=%async_computation.4 | async-start | bytes 720896 | tf_op jit(solution)/shard_map/all_to_all | solution.py:279
  173.8 0.1 squeeze.300
  173.9 0.1 squeeze.299
  174.0 0.6 div.109
  174.7 0.8 add_bitcast_fusion
  175.4 6.0 %all-to-all-done.3 = bf16[8,11,16,128]{3,2,1,0:T(8,128)(2,1)S(1)} async-done(((bf16[8,11,16,128]{3,2,1,0:T(8,128)(2,1)}), bf16[8,11,16,128]{3,2,1,0:T(8,128)(2,1)S(1)}, u32[]{:S(2)}, u32[]{:S(2)}) %all-to-all-start.3) | async-done | bytes 360480 | tf_op jit(solution)/shard_map/all_to_all | solution.py:279
  181.4 0.8 fusion.7
  (38 shorter events, 0.8 us)
Async XLA Ops:
  9.2 20.1 %all-to-all-start = ((bf16[16,128,128]{2,1,0:T(8,128)(2,1)}), bf16[16,128,128]{2,1,0:T(8,128)(2,1)S(1)}, u32[]{:S(2)}, u32[]{:S(2)}) async-start(bf16[16,128,128]{2,1,0:T(8,128)(2,1)} %shard_map.131), calls=%async_computation | async-start | bytes 1048576 | tf_op jit(solution)/shard_map/all_to_all | solution.py:279
  19.5 1.8 copy-start
  21.3 0.9 copy-start.1
  24.6 10.2 %copy-start.2 = (s32[16384]{0:T(1024)S(1)}, s32[16384]{0:T(1024)}, u32[]{:S(2)}) copy-start(s32[16384]{0:T(1024)} %param.14) | copy-start | bytes 196612
  24.6 10.3 %copy-start.3 = (s32[16384]{0:T(1024)S(1)}, s32[16384]{0:T(1024)}, u32[]{:S(2)}) copy-start(s32[16384]{0:T(1024)} %param.15) | copy-start | bytes 196612
  29.4 40.4 %all-to-all-start.1 = ((bf16[8,11,128,128]{3,2,1,0:T(8,128)(2,1)}), bf16[8,11,128,128]{3,2,1,0:T(8,128)(2,1)}, u32[]{:S(2)}, u32[]{:S(2)}) async-start(bf16[8,11,128,128]{3,2,1,0:T(8,128)(2,1)} %shard_map.130), calls=%async_computation.1 | async-start | bytes 5767168 | tf_op jit(solution)/shard_map/all_to_all | solution.py:279
  34.8 128.8 %reduce-scatter.2.cloned.1.call-start = ((), (), s32[]{:S(2)}) async-start(), calls=%async_computation.5 | async-start | bytes 6127616 | tf_op jit(solution)/shard_map/reduce_scatter | solution.py:285
  38.2 10.8 %collective-permute-start.1 = (f32[256,128]{1,0:T(8,128)S(1)}, f32[256,128]{1,0:T(8,128)S(1)}, u32[]{:S(2)}, u32[]{:S(2)}) collective-permute-start(f32[256,128]{1,0:T(8,128)S(1)} %get-tuple-element.45), channel_id=1, source_target_pairs={{0,112},{4,116},{8,120},{12,124},{16,0},{20,4},{24,8},{28,12},{32,... | collective-permute-start | bytes 393224 | tf_op jit(solution)/shard_map/ppermute | solution.py:40
  45.7 8.6 %collective-permute-start = (f32[256,128]{1,0:T(8,128)S(1)}, f32[256,128]{1,0:T(8,128)S(1)}, u32[]{:S(2)}, u32[]{:S(2)}) collective-permute-start(f32[256,128]{1,0:T(8,128)S(1)} %get-tuple-element.46), channel_id=1, source_target_pairs={{0,16},{4,20},{8,24},{12,28},{16,32},{20,36},{24,40},{28,44},{32,4... | collective-permute-start | bytes 393224 | tf_op jit(solution)/shard_map/ppermute | solution.py:40
  54.4 8.1 %collective-permute-start.2 = (f32[256,128]{1,0:T(8,128)S(1)}, f32[256,128]{1,0:T(8,128)S(1)}, u32[]{:S(2)}, u32[]{:S(2)}) collective-permute-start(f32[256,128]{1,0:T(8,128)S(1)} %get-tuple-element.16), channel_id=1, source_target_pairs={{0,16},{4,20},{8,24},{12,28},{16,32},{20,36},{24,40},{28,44},{32,4... | collective-permute-start | bytes 393224 | tf_op jit(solution)/shard_map/ppermute | solution.py:40
  56.3 7.4 %collective-permute-start.3 = (f32[256,128]{1,0:T(8,128)S(1)}, f32[256,128]{1,0:T(8,128)S(1)}, u32[]{:S(2)}, u32[]{:S(2)}) collective-permute-start(f32[256,128]{1,0:T(8,128)S(1)} %get-tuple-element.17), channel_id=1, source_target_pairs={{0,112},{4,116},{8,120},{12,124},{16,0},{20,4},{24,8},{28,12},{32,... | collective-permute-start | bytes 393224 | tf_op jit(solution)/shard_map/ppermute | solution.py:40
  80.5 19.9 %copy-start.6 = (s32[32]{0:T(128)S(1)}, s32[32]{0:T(128)}, u32[]{:S(2)}) copy-start(s32[32]{0:T(128)} %param.17) | copy-start | bytes 388
  80.5 11.4 %collective-permute-start.4 = (f32[256,128]{1,0:T(8,128)S(1)}, f32[256,128]{1,0:T(8,128)S(1)}, u32[]{:S(2)}, u32[]{:S(2)}) collective-permute-start(f32[256,128]{1,0:T(8,128)S(1)} %get-tuple-element.20), channel_id=1, source_target_pairs={{0,16},{4,20},{8,24},{12,28},{16,32},{20,36},{24,40},{28,44},{32,4... | collective-permute-start | bytes 393224 | tf_op jit(solution)/shard_map/ppermute | solution.py:40
  82.5 12.5 %collective-permute-start.5 = (f32[256,128]{1,0:T(8,128)S(1)}, f32[256,128]{1,0:T(8,128)S(1)}, u32[]{:S(2)}, u32[]{:S(2)}) collective-permute-start(f32[256,128]{1,0:T(8,128)S(1)} %get-tuple-element.21), channel_id=1, source_target_pairs={{0,112},{4,116},{8,120},{12,124},{16,0},{20,4},{24,8},{28,12},{32,... | collective-permute-start | bytes 393224 | tf_op jit(solution)/shard_map/ppermute | solution.py:40
  95.0 12.8 %collective-permute-start.6 = (f32[256,128]{1,0:T(8,128)S(1)}, f32[256,128]{1,0:T(8,128)S(1)}, u32[]{:S(2)}, u32[]{:S(2)}) collective-permute-start(f32[256,128]{1,0:T(8,128)S(1)} %bitcast_add_fusion), channel_id=1, source_target_pairs={{0,16},{4,20},{8,24},{12,28},{16,32},{20,36},{24,40},{28,44},{32,4... | collective-permute-start | bytes 393224 | tf_op jit(solution)/shard_map/ppermute | solution.py:40
  108.5 33.4 %all-to-all-start.2 = ((f32[16,16,128]{2,1,0:T(8,128)}), f32[16,16,128]{2,1,0:T(8,128)S(1)}, u32[]{:S(2)}, u32[]{:S(2)}) async-start(f32[16,16,128]{2,1,0:T(8,128)} %bitcast.10), calls=%async_computation.2 | async-start | bytes 262144 | tf_op jit(solution)/shard_map/all_to_all | solution.py:279
  114.3 19.6 %copy-start.5 = (s32[55]{0:T(128)S(1)}, s32[55]{0:T(128)}, u32[]{:S(2)}) copy-start(s32[55]{0:T(128)} %constant.161) | copy-start | bytes 664
  133.9 4.0 %copy-start.4 = (s32[55]{0:T(128)S(1)}, s32[55]{0:T(128)}, u32[]{:S(2)}) copy-start(s32[55]{0:T(128)} %constant.160) | copy-start | bytes 664
  163.6 17.8 %all-to-all-start.3 = ((bf16[8,11,16,128]{3,2,1,0:T(8,128)(2,1)}), bf16[8,11,16,128]{3,2,1,0:T(8,128)(2,1)S(1)}, u32[]{:S(2)}, u32[]{:S(2)}) async-start(bf16[8,11,16,128]{3,2,1,0:T(8,128)(2,1)} %bitcast.397), calls=%async_computation.4 | async-start | bytes 720896 | tf_op jit(solution)/shard_map/all_to_all | solution.py:279
Sparse Core Ops, SparseCore 0:
  80.6 82.9 reduce-scatter.1

commit v8 on v7

--- a/solution.py
+++ b/solution.py
@@ -9,6 +9,7 @@
 TGT_DEV = 16
 NDIAG = 11
 Z_DEV = 8
+SHIFT = 512
 
 XS, ZS, CS = 4, 16, 2
 PLANE = XS * CS
@@ -79,8 +80,8 @@
     return jax.vmap(one_shift)(shifts)
 
 
-def normal_terms(weight_sum, flux_sum, windows):
-    products = windows[:, pair_first, :] * windows[:, pair_second, :]
+def normal_terms(weight_sum, flux_sum, windows, firsts, seconds):
+    products = firsts * seconds
     matrix = jnp.einsum("ti,zpi->ztp", weight_sum, products, precision=lax.Precision.HIGHEST)
     right_side = jnp.einsum("ti,zbi->ztb", flux_sum, windows, precision=lax.Precision.HIGHEST)
     return (matrix, right_side)
@@ -307,20 +308,28 @@
         masked.reshape(XS, STATIONS, PAIR * CS * row_count), my_z // PAIR, 1, keepdims=False
     ).reshape(1, -1)
 
-    mixed = exchange(mix_pair(exposure_ivar, exposure_flux), wide_groups)
-    packed = split_lanes(exposure_ivar, jnp.transpose(exposure_res, (1, 0, 2)))
-    packed, mixed = lax.optimization_barrier((packed, mixed))
-    rows = exchange(packed, plane_groups)
+    rows = exchange(
+        split_lanes(exposure_ivar, jnp.transpose(exposure_res, (1, 0, 2))), plane_groups
+    )
+    band_index = lax.axis_index("band")
+    shifts = lax.dynamic_slice_in_dim(redshift_shift, band_index * Z_DEV, Z_DEV)
+    windows = basis_windows(rest_basis, shifts, 0, rest_basis.shape[1] - SHIFT)
+    firsts, seconds = windows[:, pair_first, :], windows[:, pair_second, :]
+    mixed = mix_pair(exposure_ivar, exposure_flux)
+    rows, mixed, windows, firsts, seconds, wide_targets = lax.optimization_barrier(
+        (rows, mixed, windows, firsts, seconds, wide_targets)
+    )
+    mixed = exchange(mixed, wide_groups)
+    part_res = coadd_res_rows(targets, rows)
+    mixed, part_res = lax.optimization_barrier((mixed, part_res))
     turns = STATIONS // 2
     part, up, down = ring_start(mix_sum(wide_targets, mixed), my_z // PAIR)
     for s in range(turns):
-        if s == turns // 2:
-            rows, up, down = lax.optimization_barrier((rows, up, down))
         part, up, down = ring_turn((part, up, down), s)
         if s < turns - 1:
             up, down = lax.optimization_barrier((up, down))
     sums = part(0) + up + down
-    res_sum = scatter_sum(coadd_res_rows(targets, rows))
+    res_sum = scatter_sum(part_res)
 
     own = exchange(sums.reshape(WIDE, TGT_DEV, -1), wide_groups)
     own = jnp.transpose(own.reshape(WIDE, TGT_DEV, 2, wave_dev // WIDE), (2, 1, 0, 3))
@@ -328,10 +337,7 @@
     everything = lax.all_gather(own.astype(jnp.bfloat16), "band", axis=2, tiled=True)
     everything = everything.astype(jnp.float32)
     coadd_flux = own[1] / own[0]
-    band_index = lax.axis_index("band")
-    shifts = lax.dynamic_slice_in_dim(redshift_shift, band_index * Z_DEV, Z_DEV)
-    windows = basis_windows(rest_basis, shifts, 0, everything.shape[2])
-    fit_gain = fit_from(*normal_terms(everything[0], everything[1], windows))
+    fit_gain = fit_from(*normal_terms(everything[0], everything[1], windows, firsts, seconds))
 
     back = exchange(res_sum, plane_groups)
     own_res = jnp.transpose(back, (1, 2, 0, 3)).reshape(NDIAG, TGT_DEV, wave_dev)

time: 190 us -> 201 us (1.058)
  blocking collectives: 12 us -> 37 us
  starting transfers between devices: 63.3 us -> 46.8 us
  waiting for transfers between devices: 37.7 us -> 45.8 us
  local copies, waits for them, and re-layouts: 31.6 us -> 23.9 us
    all_to_all x0 -> x1, blocking collectives: none -> 25.7 us  [exchange(): lax.all_to_all(values, 'tgt', split_axis=0, concat_axis=0, axis_index_gro...]
    all_to_all x4 -> x3, starting transfers between devices: 31.6 us -> 21.5 us  [exchange(): lax.all_to_all(values, 'tgt', split_axis=0, concat_axis=0, axis_index_gro...]
    gather x26, local copies, waits for them, and re-layouts: 26.5 us -> 18.8 us
    ppermute x7, waiting for transfers between devices: 20.1 us -> 27.4 us  [ring_step(): return lax.ppermute(values, 'tgt', pairs)]
    ppermute x7, starting transfers between devices: 31.7 us -> 25.3 us  [ring_step(): return lax.ppermute(values, 'tgt', pairs)]
    add x2, other arithmetic: 0.06 us -> 2.52 us  [ring_turn(): down = down + part(half + 2 + s)]
    all_to_all x4 -> x3, waiting for transfers between devices: 16.7 us -> 18.3 us  [exchange(): lax.all_to_all(values, 'tgt', split_axis=0, concat_axis=0, axis_index_gro...]
  transfers between devices with their start and end apart: 12 -> 11, of which waited for: 10 -> 9; matrix products, arithmetic and copies ran while one was open for 21% -> 17% of each run, Pallas kernels for 3% -> 8%
where the time goes in v8:
time: 201 us; the launch traced here: 200 us
  starting transfers between devices  46.8 us (23%)
  waiting for transfers between devices  45.8 us (23%)
  blocking collectives  37 us (18%)
  local copies, waits for them, and re-layouts  23.9 us (12%)
  Pallas kernels  18.9 us (9%)
  between operations  14.6 us (7%)
  matrix products  8.07 us (4%)
  other arithmetic  4.99 us (2%)
    ppermute x7, waiting for transfers between devices, ring_step(): return lax.ppermute(values, 'tgt', pairs)  27.4 us
    all_to_all x1, blocking collectives, exchange(): lax.all_to_all(values, 'tgt', split_axis=0, concat_axis=0, axis_index_gro...  25.7 us
    ppermute x7, starting transfers between devices, ring_step(): return lax.ppermute(values, 'tgt', pairs)  25.3 us
    all_to_all x3, starting transfers between devices, exchange(): lax.all_to_all(values, 'tgt', split_axis=0, concat_axis=0, axis_index_gro...  21.5 us
    all_to_all x3, waiting for transfers between devices, exchange(): lax.all_to_all(values, 'tgt', split_axis=0, concat_axis=0, axis_index_gro...  18.3 us
    all_gather x1, blocking collectives, shards(): lax.all_gather(own.astype(jnp.bfloat16), 'band', axis=2, tiled=True)  11.3 us
    gather x24, local copies, waits for them, and re-layouts  10.9 us
    pallas_call x1, Pallas kernels, coadd_res_rows(): pl.pallas_call(res_kernel, out_shape=jax.ShapeDtypeStruct(out_shape, jnp....  10.8 us
  transfers between devices with their start and end apart: 11, of which 9 were waited for; matrix products, arithmetic and copies ran while one was open for 17% of the time, Pallas kernels for 8%

profile of v8, /device:TPU:1, one launch (start us, length us, event | category | flops | bytes accessed | tf_op | source)
XLA Modules:
  0.0 200.1 jit_solution(9897594465822582231)
XLA Ops:
  7.2 1.8 copy-done
  9.0 0.9 copy-done.1
  9.9 2.3 %shard_map.130 = bf16[8,11,128,128]{3,2,1,0:T(8,128)(2,1)} custom-call(bf16[128,1024]{1,0:T(8,128)(2,1)S(1)} %copy-done.1, bf16[11,128,1024]{2,1,0:T(8,128)(2,1)S(1)} %bitcast.391), custom_call_target="tpu_custom_call" | custom-call | flops 1441792 | bytes 6291456 | tf_op jit(solution)/shard_map/pallas_call | solution.py:112
  12.2 11.3 %all-to-all-start = ((bf16[8,11,128,128]{3,2,1,0:T(8,128)(2,1)}), bf16[8,11,128,128]{3,2,1,0:T(8,128)(2,1)}, u32[]{:S(2)}, u32[]{:S(2)}) async-start(bf16[8,11,128,128]{3,2,1,0:T(8,128)(2,1)} %shard_map.130), calls=%async_computation | async-start | bytes 5767168 | tf_op jit(solution)/shard_map/all_to_all | solution.py:280
  23.5 0.1 fusion.72
  23.6 11.1 %while.1 = (s32[]{:T(128)}, f32[10,4608]{1,0:T(8,128)S(1)}, s32[8,2]{0,1:T(2,128)S(1)}, f32[8,10,4096]{2,1,0:T(8,128)S(1)}, s32[]{:T(128)}) while((s32[]{:T(128)}, f32[10,4608]{1,0:T(8,128)S(1)}, s32[8,2]{0,1:T(2,128)S(1)}, f32[8,10,4096]{2,1,0:T(8,128)S(1)}, s32[]{:T(128)}) %tuple.48), condition=%wide.while_cond, body=%wide.while_body.sunk | while | flops 2 | bytes 524393 | solution.py:78
  23.6 0.1 constant_dynamic-slice_fusion.4
  23.7 0.5 slice.757
  24.2 0.8 bitcast_dynamic-update-slice_fusion.2
  25.1 0.5 slice.757
  25.6 0.8 bitcast_dynamic-update-slice_fusion.2
  26.5 0.5 slice.757
  27.0 0.8 bitcast_dynamic-update-slice_fusion.2
  27.9 0.5 slice.757
  28.4 0.8 bitcast_dynamic-update-slice_fusion.2
  29.2 0.5 slice.757
  29.8 0.8 bitcast_dynamic-update-slice_fusion.2
  30.6 0.5 slice.757
  31.1 0.8 bitcast_dynamic-update-slice_fusion.2
  31.9 0.1 constant_dynamic-slice_fusion.4
  32.0 0.5 slice.757
  32.5 0.8 bitcast_dynamic-update-slice_fusion.2
  33.4 0.5 slice.757
  33.9 0.8 bitcast_dynamic-update-slice_fusion.2
  34.8 2.5 %shard_map.131 = bf16[16,128,128]{2,1,0:T(8,128)(2,1)} custom-call(bf16[128,1024]{1,0:T(8,128)(2,1)} %ivar_ref.3, bf16[128,1024]{1,0:T(8,128)(2,1)} %flux_ref.1), custom_call_target="tpu_custom_call" | custom-call | bytes 1048576 | tf_op jit(solution)/shard_map/pallas_call | solution.py:197
  37.3 0.8 copy.19
  38.1 3.9 %gather_fusion = f32[55,8,4096]{2,1,0:T(8,128)} fusion(f32[8,10,4096]{2,0,1:T(8,128)S(1)} %copy.19, s32[1024]{0:T(1024)S(1)} %pad_clamp_fusion.1), kind=kCustom, calls=%fused_computation | custom fusion | bytes 14418140 | tf_op jit(solution)/shard_map/gather | solution.py:317
  42.1 4.0 %gather_fusion.1 = f32[55,8,4096]{2,1,0:T(8,128)} fusion(f32[8,10,4096]{2,0,1:T(8,128)S(1)} %copy.19, s32[1024]{0:T(1024)S(1)} %pad_clamp_fusion), kind=kCustom, calls=%fused_computation.1 | custom fusion | bytes 14418140 | tf_op jit(solution)/shard_map/gather | solution.py:317
  46.1 12.3 %all-to-all-done.rows_ref = bf16[8,11,128,128]{3,2,1,0:T(8,128)(2,1)} async-done(((bf16[8,11,128,128]{3,2,1,0:T(8,128)(2,1)}), bf16[8,11,128,128]{3,2,1,0:T(8,128)(2,1)}, u32[]{:S(2)}, u32[]{:S(2)}) %all-to-all-start) | async-done | bytes 2883616 | tf_op jit(solution)/shard_map/all_to_all | solution.py:280
  58.4 4.2 %all-to-all-start.1 = ((bf16[16,128,128]{2,1,0:T(8,128)(2,1)}), bf16[16,128,128]{2,1,0:T(8,128)(2,1)S(1)}, u32[]{:S(2)}, u32[]{:S(2)}) async-start(bf16[16,128,128]{2,1,0:T(8,128)(2,1)} %shard_map.131), calls=%async_computation.1 | async-start | bytes 1048576 | tf_op jit(solution)/shard_map/all_to_all | solution.py:280
  62.7 0.6 constant_dynamic-slice_fusion.1
  63.3 10.8 %shard_map.132 = bf16[16,8,11,16,128]{4,3,2,1,0:T(8,128)(2,1)} custom-call(s32[1,1024]{1,0:T(1,128)} %bitcast.408, bf16[8,11,128,128]{3,2,1,0:T(8,128)(2,1)} %all-to-all-done.rows_ref), custom_call_target="tpu_custom_call" | custom-call | flops 5905580032 | bytes 8650752 | tf_op jit(solution)/shard_map/pallas_call | solution.py:159
  74.2 3.2 %shard_map.133 = f32[8,256,128]{2,1,0:T(8,128)S(1)} custom-call(s32[1,2048]{1,0:T(1,128)S(1)} %bitcast.392, bf16[16,128,128]{2,1,0:T(8,128)(2,1)S(1)} %all-to-all-done.1.rows_ref), custom_call_target="tpu_custom_call" | custom-call | flops 2147483648 | bytes 1572864 | tf_op jit(solution)/shard_map/pallas_call | solution.py:241
  77.5 6.3 %collective-permute-start.1 = (f32[256,128]{1,0:T(8,128)S(1)}, f32[256,128]{1,0:T(8,128)S(1)}, u32[]{:S(2)}, u32[]{:S(2)}) collective-permute-start(f32[256,128]{1,0:T(8,128)S(1)} %get-tuple-element.51), channel_id=1, source_target_pairs={{0,112},{4,116},{8,120},{12,124},{16,0},{20,4},{24,8},{28,12},{32,... | collective-permute-start | bytes 393224 | tf_op jit(solution)/shard_map/ppermute | solution.py:41
  83.8 1.9 collective-permute-start
  85.8 1.7 collective-permute-done.1
  87.5 5.2 %collective-permute-done = f32[256,128]{1,0:T(8,128)} collective-permute-done((f32[256,128]{1,0:T(8,128)S(1)}, f32[256,128]{1,0:T(8,128)}, u32[]{:S(2)}, u32[]{:S(2)}) %collective-permute-start) | collective-permute-done | bytes 131104 | tf_op jit(solution)/shard_map/ppermute | solution.py:41
  92.7 0.9 bitcast_add_fusion.3
  93.6 2.8 %collective-permute-start.3 = (f32[256,128]{1,0:T(8,128)S(1)}, f32[256,128]{1,0:T(8,128)S(1)}, u32[]{:S(2)}, u32[]{:S(2)}) collective-permute-start(f32[256,128]{1,0:T(8,128)S(1)} %get-tuple-element.22), channel_id=1, source_target_pairs={{0,112},{4,116},{8,120},{12,124},{16,0},{20,4},{24,8},{28,12},{32,... | collective-permute-start | bytes 393224 | tf_op jit(solution)/shard_map/ppermute | solution.py:41
  96.5 3.3 %collective-permute-start.2 = (f32[256,128]{1,0:T(8,128)S(1)}, f32[256,128]{1,0:T(8,128)}, u32[]{:S(2)}, u32[]{:S(2)}) collective-permute-start(f32[256,128]{1,0:T(8,128)S(1)} %get-tuple-element.21), channel_id=1, source_target_pairs={{0,16},{4,20},{8,24},{12,28},{16,32},{20,36},{24,40},{28,44},{32,4... | collective-permute-start | bytes 393224 | tf_op jit(solution)/shard_map/ppermute | solution.py:41
  99.9 3.4 %collective-permute-done.3 = f32[256,128]{1,0:T(8,128)S(1)} collective-permute-done((f32[256,128]{1,0:T(8,128)S(1)}, f32[256,128]{1,0:T(8,128)S(1)}, u32[]{:S(2)}, u32[]{:S(2)}) %collective-permute-start.3) | collective-permute-done | bytes 131104 | tf_op jit(solution)/shard_map/ppermute | solution.py:41
  103.2 4.2 %collective-permute-done.2 = f32[256,128]{1,0:T(8,128)} collective-permute-done((f32[256,128]{1,0:T(8,128)S(1)}, f32[256,128]{1,0:T(8,128)}, u32[]{:S(2)}, u32[]{:S(2)}) %collective-permute-start.2) | collective-permute-done | bytes 131104 | tf_op jit(solution)/shard_map/ppermute | solution.py:41
  107.4 1.6 bitcast_add_fusion.1
  109.0 1.9 collective-permute-start.4
  111.0 5.5 %collective-permute-start.5 = (f32[256,128]{1,0:T(8,128)}, f32[256,128]{1,0:T(8,128)S(1)}, u32[]{:S(2)}, u32[]{:S(2)}) collective-permute-start(f32[256,128]{1,0:T(8,128)} %get-tuple-element.24), channel_id=1, source_target_pairs={{0,112},{4,116},{8,120},{12,124},{16,0},{20,4},{24,8},{28,12},{32,... | collective-permute-start | bytes 393224 | tf_op jit(solution)/shard_map/ppermute | solution.py:41
  116.5 3.3 %collective-permute-done.4 = f32[256,128]{1,0:T(8,128)S(1)} collective-permute-done((f32[256,128]{1,0:T(8,128)S(1)}, f32[256,128]{1,0:T(8,128)S(1)}, u32[]{:S(2)}, u32[]{:S(2)}) %collective-permute-start.4) | collective-permute-done | bytes 131104 | tf_op jit(solution)/shard_map/ppermute | solution.py:41
  119.8 1.4 collective-permute-done.5
  121.1 3.4 %collective-permute-start.6 = (f32[256,128]{1,0:T(8,128)S(1)}, f32[256,128]{1,0:T(8,128)S(1)}, u32[]{:S(2)}, u32[]{:S(2)}) collective-permute-start(f32[256,128]{1,0:T(8,128)S(1)} %bitcast_add_fusion), channel_id=1, source_target_pairs={{0,16},{4,20},{8,24},{12,28},{16,32},{20,36},{24,40},{28,44},{32,4... | collective-permute-start | bytes 393224 | tf_op jit(solution)/shard_map/ppermute | solution.py:41
  124.6 8.3 %collective-permute-done.6 = f32[256,128]{1,0:T(8,128)S(1)} collective-permute-done((f32[256,128]{1,0:T(8,128)S(1)}, f32[256,128]{1,0:T(8,128)S(1)}, u32[]{:S(2)}, u32[]{:S(2)}) %collective-permute-start.6) | collective-permute-done | bytes 131104 | tf_op jit(solution)/shard_map/ppermute | solution.py:41
  132.9 25.7 %all_to_all.20 = f32[16,16,128]{2,1,0:T(8,128)S(1)} all-to-all(f32[16,16,128]{2,1,0:T(8,128)S(1)} %bitcast.396), channel_id=1, replica_groups={{0,4,8,12,128,132,136,140,256,260,264,268,384,388,392,396},{16,20,24,28..., dimensions={0} | all-to-all | bytes 262144 | tf_op jit(solution)/shard_map/all_to_all | solution.py:280
  158.7 0.2 reshape.239
  158.9 0.1 bitcast_convert_fusion
  159.0 0.1 convert_element_type.24
  159.2 11.3 %all_gather.3 = bf16[2,16,4096]{2,1,0:T(8,128)(2,1)S(1)} all-gather(bf16[2,16,1024]{2,1,0:T(8,128)(2,1)S(1)} %convert_element_type.24), channel_id=1, replica_groups=mesh['tgt'=128,'band'=4] {'band'}, dimensions={2}, use_global_device_ids=true | all-gather | bytes 327680 | tf_op jit(solution)/shard_map/all_gather | solution.py:337
  170.4 0.2 fusion.73
  170.6 1.1 convolution_bitcast_fusion
  171.7 7.0 %fusion.2 = f32[55,8,16]{2,1,0:T(8,128)S(1)} fusion(f32[8,55,4096]{2,0,1:T(8,128)} %bitcast.393, f32[8,55,4096]{2,0,1:T(8,128)} %bitcast.394, bf16[2,16,4096]{2,1,0:T(8,128)(2,1)S(1)} %all_gather.3), kind=kOutput, calls=%fused_computation.6 | convolution fusion | flops 347832320 | bytes 14577152 | tf_op jit(solution)/shard_map/ti,zpi->ztp/dot_general | solution.py:85
  178.8 6.0 %all-to-all-start.3 = ((bf16[8,11,16,128]{3,2,1,0:T(8,128)(2,1)}), bf16[8,11,16,128]{3,2,1,0:T(8,128)(2,1)S(1)}, u32[]{:S(2)}, u32[]{:S(2)}) async-start(bf16[8,11,16,128]{3,2,1,0:T(8,128)(2,1)} %bitcast.397), calls=%async_computation.4 | async-start | bytes 720896 | tf_op jit(solution)/shard_map/all_to_all | solution.py:280
  184.8 0.1 squeeze.299
  185.0 0.1 squeeze.300
  185.1 0.6 div.109
  185.7 0.8 add_bitcast_fusion
  186.5 6.0 %all-to-all-done.3 = bf16[8,11,16,128]{3,2,1,0:T(8,128)(2,1)S(1)} async-done(((bf16[8,11,16,128]{3,2,1,0:T(8,128)(2,1)}), bf16[8,11,16,128]{3,2,1,0:T(8,128)(2,1)S(1)}, u32[]{:S(2)}, u32[]{:S(2)}) %all-to-all-start.3) | async-done | bytes 360480 | tf_op jit(solution)/shard_map/all_to_all | solution.py:280
  192.5 0.8 fusion.6
  (43 shorter events, 0.9 us)
Async XLA Ops:
  7.2 1.8 copy-start
  9.0 0.9 copy-start.1
  12.2 11.3 %copy-start.9 = (s32[32]{0:T(128)S(1)}, s32[32]{0:T(128)}, u32[]{:S(2)}) copy-start(s32[32]{0:T(128)} %param.17) | copy-start | bytes 388
  12.2 11.4 %copy-start.4 = (f32[10,4608]{1,0:T(8,128)S(1)}, f32[10,4608]{1,0:T(8,128)}, u32[]{:S(2)}) copy-start(f32[10,4608]{1,0:T(8,128)} %param.16) | copy-start | bytes 552964
  12.2 46.2 %all-to-all-start = ((bf16[8,11,128,128]{3,2,1,0:T(8,128)(2,1)}), bf16[8,11,128,128]{3,2,1,0:T(8,128)(2,1)}, u32[]{:S(2)}, u32[]{:S(2)}) async-start(bf16[8,11,128,128]{3,2,1,0:T(8,128)(2,1)} %shard_map.130), calls=%async_computation | async-start | bytes 5767168 | tf_op jit(solution)/shard_map/all_to_all | solution.py:280
  34.7 7.3 %copy-start.2 = (f32[8,10,4096]{2,1,0:T(8,128)}, f32[8,10,4096]{2,1,0:T(8,128)S(1)}, u32[]{:S(2)}) copy-start(f32[8,10,4096]{2,1,0:T(8,128)S(1)} %get-tuple-element.28) | copy-start | bytes 3932164
  34.7 3.4 %copy-start.8 = (s32[55]{0:T(128)S(1)}, s32[55]{0:T(128)}, u32[]{:S(2)}) copy-start(s32[55]{0:T(128)} %constant.160) | copy-start | bytes 664
  38.1 3.9 %copy-start.7 = (s32[55]{0:T(128)S(1)}, s32[55]{0:T(128)}, u32[]{:S(2)}) copy-start(s32[55]{0:T(128)} %constant.161) | copy-start | bytes 664
  42.0 4.0 %copy-start.5 = (s32[16384]{0:T(1024)S(1)}, s32[16384]{0:T(1024)}, u32[]{:S(2)}) copy-start(s32[16384]{0:T(1024)} %param.14) | copy-start | bytes 196612
  42.1 4.0 %copy-start.6 = (s32[16384]{0:T(1024)S(1)}, s32[16384]{0:T(1024)}, u32[]{:S(2)}) copy-start(s32[16384]{0:T(1024)} %param.15) | copy-start | bytes 196612
  58.4 15.7 %all-to-all-start.1 = ((bf16[16,128,128]{2,1,0:T(8,128)(2,1)}), bf16[16,128,128]{2,1,0:T(8,128)(2,1)S(1)}, u32[]{:S(2)}, u32[]{:S(2)}) async-start(bf16[16,128,128]{2,1,0:T(8,128)(2,1)} %shard_map.131), calls=%async_computation.1 | async-start | bytes 1048576 | tf_op jit(solution)/shard_map/all_to_all | solution.py:280
  62.6 116.1 %reduce-scatter.2.cloned.1.call-start = ((), (), s32[]{:S(2)}) async-start(), calls=%async_computation.5 | async-start | bytes 6127616 | tf_op jit(solution)/shard_map/reduce_scatter | solution.py:286
  77.4 93.2 %copy-start.3 = (f32[8,10,4096]{2,1,0:T(8,128)S(1)}, f32[8,10,4096]{2,1,0:T(8,128)}, u32[]{:S(2)}) copy-start(f32[8,10,4096]{2,1,0:T(8,128)} %copy-done.2) | copy-start | bytes 3932164
  77.5 10.0 %collective-permute-start.1 = (f32[256,128]{1,0:T(8,128)S(1)}, f32[256,128]{1,0:T(8,128)S(1)}, u32[]{:S(2)}, u32[]{:S(2)}) collective-permute-start(f32[256,128]{1,0:T(8,128)S(1)} %get-tuple-element.51), channel_id=1, source_target_pairs={{0,112},{4,116},{8,120},{12,124},{16,0},{20,4},{24,8},{28,12},{32,... | collective-permute-start | bytes 393224 | tf_op jit(solution)/shard_map/ppermute | solution.py:41
  83.8 8.9 %collective-permute-start = (f32[256,128]{1,0:T(8,128)S(1)}, f32[256,128]{1,0:T(8,128)}, u32[]{:S(2)}, u32[]{:S(2)}) collective-permute-start(f32[256,128]{1,0:T(8,128)S(1)} %get-tuple-element.52), channel_id=1, source_target_pairs={{0,16},{4,20},{8,24},{12,28},{16,32},{20,36},{24,40},{28,44},{32,4... | collective-permute-start | bytes 393224 | tf_op jit(solution)/shard_map/ppermute | solution.py:41
  93.6 9.6 %collective-permute-start.3 = (f32[256,128]{1,0:T(8,128)S(1)}, f32[256,128]{1,0:T(8,128)S(1)}, u32[]{:S(2)}, u32[]{:S(2)}) collective-permute-start(f32[256,128]{1,0:T(8,128)S(1)} %get-tuple-element.22), channel_id=1, source_target_pairs={{0,112},{4,116},{8,120},{12,124},{16,0},{20,4},{24,8},{28,12},{32,... | collective-permute-start | bytes 393224 | tf_op jit(solution)/shard_map/ppermute | solution.py:41
  96.5 11.0 %collective-permute-start.2 = (f32[256,128]{1,0:T(8,128)S(1)}, f32[256,128]{1,0:T(8,128)}, u32[]{:S(2)}, u32[]{:S(2)}) collective-permute-start(f32[256,128]{1,0:T(8,128)S(1)} %get-tuple-element.21), channel_id=1, source_target_pairs={{0,16},{4,20},{8,24},{12,28},{16,32},{20,36},{24,40},{28,44},{32,4... | collective-permute-start | bytes 393224 | tf_op jit(solution)/shard_map/ppermute | solution.py:41
  109.0 10.7 %collective-permute-start.4 = (f32[256,128]{1,0:T(8,128)S(1)}, f32[256,128]{1,0:T(8,128)S(1)}, u32[]{:S(2)}, u32[]{:S(2)}) collective-permute-start(f32[256,128]{1,0:T(8,128)S(1)} %get-tuple-element.23), channel_id=1, source_target_pairs={{0,16},{4,20},{8,24},{12,28},{16,32},{20,36},{24,40},{28,44},{32,4... | collective-permute-start | bytes 393224 | tf_op jit(solution)/shard_map/ppermute | solution.py:41
  111.0 10.2 %collective-permute-start.5 = (f32[256,128]{1,0:T(8,128)}, f32[256,128]{1,0:T(8,128)S(1)}, u32[]{:S(2)}, u32[]{:S(2)}) collective-permute-start(f32[256,128]{1,0:T(8,128)} %get-tuple-element.24), channel_id=1, source_target_pairs={{0,112},{4,116},{8,120},{12,124},{16,0},{20,4},{24,8},{28,12},{32,... | collective-permute-start | bytes 393224 | tf_op jit(solution)/shard_map/ppermute | solution.py:41
  121.1 11.8 %collective-permute-start.6 = (f32[256,128]{1,0:T(8,128)S(1)}, f32[256,128]{1,0:T(8,128)S(1)}, u32[]{:S(2)}, u32[]{:S(2)}) collective-permute-start(f32[256,128]{1,0:T(8,128)S(1)} %bitcast_add_fusion), channel_id=1, source_target_pairs={{0,16},{4,20},{8,24},{12,28},{16,32},{20,36},{24,40},{28,44},{32,4... | collective-permute-start | bytes 393224 | tf_op jit(solution)/shard_map/ppermute | solution.py:41
  178.8 13.7 %all-to-all-start.3 = ((bf16[8,11,16,128]{3,2,1,0:T(8,128)(2,1)}), bf16[8,11,16,128]{3,2,1,0:T(8,128)(2,1)S(1)}, u32[]{:S(2)}, u32[]{:S(2)}) async-start(bf16[8,11,16,128]{3,2,1,0:T(8,128)(2,1)} %bitcast.397), calls=%async_computation.4 | async-start | bytes 720896 | tf_op jit(solution)/shard_map/all_to_all | solution.py:280
Sparse Core Ops, SparseCore 0:
  74.3 96.9 reduce-scatter.1
